TPU v7x, 128 devices: a whole 4x4x4 slice. The times are simulated.
128 devices in a mesh: chan: 16 (over y, z), tm: 8 (over x, core).
Axes of the slice: x: 4, y: 4, z: 4, core: 2. Of those that a mesh axis runs over, the one named last changes fastest.
Arguments:
- filterbank: bfloat16 [4096, 8192], P('chan', 'tm'), may hold values from -6 to 6
- first_rows: int32 [12, 2048], replicated, may hold values from 0 to 1023, as said below
- second_rows: int32 [12, 2048], replicated, may hold values from 0 to 1023, as said below
- shifts: int32 [12, 2048], replicated, may hold values from 0 to 15, as said below
- harmonic_bins: int32 [8, 512], replicated, may hold values from 0 to 4095, as said below
Outputs:
- power: float32 [2048, 4096], P(('chan', 'tm'))
- harmonic_sum: float32 [2048, 512], P(('chan', 'tm'))
Inputs may be any that keep to these rules, and one draw needn't show every extreme that they name: Only entries with r < min(2^(l+1), 2048) of row l are read. first_rows[l, r] lies below min(2^l, 1024). Only entries with r < min(2^(l+1), 2048) of row l are read. second_rows[l, r] lies below min(2^l, 1024). `shifts`: only entries with r < min(2^(l+1), 2048) of row l are read. harmonic_bins[h, k] = floor((h + 1) * (8 * k + u_k) / 8) with whole u_k from 0 to 7; u of the last fundamental is 7.
All inputs are finite; a program needn't handle non-finite values.
Results may differ from a plain program's by a relative error of at most 0.0003.
Values may be sent and summed in bfloat16 or wider, within the bound.
A program may use at most 192 MiB of HBM per device.

v0:
```python
import functools
import math

import jax
import jax.numpy as jnp
from jax import lax
from jax.experimental import pallas as pl
from jax.experimental.pallas import tpu as pltpu
from jax.sharding import PartitionSpec as P

C = 4096
NDM = 2048
SHIFT = 16
DFT_OUTER = 64
HARM = 8
RAW_HALO = 256
SUB_HALO = 64


def shift_right(value, amount):
    width = value.shape[-1]
    pad = [(0, 0)] * (value.ndim - 1) + [(amount, 0)]
    return jnp.pad(value, pad)[..., :width]


def merge_level(paired, rows_first, rows_second, delays):
    lower_bands = jnp.take(paired[0::2], rows_first, axis=1)
    upper_bands = jnp.take(paired[1::2], rows_second, axis=1)
    delay_col = delays[None, :, None]
    shifted = upper_bands
    for bit in (1, 2, 4, 8):
        shifted = jnp.where((delay_col & bit) != 0, shift_right(shifted, bit), shifted)
    return lower_bands + shifted


def level_merge(layers, first_rows, second_rows, shifts, level):
    count = min(2 ** (level + 1), NDM)
    return merge_level(
        layers, first_rows[level, :count], second_rows[level, :count], shifts[level, :count]
    )


def levels_kernel(plan, first_ref, second_ref, shift_ref, x_ref, out_ref, buf_a, buf_b):
    source = x_ref
    for step, (row_in, row_out, rows_total) in enumerate(plan):
        target = out_ref if step == len(plan) - 1 else (buf_a, buf_b)[step % 2]
        log_out = row_out.bit_length() - 1

        def body(out_row, carry, source=source, target=target, step=step,
                 row_in=row_in, row_out=row_out, log_out=log_out):
            band = lax.shift_right_logical(out_row, log_out)
            row = lax.bitwise_and(out_row, row_out - 1)
            low = 2 * band * row_in + first_ref[step, row]
            high = (2 * band + 1) * row_in + second_ref[step, row]
            amount = shift_ref[step, row]
            lower = source[pl.ds(low, 1), :]
            upper = source[pl.ds(high, 1), :]
            target[pl.ds(out_row, 1), :] = lower + pltpu.roll(upper, amount, 1)
            return carry

        lax.fori_loop(0, rows_total, body, 0, unroll=8)
        source = target


def run_levels(state, first_rows, second_rows, shifts, plan):
    rows, width = state.shape
    out_rows = plan[-1][2]
    buf_rows = max(p[2] for p in plan)
    smem = pl.BlockSpec(memory_space=pltpu.SMEM)
    vmem = pl.BlockSpec(memory_space=pltpu.VMEM)
    return pl.pallas_call(
        functools.partial(levels_kernel, plan),
        out_shape=jax.ShapeDtypeStruct((out_rows, width), jnp.float32),
        in_specs=[smem, smem, smem, vmem],
        out_specs=vmem,
        scratch_shapes=[pltpu.VMEM((buf_rows, width), jnp.float32)] * 2,
        compiler_params=pltpu.CompilerParams(vmem_limit_bytes=48 * 1024 * 1024),
    )(first_rows, second_rows, shifts, state)


def spectra(series, harmonic_bins):
    count = series.shape[0]
    total = series.shape[1]
    outer = DFT_OUTER
    inner = total // outer
    half_inner = inner // 2
    highest = lax.Precision.HIGHEST
    grid = series.reshape(count, outer, inner)
    outer_index = jnp.arange(outer, dtype=jnp.int32)
    inner_index = jnp.arange(inner, dtype=jnp.int32)
    half_index = jnp.arange(half_inner, dtype=jnp.int32)
    angle_outer = (
        2.0
        * math.pi
        / outer
        * (outer_index[:, None] * outer_index[None, :] % outer).astype(jnp.float32)
    )
    outer_table = jnp.concatenate([jnp.cos(angle_outer), jnp.sin(angle_outer)], axis=1)
    section_one = jnp.einsum("npq,pk->nkq", grid, outer_table, precision=highest)
    section_re = section_one[:, :outer]
    section_im = -section_one[:, outer:]
    angle_twist = (
        2.0
        * math.pi
        / total
        * (outer_index[:, None] * inner_index[None, :] % total).astype(jnp.float32)
    )
    twist_cos = jnp.cos(angle_twist)
    twist_sin = jnp.sin(angle_twist)
    rotated = jnp.stack(
        [
            section_re * twist_cos + section_im * twist_sin,
            section_im * twist_cos - section_re * twist_sin,
        ]
    )
    angle_inner = (
        2.0
        * math.pi
        / inner
        * (inner_index[:, None] * half_index[None, :] % inner).astype(jnp.float32)
    )
    inner_table = jnp.concatenate([jnp.cos(angle_inner), jnp.sin(angle_inner)], axis=1)
    section_two = jnp.einsum("snkq,qm->snkm", rotated, inner_table, precision=highest)
    final_re = section_two[0, :, :, :half_inner] + section_two[1, :, :, half_inner:]
    final_im = section_two[1, :, :, :half_inner] - section_two[0, :, :, half_inner:]
    spectrum_power = (final_re * final_re + final_im * final_im) / (C * total)
    spectrum_power = jnp.transpose(spectrum_power, (0, 2, 1)).reshape(count, total // 2)
    harmonic = jnp.sum(jnp.take(spectrum_power, harmonic_bins, axis=1), axis=1) / HARM
    return spectrum_power, harmonic


def on_device(filterbank, first_rows, second_rows, shifts, harmonic_bins):
    channels = filterbank.shape[0]
    samples = filterbank.shape[1]
    local_levels = channels.bit_length() - 1
    chan_count = lax.axis_size("chan")
    tm_count = lax.axis_size("tm")
    cross_levels = chan_count.bit_length() - 1
    levels = local_levels + cross_levels
    rim = lax.ppermute(
        filterbank[:, samples - RAW_HALO :],
        "tm",
        [(source, source + 1) for source in range(tm_count - 1)],
    )
    widened = jnp.concatenate([rim, filterbank], axis=1)
    local_plan = [(2**level, 2 ** (level + 1), channels) for level in range(local_levels)]
    band = run_levels(
        widened.astype(jnp.float32),
        first_rows[:local_levels, :channels],
        second_rows[:local_levels, :channels],
        shifts[:local_levels, :channels],
        local_plan,
    )
    sub = samples // chan_count
    window = sub + SUB_HALO
    base = RAW_HALO - SUB_HALO
    pieces = jnp.stack(
        [band[:, base + sub * dest : base + sub * dest + window] for dest in range(chan_count)]
    )
    layers = lax.all_to_all(pieces, "chan", split_axis=0, concat_axis=0, tiled=True)
    cross_plan = []
    bands = chan_count
    for level in range(local_levels, levels):
        bands //= 2
        rows_out = min(2 ** (level + 1), NDM)
        cross_plan.append((min(2**level, NDM), rows_out, bands * rows_out))
    plane = run_levels(
        layers.reshape(chan_count * channels, window),
        first_rows[local_levels:],
        second_rows[local_levels:],
        shifts[local_levels:],
        cross_plan,
    )[:, SUB_HALO:]
    groups = chan_count * tm_count
    share = NDM // groups
    outgoing = plane.reshape(groups, share, sub)
    incoming = lax.all_to_all(outgoing, ("chan", "tm"), split_axis=0, concat_axis=0, tiled=True)
    series = (
        incoming.reshape(chan_count, tm_count, share, sub)
        .transpose(2, 1, 0, 3)
        .reshape(share, tm_count * samples)
    )
    return spectra(series, harmonic_bins)


def solution(mesh):
    in_specs = (P("chan", "tm"), P(), P(), P(), P())
    out_specs = (P(("chan", "tm"), None), P(("chan", "tm"), None))
    return jax.shard_map(
        on_device, mesh=mesh, in_specs=in_specs, out_specs=out_specs, check_vma=False
    )
```

profile of v0, /device:TPU:1, one launch (start us, length us, event | category | flops | bytes accessed | tf_op | source)
XLA Modules:
  0.0 313.8 jit_solution(14611826962540548477)
XLA Ops:
  0.6 0.9 slice.96
  1.5 4.5 %collective-permute-start = (bf16[256,256]{1,0:T(8,128)(2,1)S(1)}, bf16[256,256]{1,0:T(8,128)(2,1)S(1)}, u32[]{:S(2)}, u32[]{:S(2)}) collective-permute-start(bf16[256,256]{1,0:T(8,128)(2,1)S(1)} %slice.96), channel_id=1, source_target_pairs={{0,1},{1,2},{2,3},{3,4},{4,5},{5,6},{6,7},{8,9},{9,10},{10,11},{11... | collective-permute-start | bytes 393224 | tf_op jit(solution)/shard_map/ppermute | solution.py:140
  6.1 0.7 slice.93.first_ref
  6.8 0.7 slice.94.second_ref
  7.5 0.7 slice.95.shift_ref
  8.2 1.1 maximum_convert_fusion.x_ref
  9.3 44.7 %shard_map.68 = f32[256,1280]{1,0:T(8,128)S(1)} custom-call(s32[8,256]{1,0:T(8,128)S(1)} %slice.93.first_ref, s32[8,256]{1,0:T(8,128)S(1)} %slice.94.second_ref, s32[8,256]{1,0:T(8,128)S(1)} %slice.95.shift_ref, f32[256,1280]{1,0:T(8,128)S(1)} %maximum_convert_fusion.x_ref), custom_call_target="tpu_custom_call" | custom-call | tf_op jit(solution)/shard_map/pallas_call | solution.py:71
  54.0 0.7 fusion.24
  54.7 0.7 fusion.23
  55.4 0.7 fusion.22
  56.1 0.7 fusion.21
  56.8 0.7 fusion.20
  57.6 0.7 fusion.19
  58.2 0.8 fusion.18
  59.0 0.7 fusion.17
  59.6 0.7 fusion.16
  60.4 0.7 fusion.15
  61.0 0.8 fusion.14
  61.8 0.6 fusion.13
  62.4 0.8 fusion.12
  63.2 0.7 fusion.11
  63.8 0.8 fusion.10
  64.6 0.7 fusion.9
  65.2 7.9 %all-to-all-start = ((f32[16,256,128]{2,1,0:T(8,128)}), f32[16,256,128]{2,1,0:T(8,128)S(1)}, u32[]{:S(2)}, u32[]{:S(2)}) async-start(f32[16,256,128]{2,1,0:T(8,128)} %fusion.9), calls=%async_computation | async-start | bytes 4194304 | tf_op jit(solution)/shard_map/all_to_all | solution.py:160
  73.2 0.8 slice.90.first_ref
  74.0 0.8 slice.91.second_ref
  74.8 0.8 slice.92.shift_ref
  75.9 0.3 fusion.41
  76.1 26.5 %all-to-all-done = f32[16,256,128]{2,1,0:T(8,128)S(1)} async-done(((f32[16,256,128]{2,1,0:T(8,128)}), f32[16,256,128]{2,1,0:T(8,128)S(1)}, u32[]{:S(2)}, u32[]{:S(2)}) %all-to-all-start) | async-done | bytes 2097184 | tf_op jit(solution)/shard_map/all_to_all | solution.py:160
  102.7 164.9 %shard_map.69 = f32[2048,128]{1,0:T(8,128)S(1)} custom-call(s32[4,2048]{1,0:T(4,128)S(1)} %slice.90.first_ref, s32[4,2048]{1,0:T(4,128)S(1)} %slice.91.second_ref, s32[4,2048]{1,0:T(4,128)S(1)} %slice.92.shift_ref, f32[4096,128]{1,0:T(8,128)S(1)} %bitcast.97), custom_call_target="tpu_custom_call" | custom-call | tf_op jit(solution)/shard_map/pallas_call | solution.py:71
  267.6 0.3 slice.138
  267.9 1.4 reshape.80
  269.4 6.7 %all-to-all-start.1 = ((f32[128,1,1024]{2,1,0:T(1,128)}), f32[128,1,1024]{2,1,0:T(1,128)S(1)}, u32[]{:S(2)}, u32[]{:S(2)}) async-start(f32[128,1,1024]{2,1,0:T(1,128)} %reshape.80), calls=%async_computation.1 | async-start | bytes 1048576 | tf_op jit(solution)/shard_map/all_to_all | solution.py:177
  276.2 13.5 %all-to-all-done.1 = f32[128,1,1024]{2,1,0:T(1,128)S(1)} async-done(((f32[128,1,1024]{2,1,0:T(1,128)}), f32[128,1,1024]{2,1,0:T(1,128)S(1)}, u32[]{:S(2)}, u32[]{:S(2)}) %all-to-all-start.1) | async-done | bytes 524320 | tf_op jit(solution)/shard_map/all_to_all | solution.py:177
  289.8 0.5 broadcast.105
  290.3 1.9 reduce.2
  292.2 0.3 reshape.81
  292.4 0.6 copy.19
  293.1 0.2 reshape_reshape.3
  293.3 1.1 convolution_bitcast_fusion
  294.5 1.0 fusion
  295.6 0.3 fusion.7
  295.9 0.2 copy.13
  296.1 0.2 reshape.67
  296.3 0.6 copy.14
  296.9 14.1 %gather_fusion = f32[4096,16]{1,0:T(8,128)} fusion(f32[16,4096]{0,1:T(8,128)S(1)} %copy.14, s32[4096]{0:T(1024)S(1)} %broadcast_clamp_fusion), kind=kCustom, calls=%fused_computation | custom fusion | bytes 540672 | tf_op jit(solution)/shard_map/jit(_take)/gather | solution.py:128
  311.1 1.9 select_reduce_fusion
  313.0 0.7 copy.15
  (13 shorter events, 0.5 us)
Async XLA Ops:
  1.5 6.6 %collective-permute-start = (bf16[256,256]{1,0:T(8,128)(2,1)S(1)}, bf16[256,256]{1,0:T(8,128)(2,1)S(1)}, u32[]{:S(2)}, u32[]{:S(2)}) collective-permute-start(bf16[256,256]{1,0:T(8,128)(2,1)S(1)} %slice.96), channel_id=1, source_target_pairs={{0,1},{1,2},{2,3},{3,4},{4,5},{5,6},{6,7},{8,9},{9,10},{10,11},{11... | collective-permute-start | bytes 393224 | tf_op jit(solution)/shard_map/ppermute | solution.py:140
  65.2 10.4 %copy-start.1 = (s32[8,512]{1,0:T(8,128)S(1)}, s32[8,512]{1,0:T(8,128)}, u32[]{:S(2)}) copy-start(s32[8,512]{1,0:T(8,128)} %param.9) | copy-start | bytes 49156
  65.2 37.4 %all-to-all-start = ((f32[16,256,128]{2,1,0:T(8,128)}), f32[16,256,128]{2,1,0:T(8,128)S(1)}, u32[]{:S(2)}, u32[]{:S(2)}) async-start(f32[16,256,128]{2,1,0:T(8,128)} %fusion.9), calls=%async_computation | async-start | bytes 4194304 | tf_op jit(solution)/shard_map/all_to_all | solution.py:160
  269.4 20.4 %all-to-all-start.1 = ((f32[128,1,1024]{2,1,0:T(1,128)}), f32[128,1,1024]{2,1,0:T(1,128)S(1)}, u32[]{:S(2)}, u32[]{:S(2)}) async-start(f32[128,1,1024]{2,1,0:T(1,128)} %reshape.80), calls=%async_computation.1 | async-start | bytes 1048576 | tf_op jit(solution)/shard_map/all_to_all | solution.py:177
  296.3 14.7 %copy-start = (f32[16,4096]{1,0:T(8,128)}, f32[16,4096]{1,0:T(8,128)S(1)}, u32[]{:S(2)}) copy-start(f32[16,4096]{1,0:T(8,128)S(1)} %reshape.67) | copy-start | bytes 786436
where the time goes:
time: 314 us
  Pallas kernels  210 us (67%)
  waiting for transfers between devices  40.1 us (13%)
  local copies, waits for them, and re-layouts  36 us (11%)
  starting transfers between devices  19.1 us (6%)
  other arithmetic  6.06 us (2%)
    pallas_call x2, Pallas kernels, run_levels(): pl.pallas_call(functools.partial(levels_kernel, plan), out_shape=jax.Shap...  210 us
    all_to_all x1, waiting for transfers between devices, on_device(): lax.all_to_all(pieces, 'chan', split_axis=0, concat_axis=0, tiled=True)  26.5 us
    gather x1, local copies, waits for them, and re-layouts, spectra(): jnp.take(spectrum_power, harmonic_bins, axis=1)  14.1 us
    all_to_all x1, waiting for transfers between devices, on_device(): lax.all_to_all(outgoing, ('chan', 'tm'), split_axis=0, concat_axis=0, til...  13.5 us
    unnamed x23, local copies, waits for them, and re-layouts  13 us
    all_to_all x1, starting transfers between devices, on_device(): lax.all_to_all(pieces, 'chan', split_axis=0, concat_axis=0, tiled=True)  7.9 us
    all_to_all x1, starting transfers between devices, on_device(): lax.all_to_all(outgoing, ('chan', 'tm'), split_axis=0, concat_axis=0, til...  6.67 us
  transfers between devices with their start and end apart: 3, of which 2 were waited for; matrix products, arithmetic and copies ran while one was open for 2% of the time, Pallas kernels for 0%

commit v1 on v0

--- a/solution.py
+++ b/solution.py
@@ -15,6 +15,7 @@
 HARM = 8
 RAW_HALO = 256
 SUB_HALO = 64
+TILE = 256
 
 
 def shift_right(value, amount):
@@ -76,6 +77,78 @@
         scratch_shapes=[pltpu.VMEM((buf_rows, width), jnp.float32)] * 2,
         compiler_params=pltpu.CompilerParams(vmem_limit_bytes=48 * 1024 * 1024),
     )(first_rows, second_rows, shifts, state)
+
+
+def split_three(block):
+    high = block.astype(jnp.bfloat16)
+    rest = block - high.astype(jnp.float32)
+    middle = rest.astype(jnp.bfloat16)
+    low = (rest - middle.astype(jnp.float32)).astype(jnp.bfloat16)
+    return high, middle, low
+
+
+def matmul_kernel(plan, x_ref, *refs):
+    count = len(plan)
+    tables = refs[: 3 * count]
+    out_ref, buf_a, buf_b, parts = refs[3 * count :]
+    source = x_ref
+    for step, (row_in, row_out, bands_out, depth) in enumerate(plan):
+        pick_low, pick_high, delay = tables[3 * step : 3 * step + 3]
+        target = out_ref if step == count - 1 else (buf_a, buf_b)[step % 2]
+        for band in range(bands_out):
+            for side in range(2):
+                block = source[pl.ds((2 * band + side) * row_in, depth), :]
+                for piece, value in enumerate(split_three(block)):
+                    parts[side, piece, pl.ds(0, depth), :] = value
+
+            def tile(index, carry, target=target, band=band, depth=depth, row_out=row_out,
+                     pick_low=pick_low, pick_high=pick_high, delay=delay):
+                rows = pl.ds(pl.multiple_of(index * TILE, TILE), TILE)
+                low_sel = pick_low[rows, :]
+                high_sel = pick_high[rows, :]
+                lower = None
+                upper = None
+                for piece in range(3):
+                    term = jnp.dot(low_sel, parts[0, piece, pl.ds(0, depth), :],
+                                   preferred_element_type=jnp.float32)
+                    lower = term if lower is None else lower + term
+                    term = jnp.dot(high_sel, parts[1, piece, pl.ds(0, depth), :],
+                                   preferred_element_type=jnp.float32)
+                    upper = term if upper is None else upper + term
+                amount = delay[rows, :]
+                for bit in (1, 2, 4, 8):
+                    upper = jnp.where((amount & bit) != 0, pltpu.roll(upper, bit, 1), upper)
+                start = pl.multiple_of(band * row_out + index * TILE, TILE)
+                target[pl.ds(start, TILE), :] = lower + upper
+                return carry
+
+            lax.fori_loop(0, row_out // TILE, tile, 0)
+        source = target
+
+
+def run_matmul_levels(state, first_rows, second_rows, shifts, levels, plan):
+    width = state.shape[1]
+    tables = []
+    for level, (row_in, row_out, bands_out, depth) in zip(levels, plan):
+        columns = jnp.arange(depth, dtype=jnp.int32)[None, :]
+        tables.append((first_rows[level, :row_out, None] == columns).astype(jnp.bfloat16))
+        tables.append((second_rows[level, :row_out, None] == columns).astype(jnp.bfloat16))
+        tables.append(shifts[level, :row_out, None])
+    buf_rows = max(p[1] * p[2] for p in plan)
+    depth_most = max(p[3] for p in plan)
+    vmem = pl.BlockSpec(memory_space=pltpu.VMEM)
+    return pl.pallas_call(
+        functools.partial(matmul_kernel, plan),
+        out_shape=jax.ShapeDtypeStruct((plan[-1][1] * plan[-1][2], width), jnp.float32),
+        in_specs=[vmem] * (1 + len(tables)),
+        out_specs=vmem,
+        scratch_shapes=[
+            pltpu.VMEM((buf_rows, width), jnp.float32),
+            pltpu.VMEM((buf_rows, width), jnp.float32),
+            pltpu.VMEM((2, 3, depth_most, width), jnp.bfloat16),
+        ],
+        compiler_params=pltpu.CompilerParams(vmem_limit_bytes=60 * 1024 * 1024),
+    )(state, *tables)
 
 
 def spectra(series, harmonic_bins):
@@ -162,13 +235,14 @@
     bands = chan_count
     for level in range(local_levels, levels):
         bands //= 2
-        rows_out = min(2 ** (level + 1), NDM)
-        cross_plan.append((min(2**level, NDM), rows_out, bands * rows_out))
-    plane = run_levels(
+        rows_in = min(2**level, NDM)
+        cross_plan.append((rows_in, min(2 ** (level + 1), NDM), bands, min(rows_in, NDM // 2)))
+    plane = run_matmul_levels(
         layers.reshape(chan_count * channels, window),
-        first_rows[local_levels:],
-        second_rows[local_levels:],
-        shifts[local_levels:],
+        first_rows,
+        second_rows,
+        shifts,
+        list(range(local_levels, levels)),
         cross_plan,
     )[:, SUB_HALO:]
     groups = chan_count * tm_count

time: 314 us -> 233 us (0.74)
  Pallas kernels: 210 us -> 109 us
  local copies, waits for them, and re-layouts: 36 us -> 48.1 us
  other arithmetic: 6.06 us -> 16.3 us
  waiting for transfers between devices: 40.1 us -> 33.2 us
    pallas_call x2 -> x1, Pallas kernels: 210 us -> 44.7 us  [run_levels(): pl.pallas_call(functools.partial(levels_kernel, plan), out_shape=jax.Shap...]
    pallas_call x0 -> x1, Pallas kernels: none -> 64.1 us  [run_matmul_levels(): pl.pallas_call(functools.partial(matmul_kernel, plan), out_shape=jax.Shap...]
    convert_element_type x0 -> x4, other arithmetic: none -> 10.6 us  [run_matmul_levels(): (first_rows[level, :row_out, None] == columns).astype(jnp.bfloat16)]
    another operation x0 -> x7, local copies, waits for them, and re-layouts: none -> 7.06 us  [run_matmul_levels(): tables.append(shifts[level, :row_out, None])]
    all_to_all x1, waiting for transfers between devices: 26.5 us -> 19.6 us  [on_device(): lax.all_to_all(pieces, 'chan', split_axis=0, concat_axis=0, tiled=True)]
    slice x4 -> x7, local copies, waits for them, and re-layouts: 2.87 us -> 6.4 us  [the longest x3 2.42 us: run_matmul_levels(): first_rows[level, :row_out, None] == columns]
    all_to_all x1, starting transfers between devices: 6.67 us -> 9.89 us  [on_device(): lax.all_to_all(outgoing, ('chan', 'tm'), split_axis=0, concat_axis=0, til...]
    unnamed x23 -> x27, local copies, waits for them, and re-layouts: 13 us -> 14.5 us
  transfers between devices with their start and end apart: 3 -> 3, of which waited for: 2 -> 2; matrix products, arithmetic and copies ran while one was open for 2% -> 11% of each run, Pallas kernels for 0% -> 0%
where the time goes in v1:
time: 233 us; the launch traced here: 232 us
  Pallas kernels  109 us (47%)
  local copies, waits for them, and re-layouts  48.1 us (21%)
  waiting for transfers between devices  33.2 us (14%)
  starting transfers between devices  22.2 us (10%)
  other arithmetic  16.3 us (7%)
    pallas_call x1, Pallas kernels, run_matmul_levels(): pl.pallas_call(functools.partial(matmul_kernel, plan), out_shape=jax.Shap...  64.1 us
    pallas_call x1, Pallas kernels, run_levels(): pl.pallas_call(functools.partial(levels_kernel, plan), out_shape=jax.Shap...  44.7 us
    all_to_all x1, waiting for transfers between devices, on_device(): lax.all_to_all(pieces, 'chan', split_axis=0, concat_axis=0, tiled=True)  19.6 us
    unnamed x27, local copies, waits for them, and re-layouts  14.5 us
    gather x1, local copies, waits for them, and re-layouts, spectra(): jnp.take(spectrum_power, harmonic_bins, axis=1)  14.2 us
    all_to_all x1, waiting for transfers between devices, on_device(): lax.all_to_all(outgoing, ('chan', 'tm'), split_axis=0, concat_axis=0, til...  13.5 us
    convert_element_type x4, other arithmetic, run_matmul_levels(): (first_rows[level, :row_out, None] == columns).astype(jnp.bfloat16)  10.6 us
    all_to_all x1, starting transfers between devices, on_device(): lax.all_to_all(outgoing, ('chan', 'tm'), split_axis=0, concat_axis=0, til...  9.89 us
  transfers between devices with their start and end apart: 3, of which 2 were waited for; matrix products, arithmetic and copies ran while one was open for 11% of the time, Pallas kernels for 0%

profile of v1, /device:TPU:1, one launch (start us, length us, event | category | flops | bytes accessed | tf_op | source)
XLA Modules:
  0.0 231.6 jit_solution(8963550852636667578)
XLA Ops:
  0.6 0.9 slice.120
  1.5 4.5 %collective-permute-start = (bf16[256,256]{1,0:T(8,128)(2,1)S(1)}, bf16[256,256]{1,0:T(8,128)(2,1)S(1)}, u32[]{:S(2)}, u32[]{:S(2)}) collective-permute-start(bf16[256,256]{1,0:T(8,128)(2,1)S(1)} %slice.120), channel_id=1, source_target_pairs={{0,1},{1,2},{2,3},{3,4},{4,5},{5,6},{6,7},{8,9},{9,10},{10,11},{11... | collective-permute-start | bytes 393224 | tf_op jit(solution)/shard_map/ppermute | solution.py:213
  6.1 0.9 fusion.65
  7.0 0.8 slice.140
  7.8 0.9 slice_bitcast_fusion.16
  8.7 0.8 slice_bitcast_fusion.18
  9.5 0.7 slice_bitcast_fusion.19
  10.2 0.8 slice.141
  10.9 0.7 fusion.61
  11.7 1.6 fusion.4
  13.5 0.7 slice.117.first_ref
  14.2 0.7 slice.118.second_ref
  14.9 0.7 slice.119.shift_ref
  15.6 0.7 slice.137
  16.3 0.7 slice.138
  17.0 1.4 copy.18.refs_8_
  18.4 1.4 copy.19.refs_11_
  19.8 1.0 copy.17.refs_5_
  20.8 0.9 copy.16.refs_2_
  22.1 44.7 %shard_map.68 = f32[256,1280]{1,0:T(8,128)S(1)} custom-call(s32[8,256]{1,0:T(8,128)S(1)} %slice.117.first_ref, s32[8,256]{1,0:T(8,128)S(1)} %slice.118.second_ref, s32[8,256]{1,0:T(8,128)S(1)} %slice.119.shift_ref, f32[256,1280]{1,0:T(8,128)S(1)} %maximum_convert_fusion.x_ref), custom_call_target="tpu_custom_call" | custom-call | tf_op jit(solution)/shard_map/pallas_call | solution.py:72
  66.8 0.8 fusion.32
  68.2 0.8 fusion.30
  69.6 0.8 fusion.28
  71.0 0.8 fusion.26
  72.4 0.8 fusion.24
  73.2 0.7 fusion.23
  73.9 0.7 fusion.22
  75.3 0.7 fusion.20
  76.0 0.7 fusion.19
  76.7 0.8 fusion.18
  78.1 7.8 %all-to-all-start = ((f32[16,256,128]{2,1,0:T(8,128)}), f32[16,256,128]{2,1,0:T(8,128)S(1)}, u32[]{:S(2)}, u32[]{:S(2)}) async-start(f32[16,256,128]{2,1,0:T(8,128)} %fusion.17), calls=%async_computation | async-start | bytes 4194304 | tf_op jit(solution)/shard_map/all_to_all | solution.py:233
  85.9 1.0 fusion.15
  86.9 0.9 fusion.64
  87.8 4.0 %fusion = (bf16[2048,1024]{1,0:T(8,128)(2,1)}, bf16[2048,1024]{1,0:T(8,128)(2,1)}) fusion(s32[2048]{0:T(1024)S(1)} %bitcast.120, s32[2048]{0:T(1024)S(1)} %bitcast.122), kind=kLoop, calls=%fused_computation.5 | loop fusion | flops 8388608 | bytes 8404992 | tf_op jit(solution)/shard_map/convert_element_type | solution.py:134
  91.8 4.0 %fusion.2 = (bf16[2048,1024]{1,0:T(8,128)(2,1)}, bf16[2048,1024]{1,0:T(8,128)(2,1)}) fusion(s32[2048]{0:T(1024)S(1)} %bitcast.119, s32[2048]{0:T(1024)S(1)} %bitcast.121), kind=kLoop, calls=%fused_computation.7 | loop fusion | flops 8388608 | bytes 8404992 | tf_op jit(solution)/shard_map/convert_element_type | solution.py:134
  95.8 19.6 %all-to-all-done = f32[16,256,128]{2,1,0:T(8,128)S(1)} async-done(((f32[16,256,128]{2,1,0:T(8,128)}), f32[16,256,128]{2,1,0:T(8,128)S(1)}, u32[]{:S(2)}, u32[]{:S(2)}) %all-to-all-start) | async-done | bytes 2097184 | tf_op jit(solution)/shard_map/all_to_all | solution.py:233
  115.4 1.3 copy-done
  116.8 64.1 %shard_map.69 = f32[2048,128]{1,0:T(8,128)} custom-call(f32[4096,128]{1,0:T(8,128)} %bitcast.113, bf16[512,256]{1,0:T(8,128)(2,1)} %get-tuple-element.20.refs_0_, bf16[512,256]{1,0:T(8,128)(2,1)} %get-tuple-element.21.refs_1_, s32[512,1]{1,0:T(8,128)} %copy.16.refs_2_, bf16[1024,512]{1,0:T(8,128)(2,1)} %get-tuple-element.18.refs_3_, ...), custom_call_target="tpu_custom_call" | custom-call | tf_op jit(solution)/shard_map/pallas_call | solution.py:140
  180.9 1.6 slice.174
  182.4 1.4 reshape.88
  183.9 9.9 %all-to-all-start.1 = ((f32[128,1,1024]{2,1,0:T(1,128)}), f32[128,1,1024]{2,1,0:T(1,128)S(1)}, u32[]{:S(2)}, u32[]{:S(2)}) async-start(f32[128,1,1024]{2,1,0:T(1,128)} %reshape.88), calls=%async_computation.1 | async-start | bytes 1048576 | tf_op jit(solution)/shard_map/all_to_all | solution.py:251
  194.0 13.5 %all-to-all-done.1 = f32[128,1,1024]{2,1,0:T(1,128)S(1)} async-done(((f32[128,1,1024]{2,1,0:T(1,128)}), f32[128,1,1024]{2,1,0:T(1,128)S(1)}, u32[]{:S(2)}, u32[]{:S(2)}) %all-to-all-start.1) | async-done | bytes 524320 | tf_op jit(solution)/shard_map/all_to_all | solution.py:251
  208.0 1.9 reduce.2
  211.0 1.1 convolution_bitcast_fusion
  212.3 1.0 fusion.6
  214.7 14.2 %gather_fusion = f32[4096,16]{1,0:T(8,128)} fusion(f32[16,4096]{0,1:T(8,128)S(1)} %copy.22, s32[4096]{0:T(1024)S(1)} %broadcast_clamp_fusion), kind=kCustom, calls=%fused_computation | custom fusion | bytes 540672 | tf_op jit(solution)/shard_map/jit(_take)/gather | solution.py:201
  228.9 1.9 select_reduce_fusion
  230.9 0.7 copy.23
  (31 shorter events, 7.8 us)
Async XLA Ops:
  1.5 20.4 %collective-permute-start = (bf16[256,256]{1,0:T(8,128)(2,1)S(1)}, bf16[256,256]{1,0:T(8,128)(2,1)S(1)}, u32[]{:S(2)}, u32[]{:S(2)}) collective-permute-start(bf16[256,256]{1,0:T(8,128)(2,1)S(1)} %slice.120), channel_id=1, source_target_pairs={{0,1},{1,2},{2,3},{3,4},{4,5},{5,6},{6,7},{8,9},{9,10},{10,11},{11... | collective-permute-start | bytes 393224 | tf_op jit(solution)/shard_map/ppermute | solution.py:213
  13.3 8.7 %copy-start.2 = (bf16[256,1024]{1,0:T(8,128)(2,1)S(1)}, bf16[256,1024]{1,0:T(8,128)(2,1)}, u32[]{:S(2)}) copy-start(bf16[256,1024]{1,0:T(8,128)(2,1)} %param.5) | copy-start | bytes 1572868
  78.1 37.3 %all-to-all-start = ((f32[16,256,128]{2,1,0:T(8,128)}), f32[16,256,128]{2,1,0:T(8,128)S(1)}, u32[]{:S(2)}, u32[]{:S(2)}) async-start(f32[16,256,128]{2,1,0:T(8,128)} %fusion.17), calls=%async_computation | async-start | bytes 4194304 | tf_op jit(solution)/shard_map/all_to_all | solution.py:233
  115.4 1.3 copy-start
  180.9 13.1 %copy-start.3 = (s32[8,512]{1,0:T(8,128)S(1)}, s32[8,512]{1,0:T(8,128)}, u32[]{:S(2)}) copy-start(s32[8,512]{1,0:T(8,128)} %param.9) | copy-start | bytes 49156
  183.9 23.6 %all-to-all-start.1 = ((f32[128,1,1024]{2,1,0:T(1,128)}), f32[128,1,1024]{2,1,0:T(1,128)S(1)}, u32[]{:S(2)}, u32[]{:S(2)}) async-start(f32[128,1,1024]{2,1,0:T(1,128)} %reshape.88), calls=%async_computation.1 | async-start | bytes 1048576 | tf_op jit(solution)/shard_map/all_to_all | solution.py:251
  214.1 14.8 %copy-start.1 = (f32[16,4096]{1,0:T(8,128)}, f32[16,4096]{1,0:T(8,128)S(1)}, u32[]{:S(2)}) copy-start(f32[16,4096]{1,0:T(8,128)S(1)} %reshape.75) | copy-start | bytes 786436

commit v2 on v1

--- a/solution.py
+++ b/solution.py
@@ -91,17 +91,23 @@
     count = len(plan)
     tables = refs[: 3 * count]
     out_ref, buf_a, buf_b, parts = refs[3 * count :]
+    width = x_ref.shape[1]
     source = x_ref
     for step, (row_in, row_out, bands_out, depth) in enumerate(plan):
         pick_low, pick_high, delay = tables[3 * step : 3 * step + 3]
         target = out_ref if step == count - 1 else (buf_a, buf_b)[step % 2]
-        for band in range(bands_out):
-            for side in range(2):
-                block = source[pl.ds((2 * band + side) * row_in, depth), :]
-                for piece, value in enumerate(split_three(block)):
-                    parts[side, piece, pl.ds(0, depth), :] = value
-
-            def tile(index, carry, target=target, band=band, depth=depth, row_out=row_out,
+        group = 2 if bands_out >= 2 else 1
+        lanes = group * width
+        for first_band in range(0, bands_out, group):
+            for member in range(group):
+                band = first_band + member
+                for side in range(2):
+                    block = source[pl.ds((2 * band + side) * row_in, depth), :]
+                    for piece, value in enumerate(split_three(block)):
+                        parts[side, piece, pl.ds(0, depth), pl.ds(member * width, width)] = value
+
+            def tile(index, carry, target=target, first_band=first_band, depth=depth,
+                     row_out=row_out, group=group, lanes=lanes,
                      pick_low=pick_low, pick_high=pick_high, delay=delay):
                 rows = pl.ds(pl.multiple_of(index * TILE, TILE), TILE)
                 low_sel = pick_low[rows, :]
@@ -109,17 +115,19 @@
                 lower = None
                 upper = None
                 for piece in range(3):
-                    term = jnp.dot(low_sel, parts[0, piece, pl.ds(0, depth), :],
+                    term = jnp.dot(low_sel, parts[0, piece, pl.ds(0, depth), pl.ds(0, lanes)],
                                    preferred_element_type=jnp.float32)
                     lower = term if lower is None else lower + term
-                    term = jnp.dot(high_sel, parts[1, piece, pl.ds(0, depth), :],
+                    term = jnp.dot(high_sel, parts[1, piece, pl.ds(0, depth), pl.ds(0, lanes)],
                                    preferred_element_type=jnp.float32)
                     upper = term if upper is None else upper + term
                 amount = delay[rows, :]
                 for bit in (1, 2, 4, 8):
                     upper = jnp.where((amount & bit) != 0, pltpu.roll(upper, bit, 1), upper)
-                start = pl.multiple_of(band * row_out + index * TILE, TILE)
-                target[pl.ds(start, TILE), :] = lower + upper
+                merged = lower + upper
+                for member in range(group):
+                    start = pl.multiple_of((first_band + member) * row_out + index * TILE, TILE)
+                    target[pl.ds(start, TILE), :] = merged[:, member * width : (member + 1) * width]
                 return carry
 
             lax.fori_loop(0, row_out // TILE, tile, 0)
@@ -145,7 +153,7 @@
         scratch_shapes=[
             pltpu.VMEM((buf_rows, width), jnp.float32),
             pltpu.VMEM((buf_rows, width), jnp.float32),
-            pltpu.VMEM((2, 3, depth_most, width), jnp.bfloat16),
+            pltpu.VMEM((2, 3, depth_most, 2 * width), jnp.bfloat16),
         ],
         compiler_params=pltpu.CompilerParams(vmem_limit_bytes=60 * 1024 * 1024),
     )(state, *tables)

time: 233 us -> 212 us (0.910)
  Pallas kernels: 109 us -> 87.9 us
    pallas_call x1, Pallas kernels: 64.1 us -> 43.2 us  [run_matmul_levels(): pl.pallas_call(functools.partial(matmul_kernel, plan), out_shape=jax.Shap...]
  transfers between devices with their start and end apart: 3 -> 3, of which waited for: 2 -> 2; matrix products, arithmetic and copies ran while one was open for 11% -> 12% of each run, Pallas kernels for 0% -> 0%
where the time goes in v2:
time: 212 us; the launch traced here: 211 us
  Pallas kernels  87.9 us (41%)
  local copies, waits for them, and re-layouts  48.1 us (23%)
  waiting for transfers between devices  33.2 us (16%)
  starting transfers between devices  22.2 us (10%)
  other arithmetic  16.3 us (8%)
  matrix products  2.15 us (1%)
    pallas_call x1, Pallas kernels, run_levels(): pl.pallas_call(functools.partial(levels_kernel, plan), out_shape=jax.Shap...  44.7 us
    pallas_call x1, Pallas kernels, run_matmul_levels(): pl.pallas_call(functools.partial(matmul_kernel, plan), out_shape=jax.Shap...  43.2 us
    all_to_all x1, waiting for transfers between devices, on_device(): lax.all_to_all(pieces, 'chan', split_axis=0, concat_axis=0, tiled=True)  19.6 us
    unnamed x27, local copies, waits for them, and re-layouts  14.5 us
    gather x1, local copies, waits for them, and re-layouts, spectra(): jnp.take(spectrum_power, harmonic_bins, axis=1)  14.2 us
    all_to_all x1, waiting for transfers between devices, on_device(): lax.all_to_all(outgoing, ('chan', 'tm'), split_axis=0, concat_axis=0, til...  13.5 us
    convert_element_type x4, other arithmetic, run_matmul_levels(): (first_rows[level, :row_out, None] == columns).astype(jnp.bfloat16)  10.6 us
    all_to_all x1, starting transfers between devices, on_device(): lax.all_to_all(outgoing, ('chan', 'tm'), split_axis=0, concat_axis=0, til...  9.9 us
  transfers between devices with their start and end apart: 3, of which 2 were waited for; matrix products, arithmetic and copies ran while one was open for 12% of the time, Pallas kernels for 0%

profile of v2, /device:TPU:1, one launch (start us, length us, event | category | flops | bytes accessed | tf_op | source)
XLA Modules:
  0.0 210.6 jit_solution(13568128760744631097)
XLA Ops:
  0.6 0.9 slice.120
  1.5 4.5 %collective-permute-start = (bf16[256,256]{1,0:T(8,128)(2,1)S(1)}, bf16[256,256]{1,0:T(8,128)(2,1)S(1)}, u32[]{:S(2)}, u32[]{:S(2)}) collective-permute-start(bf16[256,256]{1,0:T(8,128)(2,1)S(1)} %slice.120), channel_id=1, source_target_pairs={{0,1},{1,2},{2,3},{3,4},{4,5},{5,6},{6,7},{8,9},{9,10},{10,11},{11... | collective-permute-start | bytes 393224 | tf_op jit(solution)/shard_map/ppermute | solution.py:221
  6.1 0.9 fusion.65
  7.0 0.8 slice.140
  7.8 0.9 slice_bitcast_fusion.16
  8.7 0.8 slice_bitcast_fusion.18
  9.5 0.7 slice_bitcast_fusion.19
  10.2 0.8 slice.141
  10.9 0.7 fusion.61
  11.7 1.6 fusion.4
  13.5 0.7 slice.117.first_ref
  14.2 0.7 slice.118.second_ref
  14.9 0.7 slice.119.shift_ref
  15.6 0.7 slice.137
  16.3 0.7 slice.138
  17.0 1.4 copy.18.refs_8_
  18.4 1.4 copy.19.refs_11_
  19.8 1.0 copy.17.refs_5_
  20.8 0.9 copy.16.refs_2_
  22.1 44.7 %shard_map.68 = f32[256,1280]{1,0:T(8,128)S(1)} custom-call(s32[8,256]{1,0:T(8,128)S(1)} %slice.117.first_ref, s32[8,256]{1,0:T(8,128)S(1)} %slice.118.second_ref, s32[8,256]{1,0:T(8,128)S(1)} %slice.119.shift_ref, f32[256,1280]{1,0:T(8,128)S(1)} %maximum_convert_fusion.x_ref), custom_call_target="tpu_custom_call" | custom-call | tf_op jit(solution)/shard_map/pallas_call | solution.py:72
  66.8 0.8 fusion.32
  68.2 0.8 fusion.30
  69.6 0.8 fusion.28
  71.0 0.8 fusion.26
  72.4 0.8 fusion.24
  73.2 0.7 fusion.23
  73.9 0.7 fusion.22
  75.3 0.7 fusion.20
  76.0 0.7 fusion.19
  76.7 0.8 fusion.18
  78.1 7.8 %all-to-all-start = ((f32[16,256,128]{2,1,0:T(8,128)}), f32[16,256,128]{2,1,0:T(8,128)S(1)}, u32[]{:S(2)}, u32[]{:S(2)}) async-start(f32[16,256,128]{2,1,0:T(8,128)} %fusion.17), calls=%async_computation | async-start | bytes 4194304 | tf_op jit(solution)/shard_map/all_to_all | solution.py:241
  85.9 1.0 fusion.15
  86.9 0.9 fusion.64
  87.8 4.0 %fusion = (bf16[2048,1024]{1,0:T(8,128)(2,1)}, bf16[2048,1024]{1,0:T(8,128)(2,1)}) fusion(s32[2048]{0:T(1024)S(1)} %bitcast.120, s32[2048]{0:T(1024)S(1)} %bitcast.122), kind=kLoop, calls=%fused_computation.5 | loop fusion | flops 8388608 | bytes 8404992 | tf_op jit(solution)/shard_map/convert_element_type | solution.py:142
  91.8 4.0 %fusion.2 = (bf16[2048,1024]{1,0:T(8,128)(2,1)}, bf16[2048,1024]{1,0:T(8,128)(2,1)}) fusion(s32[2048]{0:T(1024)S(1)} %bitcast.119, s32[2048]{0:T(1024)S(1)} %bitcast.121), kind=kLoop, calls=%fused_computation.7 | loop fusion | flops 8388608 | bytes 8404992 | tf_op jit(solution)/shard_map/convert_element_type | solution.py:142
  95.8 19.6 %all-to-all-done = f32[16,256,128]{2,1,0:T(8,128)S(1)} async-done(((f32[16,256,128]{2,1,0:T(8,128)}), f32[16,256,128]{2,1,0:T(8,128)S(1)}, u32[]{:S(2)}, u32[]{:S(2)}) %all-to-all-start) | async-done | bytes 2097184 | tf_op jit(solution)/shard_map/all_to_all | solution.py:241
  115.4 1.3 copy-done
  116.8 43.2 %shard_map.69 = f32[2048,128]{1,0:T(8,128)} custom-call(f32[4096,128]{1,0:T(8,128)} %bitcast.113, bf16[512,256]{1,0:T(8,128)(2,1)} %get-tuple-element.20.refs_0_, bf16[512,256]{1,0:T(8,128)(2,1)} %get-tuple-element.21.refs_1_, s32[512,1]{1,0:T(8,128)} %copy.16.refs_2_, bf16[1024,512]{1,0:T(8,128)(2,1)} %get-tuple-element.18.refs_3_, ...), custom_call_target="tpu_custom_call" | custom-call | tf_op jit(solution)/shard_map/pallas_call | solution.py:148
  159.9 1.6 slice.174
  161.5 1.4 reshape.88
  162.9 9.9 %all-to-all-start.1 = ((f32[128,1,1024]{2,1,0:T(1,128)}), f32[128,1,1024]{2,1,0:T(1,128)S(1)}, u32[]{:S(2)}, u32[]{:S(2)}) async-start(f32[128,1,1024]{2,1,0:T(1,128)} %reshape.88), calls=%async_computation.1 | async-start | bytes 1048576 | tf_op jit(solution)/shard_map/all_to_all | solution.py:259
  173.0 13.5 %all-to-all-done.1 = f32[128,1,1024]{2,1,0:T(1,128)S(1)} async-done(((f32[128,1,1024]{2,1,0:T(1,128)}), f32[128,1,1024]{2,1,0:T(1,128)S(1)}, u32[]{:S(2)}, u32[]{:S(2)}) %all-to-all-start.1) | async-done | bytes 524320 | tf_op jit(solution)/shard_map/all_to_all | solution.py:259
  187.1 1.9 reduce.2
  190.1 1.1 convolution_bitcast_fusion
  191.3 1.0 fusion.6
  193.7 14.2 %gather_fusion = f32[4096,16]{1,0:T(8,128)} fusion(f32[16,4096]{0,1:T(8,128)S(1)} %copy.22, s32[4096]{0:T(1024)S(1)} %broadcast_clamp_fusion), kind=kCustom, calls=%fused_computation | custom fusion | bytes 540672 | tf_op jit(solution)/shard_map/jit(_take)/gather | solution.py:209
  207.9 1.9 select_reduce_fusion
  209.9 0.7 copy.23
  (31 shorter events, 7.8 us)
Async XLA Ops:
  1.5 20.4 %collective-permute-start = (bf16[256,256]{1,0:T(8,128)(2,1)S(1)}, bf16[256,256]{1,0:T(8,128)(2,1)S(1)}, u32[]{:S(2)}, u32[]{:S(2)}) collective-permute-start(bf16[256,256]{1,0:T(8,128)(2,1)S(1)} %slice.120), channel_id=1, source_target_pairs={{0,1},{1,2},{2,3},{3,4},{4,5},{5,6},{6,7},{8,9},{9,10},{10,11},{11... | collective-permute-start | bytes 393224 | tf_op jit(solution)/shard_map/ppermute | solution.py:221
  13.3 8.7 %copy-start.2 = (bf16[256,1024]{1,0:T(8,128)(2,1)S(1)}, bf16[256,1024]{1,0:T(8,128)(2,1)}, u32[]{:S(2)}) copy-start(bf16[256,1024]{1,0:T(8,128)(2,1)} %param.5) | copy-start | bytes 1572868
  78.1 37.3 %all-to-all-start = ((f32[16,256,128]{2,1,0:T(8,128)}), f32[16,256,128]{2,1,0:T(8,128)S(1)}, u32[]{:S(2)}, u32[]{:S(2)}) async-start(f32[16,256,128]{2,1,0:T(8,128)} %fusion.17), calls=%async_computation | async-start | bytes 4194304 | tf_op jit(solution)/shard_map/all_to_all | solution.py:241
  115.4 1.3 copy-start
  159.9 13.1 %copy-start.3 = (s32[8,512]{1,0:T(8,128)S(1)}, s32[8,512]{1,0:T(8,128)}, u32[]{:S(2)}) copy-start(s32[8,512]{1,0:T(8,128)} %param.9) | copy-start | bytes 49156
  162.9 23.6 %all-to-all-start.1 = ((f32[128,1,1024]{2,1,0:T(1,128)}), f32[128,1,1024]{2,1,0:T(1,128)S(1)}, u32[]{:S(2)}, u32[]{:S(2)}) async-start(f32[128,1,1024]{2,1,0:T(1,128)} %reshape.88), calls=%async_computation.1 | async-start | bytes 1048576 | tf_op jit(solution)/shard_map/all_to_all | solution.py:259
  193.1 14.8 %copy-start.1 = (f32[16,4096]{1,0:T(8,128)}, f32[16,4096]{1,0:T(8,128)S(1)}, u32[]{:S(2)}) copy-start(f32[16,4096]{1,0:T(8,128)S(1)} %reshape.75) | copy-start | bytes 786436

commit v3 on v2

--- a/solution.py
+++ b/solution.py
@@ -206,7 +206,20 @@
     final_im = section_two[1, :, :, :half_inner] - section_two[0, :, :, half_inner:]
     spectrum_power = (final_re * final_re + final_im * final_im) / (C * total)
     spectrum_power = jnp.transpose(spectrum_power, (0, 2, 1)).reshape(count, total // 2)
-    harmonic = jnp.sum(jnp.take(spectrum_power, harmonic_bins, axis=1), axis=1) / HARM
+    power_t = jnp.transpose(spectrum_power)
+    fundamentals = harmonic_bins.shape[1]
+    fundamental = jnp.arange(fundamentals, dtype=jnp.int32)
+    total_t = None
+    for order in range(HARM):
+        stride = order + 1
+        offset = (harmonic_bins[order] - stride * fundamental)[:, None]
+        for phase in range(stride):
+            picked = lax.slice(
+                power_t, (phase, 0), (phase + stride * (fundamentals - 1) + 1, count), (stride, 1)
+            )
+            term = jnp.where(offset == phase, picked, 0.0)
+            total_t = term if total_t is None else total_t + term
+    harmonic = jnp.transpose(total_t) / HARM
     return spectrum_power, harmonic
 
 
@@ -225,12 +238,9 @@
     )
     widened = jnp.concatenate([rim, filterbank], axis=1)
     local_plan = [(2**level, 2 ** (level + 1), channels) for level in range(local_levels)]
-    band = run_levels(
-        widened.astype(jnp.float32),
-        first_rows[:local_levels, :channels],
-        second_rows[:local_levels, :channels],
-        shifts[:local_levels, :channels],
-        local_plan,
+    band = run_levels(widened.astype(jnp.float32), first_rows, second_rows, shifts, local_plan)
+    band, first_rows, second_rows, shifts = lax.optimization_barrier(
+        (band, first_rows, second_rows, shifts)
     )
     sub = samples // chan_count
     window = sub + SUB_HALO

time: 212 us -> 220 us (1.038)
  local copies, waits for them, and re-layouts: 48.1 us -> 56.6 us
  Pallas kernels: 87.9 us -> 93.9 us
  waiting for transfers between devices: 33.2 us -> 27.4 us
  starting transfers between devices: 22.2 us -> 19.5 us
    slice x3 -> x36, local copies, waits for them, and re-layouts: 2.12 us -> 33.4 us  [the longest x35 32.4 us: spectra(): lax.slice(power_t, (phase, 0), (phase + stride * (fundamentals - 1) + 1,...]
    gather x1 -> x0, local copies, waits for them, and re-layouts: 14.2 us -> none  [spectra(): jnp.take(spectrum_power, harmonic_bins, axis=1)]
    pallas_call x1, Pallas kernels: 44.7 us -> 50.8 us  [run_levels(): pl.pallas_call(functools.partial(levels_kernel, plan), out_shape=jax.Shap...]
    all_to_all x1, waiting for transfers between devices: 19.6 us -> 13.6 us  [on_device(): lax.all_to_all(pieces, 'chan', split_axis=0, concat_axis=0, tiled=True)]
    convert_element_type x0 -> x2, other arithmetic: none -> 4.73 us  [run_matmul_levels(): (second_rows[level, :row_out, None] == columns).astype(jnp.bfloat16)]
    convert_element_type x4 -> x3, other arithmetic: 10.6 us -> 6.64 us  [run_matmul_levels(): (first_rows[level, :row_out, None] == columns).astype(jnp.bfloat16)]
    all_to_all x1, starting transfers between devices: 9.9 us -> 6.65 us  [on_device(): lax.all_to_all(outgoing, ('chan', 'tm'), split_axis=0, concat_axis=0, til...]
    slice x3 -> x2, local copies, waits for them, and re-layouts: 2.41 us -> 0.01 us  [run_matmul_levels(): second_rows[level, :row_out, None] == columns]
  transfers between devices with their start and end apart: 3 -> 3, of which waited for: 2 -> 3; matrix products, arithmetic and copies ran while one was open for 12% -> 8% of each run, Pallas kernels for 0% -> 0%
where the time goes in v3:
time: 220 us; the launch traced here: 217 us
  Pallas kernels  93.9 us (43%)
  local copies, waits for them, and re-layouts  56.6 us (26%)
  waiting for transfers between devices  27.4 us (12%)
  starting transfers between devices  19.5 us (9%)
  other arithmetic  16.4 us (7%)
    pallas_call x1, Pallas kernels, run_levels(): pl.pallas_call(functools.partial(levels_kernel, plan), out_shape=jax.Shap...  50.8 us
    pallas_call x1, Pallas kernels, run_matmul_levels(): pl.pallas_call(functools.partial(matmul_kernel, plan), out_shape=jax.Shap...  43.1 us
    slice x35, local copies, waits for them, and re-layouts, spectra(): lax.slice(power_t, (phase, 0), (phase + stride * (fundamentals - 1) + 1,...  32.4 us
    unnamed x27, local copies, waits for them, and re-layouts  13.6 us
    all_to_all x1, waiting for transfers between devices, on_device(): lax.all_to_all(pieces, 'chan', split_axis=0, concat_axis=0, tiled=True)  13.6 us
    all_to_all x1, waiting for transfers between devices, on_device(): lax.all_to_all(outgoing, ('chan', 'tm'), split_axis=0, concat_axis=0, til...  13.4 us
    all_to_all x1, starting transfers between devices, on_device(): lax.all_to_all(pieces, 'chan', split_axis=0, concat_axis=0, tiled=True)  8.3 us
    all_to_all x1, starting transfers between devices, on_device(): lax.all_to_all(outgoing, ('chan', 'tm'), split_axis=0, concat_axis=0, til...  6.65 us
  transfers between devices with their start and end apart: 3, of which 3 were waited for; matrix products, arithmetic and copies ran while one was open for 8% of the time, Pallas kernels for 0%

profile of v3, /device:TPU:1, one launch (start us, length us, event | category | flops | bytes accessed | tf_op | source)
XLA Modules:
  0.0 217.3 jit_solution(14491464688058575260)
XLA Ops:
  0.7 1.0 slice.240
  1.6 4.5 %collective-permute-start = (bf16[256,256]{1,0:T(8,128)(2,1)S(1)}, bf16[256,256]{1,0:T(8,128)(2,1)S(1)}, u32[]{:S(2)}, u32[]{:S(2)}) collective-permute-start(bf16[256,256]{1,0:T(8,128)(2,1)S(1)} %slice.240), channel_id=1, source_target_pairs={{0,1},{1,2},{2,3},{3,4},{4,5},{5,6},{6,7},{8,9},{9,10},{10,11},{11... | collective-permute-start | bytes 393224 | tf_op jit(solution)/shard_map/ppermute | solution.py:234
  6.1 1.0 fusion.78
  8.1 1.1 maximum_convert_fusion.x_ref
  9.2 50.8 %shard_map.68 = f32[256,1280]{1,0:T(8,128)S(1)} custom-call(s32[12,2048]{1,0:T(8,128)S(1)} %copy-done, s32[12,2048]{1,0:T(8,128)S(1)} %copy-done.1, s32[12,2048]{1,0:T(8,128)S(1)} %copy-done.2, f32[256,1280]{1,0:T(8,128)S(1)} %maximum_convert_fusion.x_ref), custom_call_target="tpu_custom_call" | custom-call | tf_op jit(solution)/shard_map/pallas_call | solution.py:72
  65.7 0.8 bitcast_dynamic-update-slice_fusion.7
  68.5 0.8 bitcast_dynamic-update-slice_fusion.3
  71.4 8.3 %all-to-all-start = ((f32[16,256,128]{2,1,0:T(8,128)}), f32[16,256,128]{2,1,0:T(8,128)S(1)}, u32[]{:S(2)}, u32[]{:S(2)}) async-start(f32[16,256,128]{2,1,0:T(8,128)} %bitcast_dynamic-update-slice_fusion), calls=%async_computation | async-start | bytes 4194304 | tf_op jit(solution)/shard_map/all_to_all | solution.py:251
  79.7 1.4 copy.10.refs_8_
  81.0 1.4 copy.11.refs_11_
  82.4 1.0 copy.9.refs_5_
  83.4 0.9 copy.8.refs_2_
  84.3 1.6 fusion.4
  85.9 1.0 fusion.15
  86.9 2.4 %fusion.1.refs_7_ = bf16[2048,1024]{1,0:T(8,128)(2,1)} fusion(s32[2048]{0:T(1024)S(1)} %bitcast.127), kind=kLoop, calls=%fused_computation.5 | loop fusion | flops 4194304 | bytes 4202496 | tf_op jit(solution)/shard_map/convert_element_type | solution.py:143
  89.3 2.4 %fusion.3.refs_10_ = bf16[2048,1024]{1,0:T(8,128)(2,1)} fusion(s32[2048]{0:T(1024)S(1)} %bitcast.126), kind=kLoop, calls=%fused_computation.7 | loop fusion | flops 4194304 | bytes 4202496 | tf_op jit(solution)/shard_map/convert_element_type | solution.py:143
  91.6 4.0 %fusion = (bf16[2048,1024]{1,0:T(8,128)(2,1)}, bf16[2048,1024]{1,0:T(8,128)(2,1)}) fusion(s32[2048]{0:T(1024)S(1)} %bitcast.129, s32[2048]{0:T(1024)S(1)} %bitcast.128), kind=kLoop, calls=%fused_computation.4 | loop fusion | flops 8388608 | bytes 8404992 | tf_op jit(solution)/shard_map/convert_element_type | solution.py:142
  95.7 13.6 %all-to-all-done = f32[16,256,128]{2,1,0:T(8,128)S(1)} async-done(((f32[16,256,128]{2,1,0:T(8,128)}), f32[16,256,128]{2,1,0:T(8,128)S(1)}, u32[]{:S(2)}, u32[]{:S(2)}) %all-to-all-start) | async-done | bytes 2097184 | tf_op jit(solution)/shard_map/all_to_all | solution.py:251
  109.3 1.3 copy-done.3
  110.6 43.1 %shard_map.69 = f32[2048,128]{1,0:T(8,128)} custom-call(f32[4096,128]{1,0:T(8,128)} %bitcast.86, bf16[512,256]{1,0:T(8,128)(2,1)} %get-tuple-element.67.refs_0_, bf16[512,256]{1,0:T(8,128)(2,1)} %get-tuple-element.68.refs_1_, s32[512,1]{1,0:T(8,128)} %copy.8.refs_2_, bf16[1024,512]{1,0:T(8,128)(2,1)} %get-tuple-element.65.refs_3_, ...), custom_call_target="tpu_custom_call" | custom-call | tf_op jit(solution)/shard_map/pallas_call | solution.py:148
  153.7 1.6 slice.320
  155.3 1.5 reshape.356
  156.8 6.7 %all-to-all-start.1 = ((f32[128,1,1024]{2,1,0:T(1,128)}), f32[128,1,1024]{2,1,0:T(1,128)S(1)}, u32[]{:S(2)}, u32[]{:S(2)}) async-start(f32[128,1,1024]{2,1,0:T(1,128)} %reshape.356), calls=%async_computation.1 | async-start | bytes 1048576 | tf_op jit(solution)/shard_map/all_to_all | solution.py:269
  163.6 13.4 %all-to-all-done.1 = f32[128,1,1024]{2,1,0:T(1,128)S(1)} async-done(((f32[128,1,1024]{2,1,0:T(1,128)}), f32[128,1,1024]{2,1,0:T(1,128)S(1)}, u32[]{:S(2)}, u32[]{:S(2)}) %all-to-all-start.1) | async-done | bytes 524320 | tf_op jit(solution)/shard_map/all_to_all | solution.py:269
  177.5 1.9 reduce
  180.5 1.1 convolution_bitcast_fusion
  181.8 1.0 fusion.6
  183.6 1.1 slice.279
  184.7 1.1 slice.280
  187.7 1.1 slice.286
  188.8 1.1 slice.287
  190.0 1.1 slice.288
  191.1 1.3 slice.289
  195.5 1.1 slice.297
  196.7 1.1 slice.298
  197.8 1.1 slice.299
  198.9 1.1 slice.300
  200.1 1.1 slice.301
  201.2 1.1 slice.302
  206.7 1.4 slice.312
  208.1 1.1 slice.313
  209.2 1.1 slice.314
  210.4 1.1 slice.315
  211.5 1.1 slice.316
  212.6 1.1 slice.317
  213.8 1.1 slice.318
  214.9 1.1 slice.319
  216.1 0.9 multiply_bitcast_fusion
  (62 shorter events, 22.4 us)
Async XLA Ops:
  0.6 8.6 %copy-start = (s32[12,2048]{1,0:T(8,128)S(1)}, s32[12,2048]{1,0:T(8,128)}, u32[]{:S(2)}) copy-start(s32[12,2048]{1,0:T(8,128)} %first_ref.1) | copy-start | bytes 294916
  0.6 8.6 %copy-start.1 = (s32[12,2048]{1,0:T(8,128)S(1)}, s32[12,2048]{1,0:T(8,128)}, u32[]{:S(2)}) copy-start(s32[12,2048]{1,0:T(8,128)} %second_ref.1) | copy-start | bytes 294916
  0.7 8.6 %copy-start.2 = (s32[12,2048]{1,0:T(8,128)S(1)}, s32[12,2048]{1,0:T(8,128)}, u32[]{:S(2)}) copy-start(s32[12,2048]{1,0:T(8,128)} %shift_ref.1) | copy-start | bytes 294916
  1.6 6.4 %collective-permute-start = (bf16[256,256]{1,0:T(8,128)(2,1)S(1)}, bf16[256,256]{1,0:T(8,128)(2,1)S(1)}, u32[]{:S(2)}, u32[]{:S(2)}) collective-permute-start(bf16[256,256]{1,0:T(8,128)(2,1)S(1)} %slice.240), channel_id=1, source_target_pairs={{0,1},{1,2},{2,3},{3,4},{4,5},{5,6},{6,7},{8,9},{9,10},{10,11},{11... | collective-permute-start | bytes 393224 | tf_op jit(solution)/shard_map/ppermute | solution.py:234
  71.4 37.9 %all-to-all-start = ((f32[16,256,128]{2,1,0:T(8,128)}), f32[16,256,128]{2,1,0:T(8,128)S(1)}, u32[]{:S(2)}, u32[]{:S(2)}) async-start(f32[16,256,128]{2,1,0:T(8,128)} %bitcast_dynamic-update-slice_fusion), calls=%async_computation | async-start | bytes 4194304 | tf_op jit(solution)/shard_map/all_to_all | solution.py:251
  109.3 1.3 copy-start.3
  156.8 20.2 %all-to-all-start.1 = ((f32[128,1,1024]{2,1,0:T(1,128)}), f32[128,1,1024]{2,1,0:T(1,128)S(1)}, u32[]{:S(2)}, u32[]{:S(2)}) async-start(f32[128,1,1024]{2,1,0:T(1,128)} %reshape.356), calls=%async_computation.1 | async-start | bytes 1048576 | tf_op jit(solution)/shard_map/all_to_all | solution.py:269
  183.5 33.4 %copy-start.4 = (f32[16,4096]{1,0:T(8,128)}, f32[16,4096]{1,0:T(8,128)S(1)}, u32[]{:S(2)}) copy-start(f32[16,4096]{1,0:T(8,128)S(1)} %reshape.353) | copy-start | bytes 786436

commit v4 on v2

--- a/solution.py
+++ b/solution.py
@@ -159,6 +159,19 @@
     )(state, *tables)
 
 
+def harmonic_kernel(power_ref, offset_ref, out_ref):
+    fundamentals = out_ref.shape[0]
+    total = None
+    for order in range(HARM):
+        stride = order + 1
+        offset = offset_ref[order]
+        for phase in range(stride):
+            picked = power_ref[pl.ds(phase, fundamentals, stride=stride), :]
+            term = jnp.where(offset == phase, picked, 0.0)
+            total = term if total is None else total + term
+    out_ref[...] = total * (1.0 / HARM)
+
+
 def spectra(series, harmonic_bins):
     count = series.shape[0]
     total = series.shape[1]
@@ -206,7 +219,18 @@
     final_im = section_two[1, :, :, :half_inner] - section_two[0, :, :, half_inner:]
     spectrum_power = (final_re * final_re + final_im * final_im) / (C * total)
     spectrum_power = jnp.transpose(spectrum_power, (0, 2, 1)).reshape(count, total // 2)
-    harmonic = jnp.sum(jnp.take(spectrum_power, harmonic_bins, axis=1), axis=1) / HARM
+    fundamentals = harmonic_bins.shape[1]
+    fundamental = jnp.arange(fundamentals, dtype=jnp.int32)
+    stride = jnp.arange(1, HARM + 1, dtype=jnp.int32)[:, None]
+    offsets = (harmonic_bins - stride * fundamental[None, :])[:, :, None]
+    vmem = pl.BlockSpec(memory_space=pltpu.VMEM)
+    harmonic_t = pl.pallas_call(
+        harmonic_kernel,
+        out_shape=jax.ShapeDtypeStruct((fundamentals, count), jnp.float32),
+        in_specs=[vmem, vmem],
+        out_specs=vmem,
+    )(jnp.transpose(spectrum_power), offsets)
+    harmonic = jnp.transpose(harmonic_t)
     return spectrum_power, harmonic
 
 
@@ -231,6 +255,9 @@
         second_rows[:local_levels, :channels],
         shifts[:local_levels, :channels],
         local_plan,
+    )
+    band, first_rows, second_rows, shifts = lax.optimization_barrier(
+        (band, first_rows, second_rows, shifts)
     )
     sub = samples // chan_count
     window = sub + SUB_HALO

time: 212 us -> 196 us (0.925)
  local copies, waits for them, and re-layouts: 48.1 us -> 39.1 us
  waiting for transfers between devices: 33.2 us -> 24.6 us
  Pallas kernels: 87.9 us -> 94.3 us
  starting transfers between devices: 22.2 us -> 19 us
    gather x1 -> x0, local copies, waits for them, and re-layouts: 14.2 us -> none  [spectra(): jnp.take(spectrum_power, harmonic_bins, axis=1)]
    pallas_call x0 -> x1, Pallas kernels: none -> 6.48 us  [spectra(): pl.pallas_call(harmonic_kernel, out_shape=jax.ShapeDtypeStruct((fundament...]
    all_to_all x1, waiting for transfers between devices: 19.6 us -> 13.5 us  [on_device(): lax.all_to_all(pieces, 'chan', split_axis=0, concat_axis=0, tiled=True)]
    convert_element_type x0 -> x2, other arithmetic: none -> 4.71 us  [run_matmul_levels(): (second_rows[level, :row_out, None] == columns).astype(jnp.bfloat16)]
    convert_element_type x4 -> x3, other arithmetic: 10.6 us -> 6.6 us  [run_matmul_levels(): (first_rows[level, :row_out, None] == columns).astype(jnp.bfloat16)]
    all_to_all x1, starting transfers between devices: 9.9 us -> 6.67 us  [on_device(): lax.all_to_all(outgoing, ('chan', 'tm'), split_axis=0, concat_axis=0, til...]
    transpose x1, local copies, waits for them, and re-layouts: 0.2 us -> 2.85 us  [spectra(): jnp.transpose(spectrum_power, (0, 2, 1)).reshape(count, total // 2)]
    all_to_all x1, waiting for transfers between devices: 13.5 us -> 11.1 us  [on_device(): lax.all_to_all(outgoing, ('chan', 'tm'), split_axis=0, concat_axis=0, til...]
  transfers between devices with their start and end apart: 3 -> 3, of which waited for: 2 -> 2; matrix products, arithmetic and copies ran while one was open for 12% -> 11% of each run, Pallas kernels for 0% -> 0%
where the time goes in v4:
time: 196 us; the launch traced here: 195 us
  Pallas kernels  94.3 us (48%)
  local copies, waits for them, and re-layouts  39.1 us (20%)
  waiting for transfers between devices  24.6 us (13%)
  starting transfers between devices  19 us (10%)
  other arithmetic  15.5 us (8%)
  matrix products  2.13 us (1%)
    pallas_call x1, Pallas kernels, run_levels(): pl.pallas_call(functools.partial(levels_kernel, plan), out_shape=jax.Shap...  44.7 us
    pallas_call x1, Pallas kernels, run_matmul_levels(): pl.pallas_call(functools.partial(matmul_kernel, plan), out_shape=jax.Shap...  43.2 us
    unnamed x25, local copies, waits for them, and re-layouts  16.7 us
    all_to_all x1, waiting for transfers between devices, on_device(): lax.all_to_all(pieces, 'chan', split_axis=0, concat_axis=0, tiled=True)  13.5 us
    all_to_all x1, waiting for transfers between devices, on_device(): lax.all_to_all(outgoing, ('chan', 'tm'), split_axis=0, concat_axis=0, til...  11.1 us
    all_to_all x1, starting transfers between devices, on_device(): lax.all_to_all(pieces, 'chan', split_axis=0, concat_axis=0, tiled=True)  7.78 us
    another operation x7, local copies, waits for them, and re-layouts, run_matmul_levels(): tables.append(shifts[level, :row_out, None])  7.09 us
    all_to_all x1, starting transfers between devices, on_device(): lax.all_to_all(outgoing, ('chan', 'tm'), split_axis=0, concat_axis=0, til...  6.67 us
  transfers between devices with their start and end apart: 3, of which 2 were waited for; matrix products, arithmetic and copies ran while one was open for 11% of the time, Pallas kernels for 0%

profile of v4, /device:TPU:1, one launch (start us, length us, event | category | flops | bytes accessed | tf_op | source)
XLA Modules:
  0.0 195.4 jit_solution(16545162811338572541)
XLA Ops:
  0.6 0.9 slice.120
  1.5 4.5 %collective-permute-start = (bf16[256,256]{1,0:T(8,128)(2,1)S(1)}, bf16[256,256]{1,0:T(8,128)(2,1)S(1)}, u32[]{:S(2)}, u32[]{:S(2)}) collective-permute-start(bf16[256,256]{1,0:T(8,128)(2,1)S(1)} %slice.120), channel_id=1, source_target_pairs={{0,1},{1,2},{2,3},{3,4},{4,5},{5,6},{6,7},{8,9},{9,10},{10,11},{11... | collective-permute-start | bytes 393224 | tf_op jit(solution)/shard_map/ppermute | solution.py:245
  6.1 0.7 slice.117.first_ref
  6.8 0.7 slice.118.second_ref
  7.5 0.7 slice.119.shift_ref
  8.2 1.1 maximum_convert_fusion.x_ref
  9.3 44.7 %shard_map.68 = f32[256,1280]{1,0:T(8,128)S(1)} custom-call(s32[8,256]{1,0:T(8,128)S(1)} %slice.117.first_ref, s32[8,256]{1,0:T(8,128)S(1)} %slice.118.second_ref, s32[8,256]{1,0:T(8,128)S(1)} %slice.119.shift_ref, f32[256,1280]{1,0:T(8,128)S(1)} %maximum_convert_fusion.x_ref), custom_call_target="tpu_custom_call" | custom-call | tf_op jit(solution)/shard_map/pallas_call | solution.py:72
  54.0 0.9 fusion.48
  54.9 0.8 slice.140
  55.7 0.7 slice.137
  56.4 0.8 slice.141
  57.2 0.7 slice.138
  57.9 1.0 slice_bitcast_fusion
  58.9 0.8 slice_bitcast_fusion.2
  59.6 0.7 slice_bitcast_fusion.3
  60.4 0.8 bitcast_dynamic-update-slice_fusion.15
  61.8 0.8 bitcast_dynamic-update-slice_fusion.13
  63.2 0.8 bitcast_dynamic-update-slice_fusion.11
  64.6 0.8 bitcast_dynamic-update-slice_fusion.9
  66.0 0.8 bitcast_dynamic-update-slice_fusion.7
  67.5 0.7 bitcast_dynamic-update-slice_fusion.5
  68.9 0.7 bitcast_dynamic-update-slice_fusion.3
  70.3 0.8 bitcast_dynamic-update-slice_fusion.1
  71.7 7.8 %all-to-all-start = ((f32[16,256,128]{2,1,0:T(8,128)}), f32[16,256,128]{2,1,0:T(8,128)S(1)}, u32[]{:S(2)}, u32[]{:S(2)}) async-start(f32[16,256,128]{2,1,0:T(8,128)} %bitcast_dynamic-update-slice_fusion), calls=%async_computation | async-start | bytes 4194304 | tf_op jit(solution)/shard_map/all_to_all | solution.py:268
  79.5 1.4 copy.13.refs_8_
  80.9 1.4 copy.14.refs_11_
  82.2 1.0 copy.12.refs_5_
  83.3 0.9 copy.11.refs_2_
  84.1 1.6 fusion.4
  85.8 1.0 fusion.15
  86.8 2.4 %fusion.1.refs_7_ = bf16[2048,1024]{1,0:T(8,128)(2,1)} fusion(s32[2048]{0:T(1024)S(1)} %bitcast.89), kind=kLoop, calls=%fused_computation.5 | loop fusion | flops 4194304 | bytes 4202496 | tf_op jit(solution)/shard_map/convert_element_type | solution.py:143
  89.2 2.3 %fusion.3.refs_10_ = bf16[2048,1024]{1,0:T(8,128)(2,1)} fusion(s32[2048]{0:T(1024)S(1)} %bitcast.88), kind=kLoop, calls=%fused_computation.7 | loop fusion | flops 4194304 | bytes 4202496 | tf_op jit(solution)/shard_map/convert_element_type | solution.py:143
  91.5 4.0 %fusion = (bf16[2048,1024]{1,0:T(8,128)(2,1)}, bf16[2048,1024]{1,0:T(8,128)(2,1)}) fusion(s32[2048]{0:T(1024)S(1)} %bitcast.91, s32[2048]{0:T(1024)S(1)} %bitcast.90), kind=kLoop, calls=%fused_computation.4 | loop fusion | flops 8388608 | bytes 8404992 | tf_op jit(solution)/shard_map/convert_element_type | solution.py:142
  95.5 13.5 %all-to-all-done = f32[16,256,128]{2,1,0:T(8,128)S(1)} async-done(((f32[16,256,128]{2,1,0:T(8,128)}), f32[16,256,128]{2,1,0:T(8,128)S(1)}, u32[]{:S(2)}, u32[]{:S(2)}) %all-to-all-start) | async-done | bytes 2097184 | tf_op jit(solution)/shard_map/all_to_all | solution.py:268
  109.0 1.3 copy-done.1
  110.3 43.2 %shard_map.69 = f32[2048,128]{1,0:T(8,128)} custom-call(f32[4096,128]{1,0:T(8,128)} %bitcast.83, bf16[512,256]{1,0:T(8,128)(2,1)} %get-tuple-element.28.refs_0_, bf16[512,256]{1,0:T(8,128)(2,1)} %get-tuple-element.29.refs_1_, s32[512,1]{1,0:T(8,128)} %copy.11.refs_2_, bf16[1024,512]{1,0:T(8,128)(2,1)} %get-tuple-element.26.refs_3_, ...), custom_call_target="tpu_custom_call" | custom-call | tf_op jit(solution)/shard_map/pallas_call | solution.py:148
  153.5 1.6 slice.156
  155.1 1.5 reshape.77
  156.5 6.7 %all-to-all-start.1 = ((f32[128,1,1024]{2,1,0:T(1,128)}), f32[128,1,1024]{2,1,0:T(1,128)S(1)}, u32[]{:S(2)}, u32[]{:S(2)}) async-start(f32[128,1,1024]{2,1,0:T(1,128)} %reshape.77), calls=%async_computation.1 | async-start | bytes 1048576 | tf_op jit(solution)/shard_map/all_to_all | solution.py:286
  163.3 2.0 %copy.17.offset_ref = s32[8,512,1]{2,1,0:T(8,128)} copy(s32[8,512,1]{1,0,2:T(8,128)S(1)} %subtract_bitcast_fusion.1) | data formatting | bytes 32768 | tf_op jit(solution)/shard_map/broadcast_in_dim | solution.py:225
  165.9 11.1 %all-to-all-done.1 = f32[128,1,1024]{2,1,0:T(1,128)S(1)} async-done(((f32[128,1,1024]{2,1,0:T(1,128)}), f32[128,1,1024]{2,1,0:T(1,128)S(1)}, u32[]{:S(2)}, u32[]{:S(2)}) %all-to-all-start.1) | async-done | bytes 524320 | tf_op jit(solution)/shard_map/all_to_all | solution.py:286
  177.4 1.9 reduce
  180.4 1.1 convolution_bitcast_fusion
  181.7 1.0 fusion.6
  183.1 2.8 %copy.16 = f32[16,64,64]{0,2,1:T(8,128)} copy(f32[16,64,64]{1,2,0:T(8,128)S(1)} %fusion.13) | data formatting | bytes 524288 | tf_op jit(solution)/shard_map/transpose | solution.py:221
  185.9 6.5 %shard_map.70 = f32[512,16]{1,0:T(8,128)} custom-call(f32[4096,16]{1,0:T(8,128)} %bitcast.81, s32[8,512,1]{2,1,0:T(8,128)} %copy.17.offset_ref), custom_call_target="tpu_custom_call" | custom-call | tf_op jit(solution)/shard_map/pallas_call | solution.py:227
  192.4 1.7 copy.19
  194.1 1.3 copy.18
  (25 shorter events, 8.1 us)
Async XLA Ops:
  1.5 6.6 %collective-permute-start = (bf16[256,256]{1,0:T(8,128)(2,1)S(1)}, bf16[256,256]{1,0:T(8,128)(2,1)S(1)}, u32[]{:S(2)}, u32[]{:S(2)}) collective-permute-start(bf16[256,256]{1,0:T(8,128)(2,1)S(1)} %slice.120), channel_id=1, source_target_pairs={{0,1},{1,2},{2,3},{3,4},{4,5},{5,6},{6,7},{8,9},{9,10},{10,11},{11... | collective-permute-start | bytes 393224 | tf_op jit(solution)/shard_map/ppermute | solution.py:245
  71.7 37.3 %all-to-all-start = ((f32[16,256,128]{2,1,0:T(8,128)}), f32[16,256,128]{2,1,0:T(8,128)S(1)}, u32[]{:S(2)}, u32[]{:S(2)}) async-start(f32[16,256,128]{2,1,0:T(8,128)} %bitcast_dynamic-update-slice_fusion), calls=%async_computation | async-start | bytes 4194304 | tf_op jit(solution)/shard_map/all_to_all | solution.py:268
  109.0 1.3 copy-start.1
  153.5 9.7 %copy-start.2 = (s32[8,512]{1,0:T(8,128)S(1)}, s32[8,512]{1,0:T(8,128)}, u32[]{:S(2)}) copy-start(s32[8,512]{1,0:T(8,128)} %param.9) | copy-start | bytes 49156
  156.5 20.4 %all-to-all-start.1 = ((f32[128,1,1024]{2,1,0:T(1,128)}), f32[128,1,1024]{2,1,0:T(1,128)S(1)}, u32[]{:S(2)}, u32[]{:S(2)}) async-start(f32[128,1,1024]{2,1,0:T(1,128)} %reshape.77), calls=%async_computation.1 | async-start | bytes 1048576 | tf_op jit(solution)/shard_map/all_to_all | solution.py:286
  185.9 8.2 %copy-start = (f32[16,64,64]{0,2,1:T(8,128)S(1)}, f32[16,64,64]{0,2,1:T(8,128)}, u32[]{:S(2)}) copy-start(f32[16,64,64]{0,2,1:T(8,128)} %copy.16) | copy-start | bytes 786436

commit v5 on v4

--- a/solution.py
+++ b/solution.py
@@ -16,6 +16,7 @@
 RAW_HALO = 256
 SUB_HALO = 64
 TILE = 256
+LANES = 128
 
 
 def shift_right(value, amount):
@@ -39,44 +40,6 @@
     return merge_level(
         layers, first_rows[level, :count], second_rows[level, :count], shifts[level, :count]
     )
-
-
-def levels_kernel(plan, first_ref, second_ref, shift_ref, x_ref, out_ref, buf_a, buf_b):
-    source = x_ref
-    for step, (row_in, row_out, rows_total) in enumerate(plan):
-        target = out_ref if step == len(plan) - 1 else (buf_a, buf_b)[step % 2]
-        log_out = row_out.bit_length() - 1
-
-        def body(out_row, carry, source=source, target=target, step=step,
-                 row_in=row_in, row_out=row_out, log_out=log_out):
-            band = lax.shift_right_logical(out_row, log_out)
-            row = lax.bitwise_and(out_row, row_out - 1)
-            low = 2 * band * row_in + first_ref[step, row]
-            high = (2 * band + 1) * row_in + second_ref[step, row]
-            amount = shift_ref[step, row]
-            lower = source[pl.ds(low, 1), :]
-            upper = source[pl.ds(high, 1), :]
-            target[pl.ds(out_row, 1), :] = lower + pltpu.roll(upper, amount, 1)
-            return carry
-
-        lax.fori_loop(0, rows_total, body, 0, unroll=8)
-        source = target
-
-
-def run_levels(state, first_rows, second_rows, shifts, plan):
-    rows, width = state.shape
-    out_rows = plan[-1][2]
-    buf_rows = max(p[2] for p in plan)
-    smem = pl.BlockSpec(memory_space=pltpu.SMEM)
-    vmem = pl.BlockSpec(memory_space=pltpu.VMEM)
-    return pl.pallas_call(
-        functools.partial(levels_kernel, plan),
-        out_shape=jax.ShapeDtypeStruct((out_rows, width), jnp.float32),
-        in_specs=[smem, smem, smem, vmem],
-        out_specs=vmem,
-        scratch_shapes=[pltpu.VMEM((buf_rows, width), jnp.float32)] * 2,
-        compiler_params=pltpu.CompilerParams(vmem_limit_bytes=48 * 1024 * 1024),
-    )(first_rows, second_rows, shifts, state)
 
 
 def split_three(block):
@@ -172,6 +135,62 @@
     out_ref[...] = total * (1.0 / HARM)
 
 
+def delayed(value, amount):
+    rolled = pltpu.roll(value, amount, 2)
+    previous = jnp.concatenate([rolled[-1:], rolled[:-1]], axis=0)
+    lane = lax.broadcasted_iota(jnp.int32, value.shape, 2)
+    return jnp.where(lane < amount, previous, rolled)
+
+
+def local_kernel(plan, sub, base, first_ref, second_ref, shift_ref, x_ref, out_ref, *bufs):
+    count = len(plan)
+    final = bufs[-1]
+    source = x_ref
+    for step, (row_in, row_out, bands_out) in enumerate(plan):
+        target = final if step == count - 1 else bufs[step]
+
+        def body(row, carry, source=source, target=target, step=step,
+                 bands_out=bands_out, last=step == count - 1):
+            lower = source[first_ref[step, row], :, pl.ds(0, bands_out, stride=2), :]
+            upper = source[second_ref[step, row], :, pl.ds(1, bands_out, stride=2), :]
+            merged = lower + delayed(upper, shift_ref[step, row])
+            if last:
+                target[:, pl.ds(row, 1), :] = merged
+            else:
+                target[row] = merged
+            return carry
+
+        lax.fori_loop(0, row_out, body, 0, unroll=min(row_out, 8))
+        source = target
+    for dest in range(out_ref.shape[0]):
+        start = base + sub * dest
+        slab, offset = start // LANES, start % LANES
+        if offset == 0:
+            out_ref[dest] = final[slab]
+        else:
+            lane = lax.broadcasted_iota(jnp.int32, final.shape[1:], 1)
+            head = pltpu.roll(final[slab], LANES - offset, 1)
+            tail = pltpu.roll(final[slab + 1], LANES - offset, 1)
+            out_ref[dest] = jnp.where(lane < LANES - offset, head, tail)
+
+
+def run_local(state, first_rows, second_rows, shifts, plan, parts, sub, base):
+    slabs = state.shape[1]
+    rows_last = plan[-1][1]
+    smem = pl.BlockSpec(memory_space=pltpu.SMEM)
+    vmem = pl.BlockSpec(memory_space=pltpu.VMEM)
+    scratch = [pltpu.VMEM((p[1], slabs, p[2], LANES), jnp.float32) for p in plan[:-1]]
+    scratch.append(pltpu.VMEM((slabs, rows_last, LANES), jnp.float32))
+    return pl.pallas_call(
+        functools.partial(local_kernel, plan, sub, base),
+        out_shape=jax.ShapeDtypeStruct((parts, rows_last, sub + SUB_HALO), jnp.float32),
+        in_specs=[smem, smem, smem, vmem],
+        out_specs=vmem,
+        scratch_shapes=scratch,
+        compiler_params=pltpu.CompilerParams(vmem_limit_bytes=56 * 1024 * 1024),
+    )(first_rows, second_rows, shifts, state)
+
+
 def spectra(series, harmonic_bins):
     count = series.shape[0]
     total = series.shape[1]
@@ -248,23 +267,24 @@
         [(source, source + 1) for source in range(tm_count - 1)],
     )
     widened = jnp.concatenate([rim, filterbank], axis=1)
-    local_plan = [(2**level, 2 ** (level + 1), channels) for level in range(local_levels)]
-    band = run_levels(
-        widened.astype(jnp.float32),
+    local_plan = [
+        (2**level, 2 ** (level + 1), channels >> (level + 1)) for level in range(local_levels)
+    ]
+    sub = samples // chan_count
+    pieces = run_local(
+        widened.astype(jnp.float32).reshape(channels, -1, LANES).transpose(1, 0, 2)[None],
         first_rows[:local_levels, :channels],
         second_rows[:local_levels, :channels],
         shifts[:local_levels, :channels],
         local_plan,
-    )
-    band, first_rows, second_rows, shifts = lax.optimization_barrier(
-        (band, first_rows, second_rows, shifts)
-    )
-    sub = samples // chan_count
+        chan_count,
+        sub,
+        RAW_HALO - SUB_HALO,
+    )
+    pieces, first_rows, second_rows, shifts = lax.optimization_barrier(
+        (pieces, first_rows, second_rows, shifts)
+    )
     window = sub + SUB_HALO
-    base = RAW_HALO - SUB_HALO
-    pieces = jnp.stack(
-        [band[:, base + sub * dest : base + sub * dest + window] for dest in range(chan_count)]
-    )
     layers = lax.all_to_all(pieces, "chan", split_axis=0, concat_axis=0, tiled=True)
     cross_plan = []
     bands = chan_count

time: 196 us -> 159 us (0.81)
  Pallas kernels: 94.3 us -> 63.6 us
  local copies, waits for them, and re-layouts: 39.1 us -> 30.3 us
  starting transfers between devices: 19 us -> 21.7 us
    pallas_call x1, Pallas kernels: 44.7 us -> 14.1 us  [run_local(): pl.pallas_call(functools.partial(local_kernel, plan, sub, base), out_shap...]
    unnamed x25 -> x11, local copies, waits for them, and re-layouts: 16.7 us -> 7.37 us
    all_to_all x1, starting transfers between devices: 6.67 us -> 9.41 us  [on_device(): lax.all_to_all(outgoing, ('chan', 'tm'), split_axis=0, concat_axis=0, til...]
  transfers between devices with their start and end apart: 3 -> 3, of which waited for: 2 -> 2; matrix products, arithmetic and copies ran while one was open for 11% -> 14% of each run, Pallas kernels for 0% -> 0%
where the time goes in v5:
time: 159 us; the launch traced here: 158 us
  Pallas kernels  63.6 us (40%)
  local copies, waits for them, and re-layouts  30.3 us (19%)
  waiting for transfers between devices  24.6 us (15%)
  starting transfers between devices  21.7 us (14%)
  other arithmetic  14.4 us (9%)
  matrix products  2.13 us (1%)
    pallas_call x1, Pallas kernels, run_matmul_levels(): pl.pallas_call(functools.partial(matmul_kernel, plan), out_shape=jax.Shap...  43.2 us
    pallas_call x1, Pallas kernels, run_local(): pl.pallas_call(functools.partial(local_kernel, plan, sub, base), out_shap...  14.1 us
    all_to_all x1, waiting for transfers between devices, on_device(): lax.all_to_all(pieces, 'chan', split_axis=0, concat_axis=0, tiled=True)  13.5 us
    all_to_all x1, waiting for transfers between devices, on_device(): lax.all_to_all(outgoing, ('chan', 'tm'), split_axis=0, concat_axis=0, til...  11.1 us
    all_to_all x1, starting transfers between devices, on_device(): lax.all_to_all(outgoing, ('chan', 'tm'), split_axis=0, concat_axis=0, til...  9.41 us
    all_to_all x1, starting transfers between devices, on_device(): lax.all_to_all(pieces, 'chan', split_axis=0, concat_axis=0, tiled=True)  7.79 us
    unnamed x11, local copies, waits for them, and re-layouts  7.37 us
    another operation x7, local copies, waits for them, and re-layouts, run_matmul_levels(): tables.append(shifts[level, :row_out, None])  7.09 us
  transfers between devices with their start and end apart: 3, of which 2 were waited for; matrix products, arithmetic and copies ran while one was open for 14% of the time, Pallas kernels for 0%

profile of v5, /device:TPU:1, one launch (start us, length us, event | category | flops | bytes accessed | tf_op | source)
XLA Modules:
  0.0 157.6 jit_solution(15262193491523401788)
XLA Ops:
  0.6 1.2 copy.11
  1.9 4.5 %collective-permute-start = (bf16[256,256]{0,1:T(8,128)(2,1)S(1)}, bf16[256,256]{0,1:T(8,128)(2,1)S(1)}, u32[]{:S(2)}, u32[]{:S(2)}) collective-permute-start(bf16[256,256]{0,1:T(8,128)(2,1)S(1)} %slice.92), channel_id=1, source_target_pairs={{0,1},{1,2},{2,3},{3,4},{4,5},{5,6},{6,7},{8,9},{9,10},{10,11},{11... | collective-permute-start | bytes 393224 | tf_op jit(solution)/shard_map/ppermute | solution.py:264
  6.4 1.3 slice.69.first_ref
  7.7 1.3 slice.70.second_ref
  9.0 1.3 slice.71.shift_ref
  10.4 1.3 copy.13
  11.7 14.1 %shard_map.68 = f32[16,256,128]{2,1,0:T(8,128)} custom-call(s32[8,256]{1,0:T(8,128)} %slice.69.first_ref, s32[8,256]{1,0:T(8,128)} %slice.70.second_ref, s32[8,256]{1,0:T(8,128)} %slice.71.shift_ref, f32[1,10,256,128]{3,2,1,0:T(8,128)} %bitcast.57), custom_call_target="tpu_custom_call" | custom-call | tf_op jit(solution)/shard_map/pallas_call | solution.py:184
  25.8 0.7 slice.73
  26.5 0.8 slice.76
  27.3 0.7 slice.74
  28.0 0.8 slice.77
  28.8 0.7 slice_bitcast_fusion.3
  29.5 0.8 slice_bitcast_fusion.2
  30.3 0.9 fusion.48
  31.2 1.0 slice_bitcast_fusion
  32.2 7.8 %all-to-all-start = ((f32[16,256,128]{2,1,0:T(8,128)}), f32[16,256,128]{2,1,0:T(8,128)S(1)}, u32[]{:S(2)}, u32[]{:S(2)}) async-start(f32[16,256,128]{2,1,0:T(8,128)} %shard_map.68), calls=%async_computation | async-start | bytes 4194304 | tf_op jit(solution)/shard_map/all_to_all | solution.py:288
  40.0 0.9 copy.14.refs_2_
  40.8 1.0 copy.15.refs_5_
  41.9 1.4 copy.16.refs_8_
  43.2 1.4 copy.17.refs_11_
  44.6 1.6 %fusion.4 = (bf16[1024,512]{1,0:T(8,128)(2,1)}, bf16[1024,512]{1,0:T(8,128)(2,1)}) fusion(s32[1024]{0:T(1024)S(1)} %bitcast.67, s32[1024]{0:T(1024)S(1)} %bitcast.68), kind=kLoop, calls=%fused_computation.10 | loop fusion | flops 2097152 | bytes 2105344 | tf_op jit(solution)/shard_map/convert_element_type | solution.py:105
  46.2 1.0 fusion.15
  47.2 2.4 %fusion.1.refs_7_ = bf16[2048,1024]{1,0:T(8,128)(2,1)} fusion(s32[2048]{0:T(1024)S(1)} %bitcast.64), kind=kLoop, calls=%fused_computation.5 | loop fusion | flops 4194304 | bytes 4202496 | tf_op jit(solution)/shard_map/convert_element_type | solution.py:106
  49.6 2.3 %fusion.3.refs_10_ = bf16[2048,1024]{1,0:T(8,128)(2,1)} fusion(s32[2048]{0:T(1024)S(1)} %bitcast.63), kind=kLoop, calls=%fused_computation.7 | loop fusion | flops 4194304 | bytes 4202496 | tf_op jit(solution)/shard_map/convert_element_type | solution.py:106
  51.9 4.0 %fusion = (bf16[2048,1024]{1,0:T(8,128)(2,1)}, bf16[2048,1024]{1,0:T(8,128)(2,1)}) fusion(s32[2048]{0:T(1024)S(1)} %bitcast.66, s32[2048]{0:T(1024)S(1)} %bitcast.65), kind=kLoop, calls=%fused_computation.4 | loop fusion | flops 8388608 | bytes 8404992 | tf_op jit(solution)/shard_map/convert_element_type | solution.py:105
  55.9 13.5 %all-to-all-done = f32[16,256,128]{2,1,0:T(8,128)S(1)} async-done(((f32[16,256,128]{2,1,0:T(8,128)}), f32[16,256,128]{2,1,0:T(8,128)S(1)}, u32[]{:S(2)}, u32[]{:S(2)}) %all-to-all-start) | async-done | bytes 2097184 | tf_op jit(solution)/shard_map/all_to_all | solution.py:288
  69.5 1.3 copy-done.1
  70.8 43.2 %shard_map.69 = f32[2048,128]{1,0:T(8,128)} custom-call(f32[4096,128]{1,0:T(8,128)} %bitcast.56, bf16[512,256]{1,0:T(8,128)(2,1)} %get-tuple-element.28.refs_0_, bf16[512,256]{1,0:T(8,128)(2,1)} %get-tuple-element.29.refs_1_, s32[512,1]{1,0:T(8,128)} %copy.14.refs_2_, bf16[1024,512]{1,0:T(8,128)(2,1)} %get-tuple-element.26.refs_3_, ...), custom_call_target="tpu_custom_call" | custom-call | tf_op jit(solution)/shard_map/pallas_call | solution.py:111
  114.0 1.6 slice.93
  115.5 1.5 reshape.83
  117.0 9.4 %all-to-all-start.1 = ((f32[128,1,1024]{2,1,0:T(1,128)}), f32[128,1,1024]{2,1,0:T(1,128)S(1)}, u32[]{:S(2)}, u32[]{:S(2)}) async-start(f32[128,1,1024]{2,1,0:T(1,128)} %reshape.83), calls=%async_computation.1 | async-start | bytes 1048576 | tf_op jit(solution)/shard_map/all_to_all | solution.py:306
  126.5 2.0 %copy.20.offset_ref = s32[8,512,1]{2,1,0:T(8,128)} copy(s32[8,512,1]{1,0,2:T(8,128)S(1)} %subtract_bitcast_fusion.1) | data formatting | bytes 32768 | tf_op jit(solution)/shard_map/broadcast_in_dim | solution.py:244
  128.6 0.1 fusion.41
  128.8 0.3 fusion.33
  129.1 11.1 %all-to-all-done.1 = f32[128,1,1024]{2,1,0:T(1,128)S(1)} async-done(((f32[128,1,1024]{2,1,0:T(1,128)}), f32[128,1,1024]{2,1,0:T(1,128)S(1)}, u32[]{:S(2)}, u32[]{:S(2)}) %all-to-all-start.1) | async-done | bytes 524320 | tf_op jit(solution)/shard_map/all_to_all | solution.py:306
  140.1 0.5 broadcast.98
  140.6 1.9 %reduce = f32[128,1024]{1,0:T(8,128)S(1)} reduce(f32[128,1,1024]{2,1,0:T(1,128)S(1)} %all-to-all-done.1, f32[]{:T(128)} %broadcast.98), dimensions={1}, to_apply=%all_to_all.7.reduce_sub_computation | reduce | bytes 1048580 | tf_op jit(solution)/shard_map/all_to_all | solution.py:306
  142.5 0.3 reshape.84
  142.8 0.6 copy.25
  143.4 0.2 reshape_reshape.3
  143.6 1.1 convolution_bitcast_fusion
  144.7 0.2 add_bitcast_fusion
  144.9 1.0 fusion.6
  145.9 0.3 fusion.13
  146.3 1.9 %copy.19 = f32[16,64,64]{0,2,1:T(8,128)S(1)} copy(f32[16,64,64]{1,2,0:T(8,128)S(1)} %fusion.13) | data formatting | bytes 524288 | tf_op jit(solution)/shard_map/transpose | solution.py:240
  148.2 1.4 copy.21
  149.6 6.3 %shard_map.70 = f32[512,16]{1,0:T(8,128)} custom-call(f32[4096,16]{1,0:T(8,128)} %bitcast.55, s32[8,512,1]{2,1,0:T(8,128)} %copy.20.offset_ref), custom_call_target="tpu_custom_call" | custom-call | tf_op jit(solution)/shard_map/pallas_call | solution.py:246
  155.9 1.7 %copy.22 = f32[16,512]{1,0:T(8,128)} copy(f32[16,512]{0,1:T(8,128)} %bitcast.62) | data formatting | bytes 65536
  (11 shorter events, 0.3 us)
Async XLA Ops:
  1.9 8.4 %collective-permute-start = (bf16[256,256]{0,1:T(8,128)(2,1)S(1)}, bf16[256,256]{0,1:T(8,128)(2,1)S(1)}, u32[]{:S(2)}, u32[]{:S(2)}) collective-permute-start(bf16[256,256]{0,1:T(8,128)(2,1)S(1)} %slice.92), channel_id=1, source_target_pairs={{0,1},{1,2},{2,3},{3,4},{4,5},{5,6},{6,7},{8,9},{9,10},{10,11},{11... | collective-permute-start | bytes 393224 | tf_op jit(solution)/shard_map/ppermute | solution.py:264
  32.2 37.3 %all-to-all-start = ((f32[16,256,128]{2,1,0:T(8,128)}), f32[16,256,128]{2,1,0:T(8,128)S(1)}, u32[]{:S(2)}, u32[]{:S(2)}) async-start(f32[16,256,128]{2,1,0:T(8,128)} %shard_map.68), calls=%async_computation | async-start | bytes 4194304 | tf_op jit(solution)/shard_map/all_to_all | solution.py:288
  69.5 1.3 copy-start.1
  114.0 12.4 %copy-start.2 = (s32[8,512]{1,0:T(8,128)S(1)}, s32[8,512]{1,0:T(8,128)}, u32[]{:S(2)}) copy-start(s32[8,512]{1,0:T(8,128)} %param.9) | copy-start | bytes 49156
  117.0 23.1 %all-to-all-start.1 = ((f32[128,1,1024]{2,1,0:T(1,128)}), f32[128,1,1024]{2,1,0:T(1,128)S(1)}, u32[]{:S(2)}, u32[]{:S(2)}) async-start(f32[128,1,1024]{2,1,0:T(1,128)} %reshape.83), calls=%async_computation.1 | async-start | bytes 1048576 | tf_op jit(solution)/shard_map/all_to_all | solution.py:306
  148.2 1.4 copy-start

commit v6 on v5

--- a/solution.py
+++ b/solution.py
@@ -17,6 +17,7 @@
 SUB_HALO = 64
 TILE = 256
 LANES = 128
+PIECES = 2
 
 
 def shift_right(value, amount):
@@ -42,12 +43,10 @@
     )
 
 
-def split_three(block):
+def split_pieces(block):
     high = block.astype(jnp.bfloat16)
-    rest = block - high.astype(jnp.float32)
-    middle = rest.astype(jnp.bfloat16)
-    low = (rest - middle.astype(jnp.float32)).astype(jnp.bfloat16)
-    return high, middle, low
+    low = (block - high.astype(jnp.float32)).astype(jnp.bfloat16)
+    return high, low
 
 
 def matmul_kernel(plan, x_ref, *refs):
@@ -66,7 +65,7 @@
                 band = first_band + member
                 for side in range(2):
                     block = source[pl.ds((2 * band + side) * row_in, depth), :]
-                    for piece, value in enumerate(split_three(block)):
+                    for piece, value in enumerate(split_pieces(block)):
                         parts[side, piece, pl.ds(0, depth), pl.ds(member * width, width)] = value
 
             def tile(index, carry, target=target, first_band=first_band, depth=depth,
@@ -77,7 +76,7 @@
                 high_sel = pick_high[rows, :]
                 lower = None
                 upper = None
-                for piece in range(3):
+                for piece in range(PIECES):
                     term = jnp.dot(low_sel, parts[0, piece, pl.ds(0, depth), pl.ds(0, lanes)],
                                    preferred_element_type=jnp.float32)
                     lower = term if lower is None else lower + term
@@ -116,7 +115,7 @@
         scratch_shapes=[
             pltpu.VMEM((buf_rows, width), jnp.float32),
             pltpu.VMEM((buf_rows, width), jnp.float32),
-            pltpu.VMEM((2, 3, depth_most, 2 * width), jnp.bfloat16),
+            pltpu.VMEM((2, PIECES, depth_most, 2 * width), jnp.bfloat16),
         ],
         compiler_params=pltpu.CompilerParams(vmem_limit_bytes=60 * 1024 * 1024),
     )(state, *tables)

time: 159 us -> 152 us (0.956)
  Pallas kernels: 63.6 us -> 56.8 us
    pallas_call x1, Pallas kernels: 43.2 us -> 36.3 us  [run_matmul_levels(): pl.pallas_call(functools.partial(matmul_kernel, plan), out_shape=jax.Shap...]
  transfers between devices with their start and end apart: 3 -> 3, of which waited for: 2 -> 2; matrix products, arithmetic and copies ran while one was open for 14% -> 15% of each run, Pallas kernels for 0% -> 0%
where the time goes in v6:
time: 152 us; the launch traced here: 151 us
  Pallas kernels  56.8 us (37%)
  local copies, waits for them, and re-layouts  30.3 us (20%)
  waiting for transfers between devices  24.6 us (16%)
  starting transfers between devices  21.7 us (14%)
  other arithmetic  14.4 us (9%)
  matrix products  2.13 us (1%)
    pallas_call x1, Pallas kernels, run_matmul_levels(): pl.pallas_call(functools.partial(matmul_kernel, plan), out_shape=jax.Shap...  36.3 us
    pallas_call x1, Pallas kernels, run_local(): pl.pallas_call(functools.partial(local_kernel, plan, sub, base), out_shap...  14.1 us
    all_to_all x1, waiting for transfers between devices, on_device(): lax.all_to_all(pieces, 'chan', split_axis=0, concat_axis=0, tiled=True)  13.5 us
    all_to_all x1, waiting for transfers between devices, on_device(): lax.all_to_all(outgoing, ('chan', 'tm'), split_axis=0, concat_axis=0, til...  11.1 us
    all_to_all x1, starting transfers between devices, on_device(): lax.all_to_all(outgoing, ('chan', 'tm'), split_axis=0, concat_axis=0, til...  9.42 us
    all_to_all x1, starting transfers between devices, on_device(): lax.all_to_all(pieces, 'chan', split_axis=0, concat_axis=0, tiled=True)  7.79 us
    unnamed x11, local copies, waits for them, and re-layouts  7.37 us
    another operation x7, local copies, waits for them, and re-layouts, run_matmul_levels(): tables.append(shifts[level, :row_out, None])  7.09 us
  transfers between devices with their start and end apart: 3, of which 2 were waited for; matrix products, arithmetic and copies ran while one was open for 15% of the time, Pallas kernels for 0%

profile of v6, /device:TPU:1, one launch (start us, length us, event | category | flops | bytes accessed | tf_op | source)
XLA Modules:
  0.0 150.7 jit_solution(5470061806453706811)
XLA Ops:
  0.6 1.2 copy.11
  1.9 4.5 %collective-permute-start = (bf16[256,256]{0,1:T(8,128)(2,1)S(1)}, bf16[256,256]{0,1:T(8,128)(2,1)S(1)}, u32[]{:S(2)}, u32[]{:S(2)}) collective-permute-start(bf16[256,256]{0,1:T(8,128)(2,1)S(1)} %slice.92), channel_id=1, source_target_pairs={{0,1},{1,2},{2,3},{3,4},{4,5},{5,6},{6,7},{8,9},{9,10},{10,11},{11... | collective-permute-start | bytes 393224 | tf_op jit(solution)/shard_map/ppermute | solution.py:263
  6.4 1.3 slice.69.first_ref
  7.7 1.3 slice.70.second_ref
  9.0 1.3 slice.71.shift_ref
  10.4 1.3 copy.13
  11.7 14.1 %shard_map.68 = f32[16,256,128]{2,1,0:T(8,128)} custom-call(s32[8,256]{1,0:T(8,128)} %slice.69.first_ref, s32[8,256]{1,0:T(8,128)} %slice.70.second_ref, s32[8,256]{1,0:T(8,128)} %slice.71.shift_ref, f32[1,10,256,128]{3,2,1,0:T(8,128)} %bitcast.57), custom_call_target="tpu_custom_call" | custom-call | tf_op jit(solution)/shard_map/pallas_call | solution.py:183
  25.8 0.7 slice.73
  26.5 0.8 slice.76
  27.3 0.7 slice.74
  28.0 0.8 slice.77
  28.8 0.7 slice_bitcast_fusion.3
  29.5 0.8 slice_bitcast_fusion.2
  30.3 0.9 fusion.48
  31.2 1.0 slice_bitcast_fusion
  32.2 7.8 %all-to-all-start = ((f32[16,256,128]{2,1,0:T(8,128)}), f32[16,256,128]{2,1,0:T(8,128)S(1)}, u32[]{:S(2)}, u32[]{:S(2)}) async-start(f32[16,256,128]{2,1,0:T(8,128)} %shard_map.68), calls=%async_computation | async-start | bytes 4194304 | tf_op jit(solution)/shard_map/all_to_all | solution.py:287
  40.0 0.9 copy.14.refs_2_
  40.8 1.0 copy.15.refs_5_
  41.9 1.4 copy.16.refs_8_
  43.2 1.4 copy.17.refs_11_
  44.6 1.6 %fusion.4 = (bf16[1024,512]{1,0:T(8,128)(2,1)}, bf16[1024,512]{1,0:T(8,128)(2,1)}) fusion(s32[1024]{0:T(1024)S(1)} %bitcast.67, s32[1024]{0:T(1024)S(1)} %bitcast.68), kind=kLoop, calls=%fused_computation.10 | loop fusion | flops 2097152 | bytes 2105344 | tf_op jit(solution)/shard_map/convert_element_type | solution.py:104
  46.2 1.0 fusion.15
  47.2 2.4 %fusion.1.refs_7_ = bf16[2048,1024]{1,0:T(8,128)(2,1)} fusion(s32[2048]{0:T(1024)S(1)} %bitcast.64), kind=kLoop, calls=%fused_computation.5 | loop fusion | flops 4194304 | bytes 4202496 | tf_op jit(solution)/shard_map/convert_element_type | solution.py:105
  49.6 2.3 %fusion.3.refs_10_ = bf16[2048,1024]{1,0:T(8,128)(2,1)} fusion(s32[2048]{0:T(1024)S(1)} %bitcast.63), kind=kLoop, calls=%fused_computation.7 | loop fusion | flops 4194304 | bytes 4202496 | tf_op jit(solution)/shard_map/convert_element_type | solution.py:105
  52.0 4.0 %fusion = (bf16[2048,1024]{1,0:T(8,128)(2,1)}, bf16[2048,1024]{1,0:T(8,128)(2,1)}) fusion(s32[2048]{0:T(1024)S(1)} %bitcast.66, s32[2048]{0:T(1024)S(1)} %bitcast.65), kind=kLoop, calls=%fused_computation.4 | loop fusion | flops 8388608 | bytes 8404992 | tf_op jit(solution)/shard_map/convert_element_type | solution.py:104
  55.9 13.5 %all-to-all-done = f32[16,256,128]{2,1,0:T(8,128)S(1)} async-done(((f32[16,256,128]{2,1,0:T(8,128)}), f32[16,256,128]{2,1,0:T(8,128)S(1)}, u32[]{:S(2)}, u32[]{:S(2)}) %all-to-all-start) | async-done | bytes 2097184 | tf_op jit(solution)/shard_map/all_to_all | solution.py:287
  69.5 1.3 copy-done.1
  70.8 36.3 %shard_map.69 = f32[2048,128]{1,0:T(8,128)} custom-call(f32[4096,128]{1,0:T(8,128)} %bitcast.56, bf16[512,256]{1,0:T(8,128)(2,1)} %get-tuple-element.28.refs_0_, bf16[512,256]{1,0:T(8,128)(2,1)} %get-tuple-element.29.refs_1_, s32[512,1]{1,0:T(8,128)} %copy.14.refs_2_, bf16[1024,512]{1,0:T(8,128)(2,1)} %get-tuple-element.26.refs_3_, ...), custom_call_target="tpu_custom_call" | custom-call | tf_op jit(solution)/shard_map/pallas_call | solution.py:110
  107.1 1.6 %slice.93 = f32[2048,64]{1,0:T(8,128)S(1)} slice(f32[2048,128]{1,0:T(8,128)} %shard_map.69), slice={[0:2048], [64:128]} | slice | bytes 1048576 | tf_op jit(solution)/shard_map/slice | solution.py:294
  108.6 1.5 reshape.83
  110.1 9.4 %all-to-all-start.1 = ((f32[128,1,1024]{2,1,0:T(1,128)}), f32[128,1,1024]{2,1,0:T(1,128)S(1)}, u32[]{:S(2)}, u32[]{:S(2)}) async-start(f32[128,1,1024]{2,1,0:T(1,128)} %reshape.83), calls=%async_computation.1 | async-start | bytes 1048576 | tf_op jit(solution)/shard_map/all_to_all | solution.py:305
  119.6 2.0 %copy.20.offset_ref = s32[8,512,1]{2,1,0:T(8,128)} copy(s32[8,512,1]{1,0,2:T(8,128)S(1)} %subtract_bitcast_fusion.1) | data formatting | bytes 32768 | tf_op jit(solution)/shard_map/broadcast_in_dim | solution.py:243
  121.7 0.1 fusion.41
  121.9 0.3 fusion.33
  122.2 11.1 %all-to-all-done.1 = f32[128,1,1024]{2,1,0:T(1,128)S(1)} async-done(((f32[128,1,1024]{2,1,0:T(1,128)}), f32[128,1,1024]{2,1,0:T(1,128)S(1)}, u32[]{:S(2)}, u32[]{:S(2)}) %all-to-all-start.1) | async-done | bytes 524320 | tf_op jit(solution)/shard_map/all_to_all | solution.py:305
  133.2 0.5 broadcast.98
  133.8 1.9 %reduce = f32[128,1024]{1,0:T(8,128)S(1)} reduce(f32[128,1,1024]{2,1,0:T(1,128)S(1)} %all-to-all-done.1, f32[]{:T(128)} %broadcast.98), dimensions={1}, to_apply=%all_to_all.7.reduce_sub_computation | reduce | bytes 1048580 | tf_op jit(solution)/shard_map/all_to_all | solution.py:305
  135.6 0.3 reshape.84
  135.9 0.6 copy.25
  136.5 0.2 reshape_reshape.3
  136.8 1.1 convolution_bitcast_fusion
  137.9 0.2 add_bitcast_fusion
  138.0 1.0 fusion.6
  139.1 0.3 fusion.13
  139.4 1.9 %copy.19 = f32[16,64,64]{0,2,1:T(8,128)S(1)} copy(f32[16,64,64]{1,2,0:T(8,128)S(1)} %fusion.13) | data formatting | bytes 524288 | tf_op jit(solution)/shard_map/transpose | solution.py:239
  141.3 1.4 copy.21
  142.7 6.3 %shard_map.70 = f32[512,16]{1,0:T(8,128)} custom-call(f32[4096,16]{1,0:T(8,128)} %bitcast.55, s32[8,512,1]{2,1,0:T(8,128)} %copy.20.offset_ref), custom_call_target="tpu_custom_call" | custom-call | tf_op jit(solution)/shard_map/pallas_call | solution.py:245
  149.0 1.7 %copy.22 = f32[16,512]{1,0:T(8,128)} copy(f32[16,512]{0,1:T(8,128)} %bitcast.62) | data formatting | bytes 65536
  (11 shorter events, 0.3 us)
Async XLA Ops:
  1.9 8.4 %collective-permute-start = (bf16[256,256]{0,1:T(8,128)(2,1)S(1)}, bf16[256,256]{0,1:T(8,128)(2,1)S(1)}, u32[]{:S(2)}, u32[]{:S(2)}) collective-permute-start(bf16[256,256]{0,1:T(8,128)(2,1)S(1)} %slice.92), channel_id=1, source_target_pairs={{0,1},{1,2},{2,3},{3,4},{4,5},{5,6},{6,7},{8,9},{9,10},{10,11},{11... | collective-permute-start | bytes 393224 | tf_op jit(solution)/shard_map/ppermute | solution.py:263
  32.2 37.3 %all-to-all-start = ((f32[16,256,128]{2,1,0:T(8,128)}), f32[16,256,128]{2,1,0:T(8,128)S(1)}, u32[]{:S(2)}, u32[]{:S(2)}) async-start(f32[16,256,128]{2,1,0:T(8,128)} %shard_map.68), calls=%async_computation | async-start | bytes 4194304 | tf_op jit(solution)/shard_map/all_to_all | solution.py:287
  69.5 1.3 copy-start.1
  107.1 12.5 %copy-start.2 = (s32[8,512]{1,0:T(8,128)S(1)}, s32[8,512]{1,0:T(8,128)}, u32[]{:S(2)}) copy-start(s32[8,512]{1,0:T(8,128)} %param.9) | copy-start | bytes 49156
  110.1 23.1 %all-to-all-start.1 = ((f32[128,1,1024]{2,1,0:T(1,128)}), f32[128,1,1024]{2,1,0:T(1,128)S(1)}, u32[]{:S(2)}, u32[]{:S(2)}) async-start(f32[128,1,1024]{2,1,0:T(1,128)} %reshape.83), calls=%async_computation.1 | async-start | bytes 1048576 | tf_op jit(solution)/shard_map/all_to_all | solution.py:305
  141.3 1.4 copy-start

commit v7 on v6

--- a/solution.py
+++ b/solution.py
@@ -15,7 +15,7 @@
 HARM = 8
 RAW_HALO = 256
 SUB_HALO = 64
-TILE = 256
+TILE = 512
 LANES = 128
 PIECES = 2
 
@@ -141,7 +141,7 @@
     return jnp.where(lane < amount, previous, rolled)
 
 
-def local_kernel(plan, sub, base, first_ref, second_ref, shift_ref, x_ref, out_ref, *bufs):
+def local_kernel(plan, sub, base, table_ref, x_ref, out_ref, *bufs):
     count = len(plan)
     final = bufs[-1]
     source = x_ref
@@ -150,9 +150,9 @@
 
         def body(row, carry, source=source, target=target, step=step,
                  bands_out=bands_out, last=step == count - 1):
-            lower = source[first_ref[step, row], :, pl.ds(0, bands_out, stride=2), :]
-            upper = source[second_ref[step, row], :, pl.ds(1, bands_out, stride=2), :]
-            merged = lower + delayed(upper, shift_ref[step, row])
+            lower = source[table_ref[0, step, row], :, pl.ds(0, bands_out, stride=2), :]
+            upper = source[table_ref[1, step, row], :, pl.ds(1, bands_out, stride=2), :]
+            merged = lower + delayed(upper, table_ref[2, step, row])
             if last:
                 target[:, pl.ds(row, 1), :] = merged
             else:
@@ -173,7 +173,7 @@
             out_ref[dest] = jnp.where(lane < LANES - offset, head, tail)
 
 
-def run_local(state, first_rows, second_rows, shifts, plan, parts, sub, base):
+def run_local(state, tables, plan, parts, sub, base):
     slabs = state.shape[1]
     rows_last = plan[-1][1]
     smem = pl.BlockSpec(memory_space=pltpu.SMEM)
@@ -183,11 +183,11 @@
     return pl.pallas_call(
         functools.partial(local_kernel, plan, sub, base),
         out_shape=jax.ShapeDtypeStruct((parts, rows_last, sub + SUB_HALO), jnp.float32),
-        in_specs=[smem, smem, smem, vmem],
+        in_specs=[smem, vmem],
         out_specs=vmem,
         scratch_shapes=scratch,
         compiler_params=pltpu.CompilerParams(vmem_limit_bytes=56 * 1024 * 1024),
-    )(first_rows, second_rows, shifts, state)
+    )(tables, state)
 
 
 def spectra(series, harmonic_bins):
@@ -272,9 +272,7 @@
     sub = samples // chan_count
     pieces = run_local(
         widened.astype(jnp.float32).reshape(channels, -1, LANES).transpose(1, 0, 2)[None],
-        first_rows[:local_levels, :channels],
-        second_rows[:local_levels, :channels],
-        shifts[:local_levels, :channels],
+        jnp.stack([first_rows, second_rows, shifts])[:, :local_levels, :channels],
         local_plan,
         chan_count,
         sub,

time: 152 us -> 142 us (0.934)
  Pallas kernels: 56.8 us -> 52.2 us
  local copies, waits for them, and re-layouts: 30.3 us -> 26.4 us
  starting transfers between devices: 21.7 us -> 18.4 us
    pallas_call x1, Pallas kernels: 36.3 us -> 31.7 us  [run_matmul_levels(): pl.pallas_call(functools.partial(matmul_kernel, plan), out_shape=jax.Shap...]
    slice x3 -> x0, local copies, waits for them, and re-layouts: 3.88 us -> none  [the longest x1 1.3 us: on_device(): first_rows[:local_levels, :channels]]
    all_to_all x1, starting transfers between devices: 9.42 us -> 6.08 us  [on_device(): lax.all_to_all(outgoing, ('chan', 'tm'), split_axis=0, concat_axis=0, til...]
  transfers between devices with their start and end apart: 3 -> 3, of which waited for: 2 -> 3; matrix products, arithmetic and copies ran while one was open for 15% -> 14% of each run, Pallas kernels for 0% -> 0%
where the time goes in v7:
time: 142 us; the launch traced here: 141 us
  Pallas kernels  52.2 us (37%)
  local copies, waits for them, and re-layouts  26.4 us (19%)
  waiting for transfers between devices  25.7 us (18%)
  starting transfers between devices  18.4 us (13%)
  other arithmetic  15.7 us (11%)
  matrix products  2.13 us (2%)
    pallas_call x1, Pallas kernels, run_matmul_levels(): pl.pallas_call(functools.partial(matmul_kernel, plan), out_shape=jax.Shap...  31.7 us
    pallas_call x1, Pallas kernels, run_local(): pl.pallas_call(functools.partial(local_kernel, plan, sub, base), out_shap...  14.1 us
    all_to_all x1, waiting for transfers between devices, on_device(): lax.all_to_all(pieces, 'chan', split_axis=0, concat_axis=0, tiled=True)  14.1 us
    all_to_all x1, waiting for transfers between devices, on_device(): lax.all_to_all(outgoing, ('chan', 'tm'), split_axis=0, concat_axis=0, til...  11.1 us
    all_to_all x1, starting transfers between devices, on_device(): lax.all_to_all(pieces, 'chan', split_axis=0, concat_axis=0, tiled=True)  7.79 us
    unnamed x11, local copies, waits for them, and re-layouts  7.37 us
    another operation x7, local copies, waits for them, and re-layouts, run_matmul_levels(): tables.append(shifts[level, :row_out, None])  7.09 us
    convert_element_type x3, other arithmetic, run_matmul_levels(): (first_rows[level, :row_out, None] == columns).astype(jnp.bfloat16)  6.6 us
  transfers between devices with their start and end apart: 3, of which 3 were waited for; matrix products, arithmetic and copies ran while one was open for 14% of the time, Pallas kernels for 0%

profile of v7, /device:TPU:1, one launch (start us, length us, event | category | flops | bytes accessed | tf_op | source)
XLA Modules:
  0.0 141.4 jit_solution(5236784015484727821)
XLA Ops:
  0.6 1.2 copy.11
  1.9 4.5 %collective-permute-start = (bf16[256,256]{0,1:T(8,128)(2,1)S(1)}, bf16[256,256]{0,1:T(8,128)(2,1)S(1)}, u32[]{:S(2)}, u32[]{:S(2)}) collective-permute-start(bf16[256,256]{0,1:T(8,128)(2,1)S(1)} %slice.84), channel_id=1, source_target_pairs={{0,1},{1,2},{2,3},{3,4},{4,5},{5,6},{6,7},{8,9},{9,10},{10,11},{11... | collective-permute-start | bytes 393224 | tf_op jit(solution)/shard_map/ppermute | solution.py:263
  6.4 1.3 pad_add_fusion.table_ref
  7.8 0.6 collective-permute-done
  8.4 1.3 copy.13
  9.7 14.1 %shard_map.68 = f32[16,256,128]{2,1,0:T(8,128)} custom-call(s32[3,8,256]{2,1,0:T(8,128)} %pad_add_fusion.table_ref, f32[1,10,256,128]{3,2,1,0:T(8,128)} %bitcast.60), custom_call_target="tpu_custom_call" | custom-call | tf_op jit(solution)/shard_map/pallas_call | solution.py:183
  23.8 0.7 slice.65
  24.6 0.8 slice.68
  25.3 0.7 slice.66
  26.0 0.8 slice.69
  26.8 0.7 slice_bitcast_fusion.3
  27.5 0.8 slice_bitcast_fusion.2
  28.3 0.9 fusion.48
  29.2 1.0 slice_bitcast_fusion
  30.2 7.8 %all-to-all-start = ((f32[16,256,128]{2,1,0:T(8,128)}), f32[16,256,128]{2,1,0:T(8,128)S(1)}, u32[]{:S(2)}, u32[]{:S(2)}) async-start(f32[16,256,128]{2,1,0:T(8,128)} %shard_map.68), calls=%async_computation | async-start | bytes 4194304 | tf_op jit(solution)/shard_map/all_to_all | solution.py:285
  38.0 0.9 copy.14.refs_2_
  38.9 1.0 copy.15.refs_5_
  39.9 1.4 copy.16.refs_8_
  41.3 1.4 copy.17.refs_11_
  42.6 1.6 %fusion.4 = (bf16[1024,512]{1,0:T(8,128)(2,1)}, bf16[1024,512]{1,0:T(8,128)(2,1)}) fusion(s32[1024]{0:T(1024)S(1)} %bitcast.73, s32[1024]{0:T(1024)S(1)} %bitcast.74), kind=kLoop, calls=%fused_computation.10 | loop fusion | flops 2097152 | bytes 2105344 | tf_op jit(solution)/shard_map/convert_element_type | solution.py:104
  44.3 1.0 fusion.15
  45.3 2.4 %fusion.1.refs_7_ = bf16[2048,1024]{1,0:T(8,128)(2,1)} fusion(s32[2048]{0:T(1024)S(1)} %bitcast.70), kind=kLoop, calls=%fused_computation.5 | loop fusion | flops 4194304 | bytes 4202496 | tf_op jit(solution)/shard_map/convert_element_type | solution.py:105
  47.7 2.3 %fusion.3.refs_10_ = bf16[2048,1024]{1,0:T(8,128)(2,1)} fusion(s32[2048]{0:T(1024)S(1)} %bitcast.69), kind=kLoop, calls=%fused_computation.7 | loop fusion | flops 4194304 | bytes 4202496 | tf_op jit(solution)/shard_map/convert_element_type | solution.py:105
  50.0 4.0 %fusion = (bf16[2048,1024]{1,0:T(8,128)(2,1)}, bf16[2048,1024]{1,0:T(8,128)(2,1)}) fusion(s32[2048]{0:T(1024)S(1)} %bitcast.72, s32[2048]{0:T(1024)S(1)} %bitcast.71), kind=kLoop, calls=%fused_computation.4 | loop fusion | flops 8388608 | bytes 8404992 | tf_op jit(solution)/shard_map/convert_element_type | solution.py:104
  54.0 14.1 %all-to-all-done = f32[16,256,128]{2,1,0:T(8,128)S(1)} async-done(((f32[16,256,128]{2,1,0:T(8,128)}), f32[16,256,128]{2,1,0:T(8,128)S(1)}, u32[]{:S(2)}, u32[]{:S(2)}) %all-to-all-start) | async-done | bytes 2097184 | tf_op jit(solution)/shard_map/all_to_all | solution.py:285
  68.0 1.3 copy-done.1
  69.4 31.7 %shard_map.69 = f32[2048,128]{1,0:T(8,128)} custom-call(f32[4096,128]{1,0:T(8,128)} %bitcast.59, bf16[512,256]{1,0:T(8,128)(2,1)} %get-tuple-element.28.refs_0_, bf16[512,256]{1,0:T(8,128)(2,1)} %get-tuple-element.29.refs_1_, s32[512,1]{1,0:T(8,128)} %copy.14.refs_2_, bf16[1024,512]{1,0:T(8,128)(2,1)} %get-tuple-element.26.refs_3_, ...), custom_call_target="tpu_custom_call" | custom-call | tf_op jit(solution)/shard_map/pallas_call | solution.py:110
  101.1 1.6 %slice.85 = f32[2048,64]{1,0:T(8,128)S(1)} slice(f32[2048,128]{1,0:T(8,128)} %shard_map.69), slice={[0:2048], [64:128]} | slice | bytes 1048576 | tf_op jit(solution)/shard_map/slice | solution.py:292
  102.7 1.5 %reshape.83 = f32[128,1,1024]{2,1,0:T(1,128)} reshape(f32[128,16,64]{2,1,0:T(8,128)S(1)} %bitcast.61) | data formatting | bytes 1048576
  104.1 6.1 %all-to-all-start.1 = ((f32[128,1,1024]{2,1,0:T(1,128)}), f32[128,1,1024]{2,1,0:T(1,128)S(1)}, u32[]{:S(2)}, u32[]{:S(2)}) async-start(f32[128,1,1024]{2,1,0:T(1,128)} %reshape.83), calls=%async_computation.1 | async-start | bytes 1048576 | tf_op jit(solution)/shard_map/all_to_all | solution.py:303
  110.3 2.0 %copy.20.offset_ref = s32[8,512,1]{2,1,0:T(8,128)} copy(s32[8,512,1]{1,0,2:T(8,128)S(1)} %subtract_bitcast_fusion.1) | data formatting | bytes 32768 | tf_op jit(solution)/shard_map/broadcast_in_dim | solution.py:243
  112.3 0.1 fusion.43
  112.4 0.1 fusion.41
  112.6 0.3 fusion.33
  112.9 11.1 %all-to-all-done.1 = f32[128,1,1024]{2,1,0:T(1,128)S(1)} async-done(((f32[128,1,1024]{2,1,0:T(1,128)}), f32[128,1,1024]{2,1,0:T(1,128)S(1)}, u32[]{:S(2)}, u32[]{:S(2)}) %all-to-all-start.1) | async-done | bytes 524320 | tf_op jit(solution)/shard_map/all_to_all | solution.py:303
  123.9 0.5 broadcast.98
  124.4 1.9 %reduce = f32[128,1024]{1,0:T(8,128)S(1)} reduce(f32[128,1,1024]{2,1,0:T(1,128)S(1)} %all-to-all-done.1, f32[]{:T(128)} %broadcast.98), dimensions={1}, to_apply=%all_to_all.7.reduce_sub_computation | reduce | bytes 1048580 | tf_op jit(solution)/shard_map/all_to_all | solution.py:303
  126.3 0.3 reshape.84
  126.6 0.6 copy.25
  127.2 0.2 reshape_reshape.3
  127.4 1.1 convolution_bitcast_fusion
  128.5 0.2 add_bitcast_fusion
  128.7 1.0 fusion.6
  129.8 0.3 fusion.13
  130.1 1.9 %copy.19 = f32[16,64,64]{0,2,1:T(8,128)S(1)} copy(f32[16,64,64]{1,2,0:T(8,128)S(1)} %fusion.13) | data formatting | bytes 524288 | tf_op jit(solution)/shard_map/transpose | solution.py:239
  132.0 1.4 copy.21
  133.4 6.3 %shard_map.70 = f32[512,16]{1,0:T(8,128)} custom-call(f32[4096,16]{1,0:T(8,128)} %bitcast.58, s32[8,512,1]{2,1,0:T(8,128)} %copy.20.offset_ref), custom_call_target="tpu_custom_call" | custom-call | tf_op jit(solution)/shard_map/pallas_call | solution.py:245
  139.7 1.7 %copy.22 = f32[16,512]{1,0:T(8,128)} copy(f32[16,512]{0,1:T(8,128)} %bitcast.65) | data formatting | bytes 65536
  (9 shorter events, 0.1 us)
Async XLA Ops:
  1.9 6.4 %collective-permute-start = (bf16[256,256]{0,1:T(8,128)(2,1)S(1)}, bf16[256,256]{0,1:T(8,128)(2,1)S(1)}, u32[]{:S(2)}, u32[]{:S(2)}) collective-permute-start(bf16[256,256]{0,1:T(8,128)(2,1)S(1)} %slice.84), channel_id=1, source_target_pairs={{0,1},{1,2},{2,3},{3,4},{4,5},{5,6},{6,7},{8,9},{9,10},{10,11},{11... | collective-permute-start | bytes 393224 | tf_op jit(solution)/shard_map/ppermute | solution.py:263
  30.2 37.8 %all-to-all-start = ((f32[16,256,128]{2,1,0:T(8,128)}), f32[16,256,128]{2,1,0:T(8,128)S(1)}, u32[]{:S(2)}, u32[]{:S(2)}) async-start(f32[16,256,128]{2,1,0:T(8,128)} %shard_map.68), calls=%async_computation | async-start | bytes 4194304 | tf_op jit(solution)/shard_map/all_to_all | solution.py:285
  68.0 1.3 copy-start.1
  101.1 9.1 %copy-start.2 = (s32[8,512]{1,0:T(8,128)S(1)}, s32[8,512]{1,0:T(8,128)}, u32[]{:S(2)}) copy-start(s32[8,512]{1,0:T(8,128)} %param.9) | copy-start | bytes 49156
  104.1 19.8 %all-to-all-start.1 = ((f32[128,1,1024]{2,1,0:T(1,128)}), f32[128,1,1024]{2,1,0:T(1,128)S(1)}, u32[]{:S(2)}, u32[]{:S(2)}) async-start(f32[128,1,1024]{2,1,0:T(1,128)} %reshape.83), calls=%async_computation.1 | async-start | bytes 1048576 | tf_op jit(solution)/shard_map/all_to_all | solution.py:303
  132.0 1.4 copy-start

commit v8 on v7

--- a/solution.py
+++ b/solution.py
@@ -87,9 +87,12 @@
                 for bit in (1, 2, 4, 8):
                     upper = jnp.where((amount & bit) != 0, pltpu.roll(upper, bit, 1), upper)
                 merged = lower + upper
+                skip = SUB_HALO if target is out_ref else 0
                 for member in range(group):
                     start = pl.multiple_of((first_band + member) * row_out + index * TILE, TILE)
-                    target[pl.ds(start, TILE), :] = merged[:, member * width : (member + 1) * width]
+                    target[pl.ds(start, TILE), :] = merged[
+                        :, member * width + skip : (member + 1) * width
+                    ]
                 return carry
 
             lax.fori_loop(0, row_out // TILE, tile, 0)
@@ -109,7 +112,7 @@
     vmem = pl.BlockSpec(memory_space=pltpu.VMEM)
     return pl.pallas_call(
         functools.partial(matmul_kernel, plan),
-        out_shape=jax.ShapeDtypeStruct((plan[-1][1] * plan[-1][2], width), jnp.float32),
+        out_shape=jax.ShapeDtypeStruct((plan[-1][1] * plan[-1][2], width - SUB_HALO), jnp.float32),
         in_specs=[vmem] * (1 + len(tables)),
         out_specs=vmem,
         scratch_shapes=[
@@ -122,7 +125,7 @@
 
 
 def harmonic_kernel(power_ref, offset_ref, out_ref):
-    fundamentals = out_ref.shape[0]
+    fundamentals = out_ref.shape[1]
     total = None
     for order in range(HARM):
         stride = order + 1
@@ -131,7 +134,7 @@
             picked = power_ref[pl.ds(phase, fundamentals, stride=stride), :]
             term = jnp.where(offset == phase, picked, 0.0)
             total = term if total is None else total + term
-    out_ref[...] = total * (1.0 / HARM)
+    out_ref[...] = jnp.transpose(total * (1.0 / HARM))
 
 
 def delayed(value, amount):
@@ -242,13 +245,12 @@
     stride = jnp.arange(1, HARM + 1, dtype=jnp.int32)[:, None]
     offsets = (harmonic_bins - stride * fundamental[None, :])[:, :, None]
     vmem = pl.BlockSpec(memory_space=pltpu.VMEM)
-    harmonic_t = pl.pallas_call(
+    harmonic = pl.pallas_call(
         harmonic_kernel,
-        out_shape=jax.ShapeDtypeStruct((fundamentals, count), jnp.float32),
+        out_shape=jax.ShapeDtypeStruct((count, fundamentals), jnp.float32),
         in_specs=[vmem, vmem],
         out_specs=vmem,
     )(jnp.transpose(spectrum_power), offsets)
-    harmonic = jnp.transpose(harmonic_t)
     return spectrum_power, harmonic
 
 
@@ -296,7 +298,7 @@
         shifts,
         list(range(local_levels, levels)),
         cross_plan,
-    )[:, SUB_HALO:]
+    )
     groups = chan_count * tm_count
     share = NDM // groups
     outgoing = plane.reshape(groups, share, sub)

time: 142 us -> 140 us (0.986)
  local copies, waits for them, and re-layouts: 26.4 us -> 24.4 us
    slice x1 -> x0, local copies, waits for them, and re-layouts: 1.57 us -> none  [on_device(): run_matmul_levels(layers.reshape(chan_count * channels, window), first_ro...]
    unnamed x11 -> x10, local copies, waits for them, and re-layouts: 7.37 us -> 6.93 us
where the time goes in v8:
time: 140 us
  Pallas kernels  52.4 us (37%)
  waiting for transfers between devices  25.7 us (18%)
  local copies, waits for them, and re-layouts  24.4 us (17%)
  starting transfers between devices  18.4 us (13%)
  other arithmetic  15.7 us (11%)
  matrix products  2.13 us (2%)
    pallas_call x1, Pallas kernels, run_matmul_levels(): pl.pallas_call(functools.partial(matmul_kernel, plan), out_shape=jax.Shap...  32 us
    pallas_call x1, Pallas kernels, run_local(): pl.pallas_call(functools.partial(local_kernel, plan, sub, base), out_shap...  14.1 us
    all_to_all x1, waiting for transfers between devices, on_device(): lax.all_to_all(pieces, 'chan', split_axis=0, concat_axis=0, tiled=True)  14.1 us
    all_to_all x1, waiting for transfers between devices, on_device(): lax.all_to_all(outgoing, ('chan', 'tm'), split_axis=0, concat_axis=0, til...  11.1 us
    all_to_all x1, starting transfers between devices, on_device(): lax.all_to_all(pieces, 'chan', split_axis=0, concat_axis=0, tiled=True)  7.79 us
    another operation x7, local copies, waits for them, and re-layouts, run_matmul_levels(): tables.append(shifts[level, :row_out, None])  7.09 us
    unnamed x10, local copies, waits for them, and re-layouts  6.93 us
    convert_element_type x3, other arithmetic, run_matmul_levels(): (first_rows[level, :row_out, None] == columns).astype(jnp.bfloat16)  6.6 us
  transfers between devices with their start and end apart: 3, of which 3 were waited for; matrix products, arithmetic and copies ran while one was open for 14% of the time, Pallas kernels for 0%

profile of v8, /device:TPU:1, one launch (start us, length us, event | category | flops | bytes accessed | tf_op | source)
XLA Modules:
  0.0 139.6 jit_solution(7273703156681674544)
XLA Ops:
  0.6 1.2 copy.10
  1.9 4.5 %collective-permute-start = (bf16[256,256]{0,1:T(8,128)(2,1)S(1)}, bf16[256,256]{0,1:T(8,128)(2,1)S(1)}, u32[]{:S(2)}, u32[]{:S(2)}) collective-permute-start(bf16[256,256]{0,1:T(8,128)(2,1)S(1)} %slice.80), channel_id=1, source_target_pairs={{0,1},{1,2},{2,3},{3,4},{4,5},{5,6},{6,7},{8,9},{9,10},{10,11},{11... | collective-permute-start | bytes 393224 | tf_op jit(solution)/shard_map/ppermute | solution.py:265
  6.4 1.3 pad_add_fusion.table_ref
  7.8 0.6 collective-permute-done
  8.4 1.3 copy.12
  9.7 14.1 %shard_map.68 = f32[16,256,128]{2,1,0:T(8,128)} custom-call(s32[3,8,256]{2,1,0:T(8,128)} %pad_add_fusion.table_ref, f32[1,10,256,128]{3,2,1,0:T(8,128)} %bitcast.59), custom_call_target="tpu_custom_call" | custom-call | tf_op jit(solution)/shard_map/pallas_call | solution.py:186
  23.8 0.7 slice.62
  24.6 0.8 slice.65
  25.3 0.7 slice.63
  26.0 0.8 slice.66
  26.8 0.7 slice_bitcast_fusion.3
  27.5 0.8 slice_bitcast_fusion.2
  28.3 0.9 fusion.48
  29.2 1.0 slice_bitcast_fusion
  30.2 7.8 %all-to-all-start = ((f32[16,256,128]{2,1,0:T(8,128)}), f32[16,256,128]{2,1,0:T(8,128)S(1)}, u32[]{:S(2)}, u32[]{:S(2)}) async-start(f32[16,256,128]{2,1,0:T(8,128)} %shard_map.68), calls=%async_computation | async-start | bytes 4194304 | tf_op jit(solution)/shard_map/all_to_all | solution.py:287
  38.0 0.9 copy.13.refs_2_
  38.9 1.0 copy.14.refs_5_
  39.9 1.4 copy.15.refs_8_
  41.2 1.4 copy.16.refs_11_
  42.6 1.6 %fusion.4 = (bf16[1024,512]{1,0:T(8,128)(2,1)}, bf16[1024,512]{1,0:T(8,128)(2,1)}) fusion(s32[1024]{0:T(1024)S(1)} %bitcast.71, s32[1024]{0:T(1024)S(1)} %bitcast.72), kind=kLoop, calls=%fused_computation.10 | loop fusion | flops 2097152 | bytes 2105344 | tf_op jit(solution)/shard_map/convert_element_type | solution.py:107
  44.3 1.0 fusion.15
  45.3 2.4 %fusion.1.refs_7_ = bf16[2048,1024]{1,0:T(8,128)(2,1)} fusion(s32[2048]{0:T(1024)S(1)} %bitcast.68), kind=kLoop, calls=%fused_computation.5 | loop fusion | flops 4194304 | bytes 4202496 | tf_op jit(solution)/shard_map/convert_element_type | solution.py:108
  47.6 2.3 %fusion.3.refs_10_ = bf16[2048,1024]{1,0:T(8,128)(2,1)} fusion(s32[2048]{0:T(1024)S(1)} %bitcast.67), kind=kLoop, calls=%fused_computation.7 | loop fusion | flops 4194304 | bytes 4202496 | tf_op jit(solution)/shard_map/convert_element_type | solution.py:108
  50.0 4.0 %fusion = (bf16[2048,1024]{1,0:T(8,128)(2,1)}, bf16[2048,1024]{1,0:T(8,128)(2,1)}) fusion(s32[2048]{0:T(1024)S(1)} %bitcast.70, s32[2048]{0:T(1024)S(1)} %bitcast.69), kind=kLoop, calls=%fused_computation.4 | loop fusion | flops 8388608 | bytes 8404992 | tf_op jit(solution)/shard_map/convert_element_type | solution.py:107
  53.9 14.1 %all-to-all-done = f32[16,256,128]{2,1,0:T(8,128)S(1)} async-done(((f32[16,256,128]{2,1,0:T(8,128)}), f32[16,256,128]{2,1,0:T(8,128)S(1)}, u32[]{:S(2)}, u32[]{:S(2)}) %all-to-all-start) | async-done | bytes 2097184 | tf_op jit(solution)/shard_map/all_to_all | solution.py:287
  68.0 1.3 copy-done.1
  69.3 32.0 %shard_map.69 = f32[2048,64]{1,0:T(8,128)} custom-call(f32[4096,128]{1,0:T(8,128)} %bitcast.58, bf16[512,256]{1,0:T(8,128)(2,1)} %get-tuple-element.28.refs_0_, bf16[512,256]{1,0:T(8,128)(2,1)} %get-tuple-element.29.refs_1_, s32[512,1]{1,0:T(8,128)} %copy.13.refs_2_, bf16[1024,512]{1,0:T(8,128)(2,1)} %get-tuple-element.26.refs_3_, ...), custom_call_target="tpu_custom_call" | custom-call | tf_op jit(solution)/shard_map/pallas_call | solution.py:113
  101.4 2.7 %reshape.83 = f32[128,1,1024]{2,1,0:T(1,128)} reshape(f32[128,16,64]{2,1,0:T(8,128)} %bitcast.60) | data formatting | bytes 1048576
  104.0 6.1 %all-to-all-start.1 = ((f32[128,1,1024]{2,1,0:T(1,128)}), f32[128,1,1024]{2,1,0:T(1,128)S(1)}, u32[]{:S(2)}, u32[]{:S(2)}) async-start(f32[128,1,1024]{2,1,0:T(1,128)} %reshape.83), calls=%async_computation.1 | async-start | bytes 1048576 | tf_op jit(solution)/shard_map/all_to_all | solution.py:305
  110.1 0.1 subtract_bitcast_fusion.1
  110.2 2.0 %copy.19.offset_ref = s32[8,512,1]{2,1,0:T(8,128)} copy(s32[8,512,1]{1,0,2:T(8,128)S(1)} %subtract_bitcast_fusion.1) | data formatting | bytes 32768 | tf_op jit(solution)/shard_map/broadcast_in_dim | solution.py:246
  112.2 0.1 fusion.43
  112.3 0.1 fusion.41
  112.5 0.3 fusion.33
  112.8 11.1 %all-to-all-done.1 = f32[128,1,1024]{2,1,0:T(1,128)S(1)} async-done(((f32[128,1,1024]{2,1,0:T(1,128)}), f32[128,1,1024]{2,1,0:T(1,128)S(1)}, u32[]{:S(2)}, u32[]{:S(2)}) %all-to-all-start.1) | async-done | bytes 524320 | tf_op jit(solution)/shard_map/all_to_all | solution.py:305
  123.8 0.5 broadcast.98
  124.4 1.9 %reduce = f32[128,1024]{1,0:T(8,128)S(1)} reduce(f32[128,1,1024]{2,1,0:T(1,128)S(1)} %all-to-all-done.1, f32[]{:T(128)} %broadcast.98), dimensions={1}, to_apply=%all_to_all.7.reduce_sub_computation | reduce | bytes 1048580 | tf_op jit(solution)/shard_map/all_to_all | solution.py:305
  126.3 0.3 reshape.84
  126.5 0.6 copy.23
  127.1 0.2 reshape_reshape.3
  127.4 1.1 convolution_bitcast_fusion
  128.5 0.2 add_bitcast_fusion
  128.6 1.0 fusion.6
  129.7 0.3 fusion.13
  130.0 1.9 %copy.18 = f32[16,64,64]{0,2,1:T(8,128)S(1)} copy(f32[16,64,64]{1,2,0:T(8,128)S(1)} %fusion.13) | data formatting | bytes 524288 | tf_op jit(solution)/shard_map/transpose | solution.py:242
  131.9 0.0 copy-start
  131.9 1.4 copy.20
  133.3 6.3 %shard_map.70 = f32[16,512]{1,0:T(8,128)} custom-call(f32[4096,16]{1,0:T(8,128)} %bitcast.57, s32[8,512,1]{2,1,0:T(8,128)} %copy.19.offset_ref), custom_call_target="tpu_custom_call" | custom-call | tf_op jit(solution)/shard_map/pallas_call | solution.py:248
  (7 shorter events, 0.1 us)
Async XLA Ops:
  1.9 6.4 %collective-permute-start = (bf16[256,256]{0,1:T(8,128)(2,1)S(1)}, bf16[256,256]{0,1:T(8,128)(2,1)S(1)}, u32[]{:S(2)}, u32[]{:S(2)}) collective-permute-start(bf16[256,256]{0,1:T(8,128)(2,1)S(1)} %slice.80), channel_id=1, source_target_pairs={{0,1},{1,2},{2,3},{3,4},{4,5},{5,6},{6,7},{8,9},{9,10},{10,11},{11... | collective-permute-start | bytes 393224 | tf_op jit(solution)/shard_map/ppermute | solution.py:265
  30.2 37.8 %all-to-all-start = ((f32[16,256,128]{2,1,0:T(8,128)}), f32[16,256,128]{2,1,0:T(8,128)S(1)}, u32[]{:S(2)}, u32[]{:S(2)}) async-start(f32[16,256,128]{2,1,0:T(8,128)} %shard_map.68), calls=%async_computation | async-start | bytes 4194304 | tf_op jit(solution)/shard_map/all_to_all | solution.py:287
  68.0 1.3 copy-start.1
  69.3 40.8 %copy-start.2 = (s32[8,512]{1,0:T(8,128)S(1)}, s32[8,512]{1,0:T(8,128)}, u32[]{:S(2)}) copy-start(s32[8,512]{1,0:T(8,128)} %param.9) | copy-start | bytes 49156
  104.0 19.8 %all-to-all-start.1 = ((f32[128,1,1024]{2,1,0:T(1,128)}), f32[128,1,1024]{2,1,0:T(1,128)S(1)}, u32[]{:S(2)}, u32[]{:S(2)}) async-start(f32[128,1,1024]{2,1,0:T(1,128)} %reshape.83), calls=%async_computation.1 | async-start | bytes 1048576 | tf_op jit(solution)/shard_map/all_to_all | solution.py:305
  131.9 1.4 %copy-start = (f32[16,64,64]{0,2,1:T(8,128)}, f32[16,64,64]{0,2,1:T(8,128)S(1)}, u32[]{:S(2)}) copy-start(f32[16,64,64]{0,2,1:T(8,128)S(1)} %copy.18) | copy-start | bytes 786436

commit v9 on v8

--- a/solution.py
+++ b/solution.py
@@ -18,6 +18,7 @@
 TILE = 512
 LANES = 128
 PIECES = 2
+MESH = pl.DeviceIdType.MESH
 
 
 def shift_right(value, amount):
@@ -193,6 +194,65 @@
     )(tables, state)
 
 
+def exchange_kernel(axis, parts_ref, out_ref, landing, send_sem, recv_sem, local_sem):
+    count = parts_ref.shape[0]
+    me = lax.axis_index(axis)
+    barrier = pltpu.get_barrier_semaphore()
+    for step in range(1, count):
+        pl.semaphore_signal(
+            barrier, inc=1, device_id={axis: lax.rem(me + step, count)}, device_id_type=MESH
+        )
+    pl.semaphore_wait(barrier, count - 1)
+    sends = []
+    for step in range(1, count):
+        peer = lax.rem(me + step, count)
+        copy = pltpu.make_async_remote_copy(
+            src_ref=parts_ref.at[peer],
+            dst_ref=landing.at[me],
+            send_sem=send_sem.at[step],
+            recv_sem=recv_sem.at[step],
+            device_id={axis: peer},
+            device_id_type=MESH,
+        )
+        copy.start()
+        sends.append(copy)
+    local = pltpu.make_async_copy(parts_ref.at[me], landing.at[me], local_sem)
+    local.start()
+    local.wait()
+    for step in range(1, count):
+        sends[step - 1].wait_send()
+        origin = lax.rem(me - step + count, count)
+        pltpu.make_async_remote_copy(
+            src_ref=parts_ref.at[origin],
+            dst_ref=landing.at[origin],
+            send_sem=send_sem.at[step],
+            recv_sem=recv_sem.at[step],
+            device_id={axis: origin},
+            device_id_type=MESH,
+        ).wait_recv()
+    out_ref[...] = landing[...]
+
+
+def exchange(parts, axis):
+    count = parts.shape[0]
+    vmem = pl.BlockSpec(memory_space=pltpu.VMEM)
+    return pl.pallas_call(
+        functools.partial(exchange_kernel, axis),
+        out_shape=jax.ShapeDtypeStruct(parts.shape, parts.dtype),
+        in_specs=[vmem],
+        out_specs=vmem,
+        scratch_shapes=[
+            pltpu.VMEM(parts.shape, parts.dtype),
+            pltpu.SemaphoreType.DMA((count,)),
+            pltpu.SemaphoreType.DMA((count,)),
+            pltpu.SemaphoreType.DMA(()),
+        ],
+        compiler_params=pltpu.CompilerParams(
+            collective_id=0, has_side_effects=True, vmem_limit_bytes=32 * 1024 * 1024
+        ),
+    )(parts)
+
+
 def spectra(series, harmonic_bins):
     count = series.shape[0]
     total = series.shape[1]
@@ -284,7 +344,7 @@
         (pieces, first_rows, second_rows, shifts)
     )
     window = sub + SUB_HALO
-    layers = lax.all_to_all(pieces, "chan", split_axis=0, concat_axis=0, tiled=True)
+    layers = exchange(pieces, "chan")
     cross_plan = []
     bands = chan_count
     for level in range(local_levels, levels):

time: 140 us -> 162 us (1.16)
  Pallas kernels: 52.4 us -> 87 us
  waiting for transfers between devices: 25.7 us -> 11.7 us
    pallas_call x0 -> x1, Pallas kernels: none -> 34.7 us  [exchange(): pl.pallas_call(functools.partial(exchange_kernel, axis), out_shape=jax.Sh...]
    all_to_all x1 -> x0, waiting for transfers between devices: 14.1 us -> none  [on_device(): lax.all_to_all(pieces, 'chan', split_axis=0, concat_axis=0, tiled=True)]
    all_to_all x1 -> x0, starting transfers between devices: 7.79 us -> none  [on_device(): lax.all_to_all(pieces, 'chan', split_axis=0, concat_axis=0, tiled=True)]
    all_to_all x1, starting transfers between devices: 6.08 us -> 13.4 us  [on_device(): lax.all_to_all(outgoing, ('chan', 'tm'), split_axis=0, concat_axis=0, til...]
    unnamed x10 -> x12, local copies, waits for them, and re-layouts: 6.93 us -> 8.49 us
  transfers between devices with their start and end apart: 3 -> 2, of which waited for: 3 -> 2; matrix products, arithmetic and copies ran while one was open for 14% -> 2% of each run, Pallas kernels for 0% -> 0%
where the time goes in v9:
time: 162 us; the launch traced here: 161 us
  Pallas kernels  87 us (54%)
  local copies, waits for them, and re-layouts  25.9 us (16%)
  starting transfers between devices  17.9 us (11%)
  other arithmetic  15.7 us (10%)
  waiting for transfers between devices  11.7 us (7%)
  matrix products  2.13 us (1%)
    pallas_call x1, Pallas kernels, exchange(): pl.pallas_call(functools.partial(exchange_kernel, axis), out_shape=jax.Sh...  34.7 us
    pallas_call x1, Pallas kernels, run_matmul_levels(): pl.pallas_call(functools.partial(matmul_kernel, plan), out_shape=jax.Shap...  31.9 us
    pallas_call x1, Pallas kernels, run_local(): pl.pallas_call(functools.partial(local_kernel, plan, sub, base), out_shap...  14.1 us
    all_to_all x1, starting transfers between devices, on_device(): lax.all_to_all(outgoing, ('chan', 'tm'), split_axis=0, concat_axis=0, til...  13.4 us
    all_to_all x1, waiting for transfers between devices, on_device(): lax.all_to_all(outgoing, ('chan', 'tm'), split_axis=0, concat_axis=0, til...  11.1 us
    unnamed x12, local copies, waits for them, and re-layouts  8.49 us
    another operation x7, local copies, waits for them, and re-layouts, run_matmul_levels(): tables.append(shifts[level, :row_out, None])  7.08 us
    convert_element_type x3, other arithmetic, run_matmul_levels(): (first_rows[level, :row_out, None] == columns).astype(jnp.bfloat16)  6.62 us
  transfers between devices with their start and end apart: 2, of which 2 were waited for; matrix products, arithmetic and copies ran while one was open for 2% of the time, Pallas kernels for 0%

profile of v9, /device:TPU:1, one launch (start us, length us, event | category | flops | bytes accessed | tf_op | source)
XLA Modules:
  0.0 161.2 jit_solution(13910046292456367861)
XLA Ops:
  0.6 1.2 copy.10
  1.9 4.5 %collective-permute-start = (bf16[256,256]{0,1:T(8,128)(2,1)S(1)}, bf16[256,256]{0,1:T(8,128)(2,1)S(1)}, u32[]{:S(2)}, u32[]{:S(2)}) collective-permute-start(bf16[256,256]{0,1:T(8,128)(2,1)S(1)} %slice.80), channel_id=1, source_target_pairs={{0,1},{1,2},{2,3},{3,4},{4,5},{5,6},{6,7},{8,9},{9,10},{10,11},{11... | collective-permute-start | bytes 393224 | tf_op jit(solution)/shard_map/ppermute | solution.py:325
  6.4 1.3 pad_add_fusion.table_ref
  7.8 0.6 collective-permute-done
  8.4 1.3 copy.12
  9.7 14.1 %shard_map.68.parts_ref = f32[16,256,128]{2,1,0:T(8,128)} custom-call(s32[3,8,256]{2,1,0:T(8,128)} %pad_add_fusion.table_ref, f32[1,10,256,128]{3,2,1,0:T(8,128)} %bitcast.59), custom_call_target="tpu_custom_call" | custom-call | tf_op jit(solution)/shard_map/pallas_call | solution.py:187
  23.8 0.7 slice.62
  24.5 0.8 slice.65
  25.3 0.7 slice.63
  26.0 0.8 slice.66
  26.8 0.7 slice_bitcast_fusion.3
  27.5 0.8 slice_bitcast_fusion.2
  28.3 0.9 fusion.48
  29.2 1.0 slice_bitcast_fusion
  30.2 0.0 copy-start.1
  30.2 1.6 copy-done.1
  31.8 34.7 %shard_map.69 = f32[16,256,128]{2,1,0:T(8,128)S(1)} custom-call(f32[16,256,128]{2,1,0:T(8,128)S(1)} %copy-done.1), custom_call_target="tpu_custom_call" | custom-call | tf_op jit(solution)/shard_map/pallas_call | solution.py:239
  66.4 1.3 copy-done
  67.8 0.9 copy.13.refs_2_
  68.6 1.0 copy.14.refs_5_
  69.6 2.4 %fusion.1.refs_7_ = bf16[2048,1024]{1,0:T(8,128)(2,1)} fusion(s32[2048]{0:T(1024)S(1)} %bitcast.68), kind=kLoop, calls=%fused_computation.5 | loop fusion | flops 4194304 | bytes 4202496 | tf_op jit(solution)/shard_map/convert_element_type | solution.py:109
  72.0 1.4 copy.15.refs_8_
  73.4 2.3 %fusion.3.refs_10_ = bf16[2048,1024]{1,0:T(8,128)(2,1)} fusion(s32[2048]{0:T(1024)S(1)} %bitcast.67), kind=kLoop, calls=%fused_computation.7 | loop fusion | flops 4194304 | bytes 4202496 | tf_op jit(solution)/shard_map/convert_element_type | solution.py:109
  75.7 1.4 copy.16.refs_11_
  77.1 1.0 fusion.15
  78.1 1.7 %fusion.4 = (bf16[1024,512]{1,0:T(8,128)(2,1)}, bf16[1024,512]{1,0:T(8,128)(2,1)}) fusion(s32[1024]{0:T(1024)S(1)} %bitcast.71, s32[1024]{0:T(1024)S(1)} %bitcast.72), kind=kLoop, calls=%fused_computation.10 | loop fusion | flops 2097152 | bytes 2105344 | tf_op jit(solution)/shard_map/convert_element_type | solution.py:108
  79.8 3.9 %fusion = (bf16[2048,1024]{1,0:T(8,128)(2,1)}, bf16[2048,1024]{1,0:T(8,128)(2,1)}) fusion(s32[2048]{0:T(1024)S(1)} %bitcast.70, s32[2048]{0:T(1024)S(1)} %bitcast.69), kind=kLoop, calls=%fused_computation.4 | loop fusion | flops 8388608 | bytes 8404992 | tf_op jit(solution)/shard_map/convert_element_type | solution.py:108
  83.7 31.9 %shard_map.70 = f32[2048,64]{1,0:T(8,128)} custom-call(f32[4096,128]{1,0:T(8,128)} %bitcast.56, bf16[512,256]{1,0:T(8,128)(2,1)} %get-tuple-element.28.refs_0_, bf16[512,256]{1,0:T(8,128)(2,1)} %get-tuple-element.29.refs_1_, s32[512,1]{1,0:T(8,128)} %copy.13.refs_2_, bf16[1024,512]{1,0:T(8,128)(2,1)} %get-tuple-element.26.refs_3_, ...), custom_call_target="tpu_custom_call" | custom-call | tf_op jit(solution)/shard_map/pallas_call | solution.py:114
  115.7 2.7 %reshape.83 = f32[128,1,1024]{2,1,0:T(1,128)} reshape(f32[128,16,64]{2,1,0:T(8,128)} %bitcast.60) | data formatting | bytes 1048576
  118.3 13.4 %all-to-all-start = ((f32[128,1,1024]{2,1,0:T(1,128)}), f32[128,1,1024]{2,1,0:T(1,128)S(1)}, u32[]{:S(2)}, u32[]{:S(2)}) async-start(f32[128,1,1024]{2,1,0:T(1,128)} %reshape.83), calls=%async_computation | async-start | bytes 1048576 | tf_op jit(solution)/shard_map/all_to_all | solution.py:365
  131.7 0.1 subtract_bitcast_fusion.1
  131.8 2.0 %copy.19.offset_ref = s32[8,512,1]{2,1,0:T(8,128)} copy(s32[8,512,1]{1,0,2:T(8,128)S(1)} %subtract_bitcast_fusion.1) | data formatting | bytes 32768 | tf_op jit(solution)/shard_map/broadcast_in_dim | solution.py:306
  133.8 0.1 fusion.43
  133.9 0.1 fusion.41
  134.1 0.3 fusion.33
  134.4 11.1 %all-to-all-done = f32[128,1,1024]{2,1,0:T(1,128)S(1)} async-done(((f32[128,1,1024]{2,1,0:T(1,128)}), f32[128,1,1024]{2,1,0:T(1,128)S(1)}, u32[]{:S(2)}, u32[]{:S(2)}) %all-to-all-start) | async-done | bytes 524320 | tf_op jit(solution)/shard_map/all_to_all | solution.py:365
  145.4 0.5 broadcast.98
  146.0 1.9 %reduce = f32[128,1024]{1,0:T(8,128)S(1)} reduce(f32[128,1,1024]{2,1,0:T(1,128)S(1)} %all-to-all-done, f32[]{:T(128)} %broadcast.98), dimensions={1}, to_apply=%all_to_all.3.reduce_sub_computation | reduce | bytes 1048580 | tf_op jit(solution)/shard_map/all_to_all | solution.py:365
  147.8 0.3 reshape.84
  148.1 0.6 copy.23
  148.7 0.2 reshape_reshape.3
  149.0 1.1 convolution_bitcast_fusion
  150.1 0.2 add_bitcast_fusion
  150.2 1.0 fusion.6
  151.3 0.3 fusion.13
  151.6 1.9 %copy.18 = f32[16,64,64]{0,2,1:T(8,128)S(1)} copy(f32[16,64,64]{1,2,0:T(8,128)S(1)} %fusion.13) | data formatting | bytes 524288 | tf_op jit(solution)/shard_map/transpose | solution.py:302
  153.5 1.4 copy.20
  154.9 6.3 %shard_map.71 = f32[16,512]{1,0:T(8,128)} custom-call(f32[4096,16]{1,0:T(8,128)} %bitcast.58, s32[8,512,1]{2,1,0:T(8,128)} %copy.19.offset_ref), custom_call_target="tpu_custom_call" | custom-call | tf_op jit(solution)/shard_map/pallas_call | solution.py:308
  (8 shorter events, 0.1 us)
Async XLA Ops:
  1.9 6.4 %collective-permute-start = (bf16[256,256]{0,1:T(8,128)(2,1)S(1)}, bf16[256,256]{0,1:T(8,128)(2,1)S(1)}, u32[]{:S(2)}, u32[]{:S(2)}) collective-permute-start(bf16[256,256]{0,1:T(8,128)(2,1)S(1)} %slice.80), channel_id=1, source_target_pairs={{0,1},{1,2},{2,3},{3,4},{4,5},{5,6},{6,7},{8,9},{9,10},{10,11},{11... | collective-permute-start | bytes 393224 | tf_op jit(solution)/shard_map/ppermute | solution.py:325
  30.2 1.6 copy-start.1
  66.4 1.3 copy-start
  83.7 48.0 %copy-start.3 = (s32[8,512]{1,0:T(8,128)S(1)}, s32[8,512]{1,0:T(8,128)}, u32[]{:S(2)}) copy-start(s32[8,512]{1,0:T(8,128)} %param.9) | copy-start | bytes 49156
  118.3 27.1 %all-to-all-start = ((f32[128,1,1024]{2,1,0:T(1,128)}), f32[128,1,1024]{2,1,0:T(1,128)S(1)}, u32[]{:S(2)}, u32[]{:S(2)}) async-start(f32[128,1,1024]{2,1,0:T(1,128)} %reshape.83), calls=%async_computation | async-start | bytes 1048576 | tf_op jit(solution)/shard_map/all_to_all | solution.py:365
  153.5 1.4 copy-start.2

commit v10 on v8

--- a/solution.py
+++ b/solution.py
@@ -52,7 +52,7 @@
 def matmul_kernel(plan, x_ref, *refs):
     count = len(plan)
     tables = refs[: 3 * count]
-    out_ref, buf_a, buf_b, parts = refs[3 * count :]
+    out_ref, buf_a, buf_b, parts, pack = refs[3 * count :]
     width = x_ref.shape[1]
     source = x_ref
     for step, (row_in, row_out, bands_out, depth) in enumerate(plan):
@@ -87,12 +87,19 @@
                 for bit in (1, 2, 4, 8):
                     upper = jnp.where((amount & bit) != 0, pltpu.roll(upper, bit, 1), upper)
                 merged = lower + upper
-                skip = SUB_HALO if target is out_ref else 0
+                if target is out_ref:
+                    pack[...] = merged
+                    even = pack[pl.ds(0, TILE // 2, stride=2), :]
+                    odd = pack[pl.ds(1, TILE // 2, stride=2), :]
+                    lane = lax.broadcasted_iota(jnp.int32, even.shape, 1)
+                    start = pl.multiple_of(index * (TILE // 2), TILE // 2)
+                    target[pl.ds(start, TILE // 2), :] = jnp.where(
+                        lane < SUB_HALO, pltpu.roll(even, SUB_HALO, 1), odd
+                    )
+                    return carry
                 for member in range(group):
                     start = pl.multiple_of((first_band + member) * row_out + index * TILE, TILE)
-                    target[pl.ds(start, TILE), :] = merged[
-                        :, member * width + skip : (member + 1) * width
-                    ]
+                    target[pl.ds(start, TILE), :] = merged[:, member * width : (member + 1) * width]
                 return carry
 
             lax.fori_loop(0, row_out // TILE, tile, 0)
@@ -112,13 +119,14 @@
     vmem = pl.BlockSpec(memory_space=pltpu.VMEM)
     return pl.pallas_call(
         functools.partial(matmul_kernel, plan),
-        out_shape=jax.ShapeDtypeStruct((plan[-1][1] * plan[-1][2], width - SUB_HALO), jnp.float32),
+        out_shape=jax.ShapeDtypeStruct((plan[-1][1] * plan[-1][2] // 2, width), jnp.float32),
         in_specs=[vmem] * (1 + len(tables)),
         out_specs=vmem,
         scratch_shapes=[
             pltpu.VMEM((buf_rows, width), jnp.float32),
             pltpu.VMEM((buf_rows, width), jnp.float32),
             pltpu.VMEM((2, PIECES, depth_most, 2 * width), jnp.bfloat16),
+            pltpu.VMEM((TILE, width), jnp.float32),
         ],
         compiler_params=pltpu.CompilerParams(vmem_limit_bytes=60 * 1024 * 1024),
     )(state, *tables)
@@ -301,11 +309,11 @@
     )
     groups = chan_count * tm_count
     share = NDM // groups
-    outgoing = plane.reshape(groups, share, sub)
+    outgoing = plane.reshape(groups, share // 2, 2 * sub)
     incoming = lax.all_to_all(outgoing, ("chan", "tm"), split_axis=0, concat_axis=0, tiled=True)
     series = (
-        incoming.reshape(chan_count, tm_count, share, sub)
-        .transpose(2, 1, 0, 3)
+        incoming.reshape(chan_count, tm_count, share // 2, 2, sub)
+        .transpose(2, 3, 1, 0, 4)
         .reshape(share, tm_count * samples)
     )
     return spectra(series, harmonic_bins)

time: 140 us -> 136 us (0.971)
  local copies, waits for them, and re-layouts: 24.4 us -> 21.5 us
  other arithmetic: 15.7 us -> 13.9 us
    unnamed x10 -> x8, local copies, waits for them, and re-layouts: 6.93 us -> 3.97 us
    all_to_all x1 -> x0, other arithmetic: 1.88 us -> none  [on_device(): lax.all_to_all(outgoing, ('chan', 'tm'), split_axis=0, concat_axis=0, til...]
  transfers between devices with their start and end apart: 3 -> 3, of which waited for: 3 -> 3; matrix products, arithmetic and copies ran while one was open for 14% -> 15% of each run, Pallas kernels for 0% -> 0%
where the time goes in v10:
time: 136 us; the launch traced here: 135 us
  Pallas kernels  52.3 us (38%)
  waiting for transfers between devices  25.7 us (19%)
  local copies, waits for them, and re-layouts  21.5 us (16%)
  starting transfers between devices  18.4 us (14%)
  other arithmetic  13.9 us (10%)
  matrix products  2.13 us (2%)
    pallas_call x1, Pallas kernels, run_matmul_levels(): pl.pallas_call(functools.partial(matmul_kernel, plan), out_shape=jax.Shap...  31.9 us
    pallas_call x1, Pallas kernels, run_local(): pl.pallas_call(functools.partial(local_kernel, plan, sub, base), out_shap...  14.1 us
    all_to_all x1, waiting for transfers between devices, on_device(): lax.all_to_all(pieces, 'chan', split_axis=0, concat_axis=0, tiled=True)  14 us
    all_to_all x1, waiting for transfers between devices, on_device(): lax.all_to_all(outgoing, ('chan', 'tm'), split_axis=0, concat_axis=0, til...  11.1 us
    all_to_all x1, starting transfers between devices, on_device(): lax.all_to_all(pieces, 'chan', split_axis=0, concat_axis=0, tiled=True)  7.79 us
    another operation x7, local copies, waits for them, and re-layouts, run_matmul_levels(): tables.append(shifts[level, :row_out, None])  7.09 us
    convert_element_type x3, other arithmetic, run_matmul_levels(): (first_rows[level, :row_out, None] == columns).astype(jnp.bfloat16)  6.63 us
    pallas_call x1, Pallas kernels, spectra(): pl.pallas_call(harmonic_kernel, out_shape=jax.ShapeDtypeStruct((count, fu...  6.29 us
  transfers between devices with their start and end apart: 3, of which 3 were waited for; matrix products, arithmetic and copies ran while one was open for 15% of the time, Pallas kernels for 0%

profile of v10, /device:TPU:1, one launch (start us, length us, event | category | flops | bytes accessed | tf_op | source)
XLA Modules:
  0.0 134.7 jit_solution(11759903765683056182)
XLA Ops:
  0.6 1.2 copy.10
  1.9 4.5 %collective-permute-start = (bf16[256,256]{0,1:T(8,128)(2,1)S(1)}, bf16[256,256]{0,1:T(8,128)(2,1)S(1)}, u32[]{:S(2)}, u32[]{:S(2)}) collective-permute-start(bf16[256,256]{0,1:T(8,128)(2,1)S(1)} %slice.80), channel_id=1, source_target_pairs={{0,1},{1,2},{2,3},{3,4},{4,5},{5,6},{6,7},{8,9},{9,10},{10,11},{11... | collective-permute-start | bytes 393224 | tf_op jit(solution)/shard_map/ppermute | solution.py:273
  6.4 1.3 pad_add_fusion.table_ref
  7.8 0.6 collective-permute-done
  8.4 1.3 copy.12
  9.7 14.1 %shard_map.68 = f32[16,256,128]{2,1,0:T(8,128)} custom-call(s32[3,8,256]{2,1,0:T(8,128)} %pad_add_fusion.table_ref, f32[1,10,256,128]{3,2,1,0:T(8,128)} %bitcast.58), custom_call_target="tpu_custom_call" | custom-call | tf_op jit(solution)/shard_map/pallas_call | solution.py:194
  23.8 0.7 slice.62
  24.5 0.8 slice.65
  25.3 0.7 slice.63
  26.0 0.8 slice.66
  26.8 0.7 slice_bitcast_fusion.3
  27.5 0.8 slice_bitcast_fusion.2
  28.3 0.9 fusion.48
  29.2 1.0 slice_bitcast_fusion
  30.2 7.8 %all-to-all-start = ((f32[16,256,128]{2,1,0:T(8,128)}), f32[16,256,128]{2,1,0:T(8,128)S(1)}, u32[]{:S(2)}, u32[]{:S(2)}) async-start(f32[16,256,128]{2,1,0:T(8,128)} %shard_map.68), calls=%async_computation | async-start | bytes 4194304 | tf_op jit(solution)/shard_map/all_to_all | solution.py:295
  38.0 0.9 copy.13.refs_2_
  38.8 1.0 copy.14.refs_5_
  39.9 1.4 %copy.15.refs_8_ = s32[2048,1]{1,0:T(8,128)} copy(s32[2048,1]{0,1:T(1,128)S(1)} %get-tuple-element.17) | data formatting | bytes 16384 | tf_op jit(solution)/shard_map/broadcast_in_dim;squeeze | solution.py:116
  41.2 1.4 %copy.16.refs_11_ = s32[2048,1]{1,0:T(8,128)} copy(s32[2048,1]{0,1:T(1,128)S(1)} %get-tuple-element.16) | data formatting | bytes 16384 | tf_op jit(solution)/shard_map/broadcast_in_dim;squeeze | solution.py:116
  42.6 1.7 %fusion.4 = (bf16[1024,512]{1,0:T(8,128)(2,1)}, bf16[1024,512]{1,0:T(8,128)(2,1)}) fusion(s32[1024]{0:T(1024)S(1)} %bitcast.69, s32[1024]{0:T(1024)S(1)} %bitcast.70), kind=kLoop, calls=%fused_computation.10 | loop fusion | flops 2097152 | bytes 2105344 | tf_op jit(solution)/shard_map/convert_element_type | solution.py:114
  44.3 1.0 fusion.15
  45.3 2.4 %fusion.1.refs_7_ = bf16[2048,1024]{1,0:T(8,128)(2,1)} fusion(s32[2048]{0:T(1024)S(1)} %bitcast.66), kind=kLoop, calls=%fused_computation.5 | loop fusion | flops 4194304 | bytes 4202496 | tf_op jit(solution)/shard_map/convert_element_type | solution.py:115
  47.7 2.3 %fusion.3.refs_10_ = bf16[2048,1024]{1,0:T(8,128)(2,1)} fusion(s32[2048]{0:T(1024)S(1)} %bitcast.65), kind=kLoop, calls=%fused_computation.7 | loop fusion | flops 4194304 | bytes 4202496 | tf_op jit(solution)/shard_map/convert_element_type | solution.py:115
  50.0 4.0 %fusion = (bf16[2048,1024]{1,0:T(8,128)(2,1)}, bf16[2048,1024]{1,0:T(8,128)(2,1)}) fusion(s32[2048]{0:T(1024)S(1)} %bitcast.68, s32[2048]{0:T(1024)S(1)} %bitcast.67), kind=kLoop, calls=%fused_computation.4 | loop fusion | flops 8388608 | bytes 8404992 | tf_op jit(solution)/shard_map/convert_element_type | solution.py:114
  54.0 14.0 %all-to-all-done = f32[16,256,128]{2,1,0:T(8,128)S(1)} async-done(((f32[16,256,128]{2,1,0:T(8,128)}), f32[16,256,128]{2,1,0:T(8,128)S(1)}, u32[]{:S(2)}, u32[]{:S(2)}) %all-to-all-start) | async-done | bytes 2097184 | tf_op jit(solution)/shard_map/all_to_all | solution.py:295
  68.0 0.0 copy-start.1
  68.0 1.3 copy-done.1
  69.3 31.9 %shard_map.69 = f32[1024,128]{1,0:T(8,128)} custom-call(f32[4096,128]{1,0:T(8,128)} %bitcast.57, bf16[512,256]{1,0:T(8,128)(2,1)} %get-tuple-element.28.refs_0_, bf16[512,256]{1,0:T(8,128)(2,1)} %get-tuple-element.29.refs_1_, s32[512,1]{1,0:T(8,128)} %copy.13.refs_2_, bf16[1024,512]{1,0:T(8,128)(2,1)} %get-tuple-element.26.refs_3_, ...), custom_call_target="tpu_custom_call" | custom-call | tf_op jit(solution)/shard_map/pallas_call | solution.py:120
  101.2 6.1 %all-to-all-start.1 = ((f32[128,8,128]{2,1,0:T(8,128)}), f32[128,8,128]{2,1,0:T(8,128)S(1)}, u32[]{:S(2)}, u32[]{:S(2)}) async-start(f32[128,8,128]{2,1,0:T(8,128)} %bitcast.61), calls=%async_computation.1 | async-start | bytes 1048576 | tf_op jit(solution)/shard_map/all_to_all | solution.py:313
  107.3 0.0 copy-done.2
  107.4 0.1 subtract_bitcast_fusion.1
  107.4 2.0 %copy.19.offset_ref = s32[8,512,1]{2,1,0:T(8,128)} copy(s32[8,512,1]{1,0,2:T(8,128)S(1)} %subtract_bitcast_fusion.1) | data formatting | bytes 32768 | tf_op jit(solution)/shard_map/broadcast_in_dim | solution.py:254
  109.4 0.1 fusion.43
  109.6 0.1 fusion.41
  109.7 0.3 fusion.33
  110.0 11.1 %all-to-all-done.1 = f32[128,8,128]{2,1,0:T(8,128)S(1)} async-done(((f32[128,8,128]{2,1,0:T(8,128)}), f32[128,8,128]{2,1,0:T(8,128)S(1)}, u32[]{:S(2)}, u32[]{:S(2)}) %all-to-all-start.1) | async-done | bytes 524320 | tf_op jit(solution)/shard_map/all_to_all | solution.py:313
  121.1 0.6 reshape.77
  121.7 0.6 copy.23
  122.3 0.2 reshape_reshape.3
  122.5 1.1 convolution_bitcast_fusion
  123.6 0.2 add_bitcast_fusion
  123.8 1.0 fusion.6
  124.8 0.3 fusion.13
  125.2 1.9 %copy.18 = f32[16,64,64]{0,2,1:T(8,128)S(1)} copy(f32[16,64,64]{1,2,0:T(8,128)S(1)} %fusion.13) | data formatting | bytes 524288 | tf_op jit(solution)/shard_map/transpose | solution.py:250
  127.0 0.0 copy-start
  127.1 1.4 %copy.20 = f32[16,4096]{1,0:T(8,128)} copy(f32[16,4096]{0,1:T(8,128)S(1)} %bitcast.55) | data formatting | bytes 524288
  128.4 0.0 copy-done
  128.4 6.3 %shard_map.70 = f32[16,512]{1,0:T(8,128)} custom-call(f32[4096,16]{1,0:T(8,128)} %bitcast.56, s32[8,512,1]{2,1,0:T(8,128)} %copy.19.offset_ref), custom_call_target="tpu_custom_call" | custom-call | tf_op jit(solution)/shard_map/pallas_call | solution.py:256
  (4 shorter events, 0.1 us)
Async XLA Ops:
  1.9 6.4 %collective-permute-start = (bf16[256,256]{0,1:T(8,128)(2,1)S(1)}, bf16[256,256]{0,1:T(8,128)(2,1)S(1)}, u32[]{:S(2)}, u32[]{:S(2)}) collective-permute-start(bf16[256,256]{0,1:T(8,128)(2,1)S(1)} %slice.80), channel_id=1, source_target_pairs={{0,1},{1,2},{2,3},{3,4},{4,5},{5,6},{6,7},{8,9},{9,10},{10,11},{11... | collective-permute-start | bytes 393224 | tf_op jit(solution)/shard_map/ppermute | solution.py:273
  30.2 37.8 %all-to-all-start = ((f32[16,256,128]{2,1,0:T(8,128)}), f32[16,256,128]{2,1,0:T(8,128)S(1)}, u32[]{:S(2)}, u32[]{:S(2)}) async-start(f32[16,256,128]{2,1,0:T(8,128)} %shard_map.68), calls=%async_computation | async-start | bytes 4194304 | tf_op jit(solution)/shard_map/all_to_all | solution.py:295
  68.0 1.3 copy-start.1
  69.3 38.0 %copy-start.2 = (s32[8,512]{1,0:T(8,128)S(1)}, s32[8,512]{1,0:T(8,128)}, u32[]{:S(2)}) copy-start(s32[8,512]{1,0:T(8,128)} %param.9) | copy-start | bytes 49156
  101.2 19.8 %all-to-all-start.1 = ((f32[128,8,128]{2,1,0:T(8,128)}), f32[128,8,128]{2,1,0:T(8,128)S(1)}, u32[]{:S(2)}, u32[]{:S(2)}) async-start(f32[128,8,128]{2,1,0:T(8,128)} %bitcast.61), calls=%async_computation.1 | async-start | bytes 1048576 | tf_op jit(solution)/shard_map/all_to_all | solution.py:313
  127.0 1.4 %copy-start = (f32[16,64,64]{0,2,1:T(8,128)}, f32[16,64,64]{0,2,1:T(8,128)S(1)}, u32[]{:S(2)}) copy-start(f32[16,64,64]{0,2,1:T(8,128)S(1)} %copy.18) | copy-start | bytes 786436

commit v11 on v10

--- a/solution.py
+++ b/solution.py
@@ -15,7 +15,7 @@
 HARM = 8
 RAW_HALO = 256
 SUB_HALO = 64
-TILE = 512
+TILE = 1024
 LANES = 128
 PIECES = 2
 
@@ -60,6 +60,7 @@
         target = out_ref if step == count - 1 else (buf_a, buf_b)[step % 2]
         group = 2 if bands_out >= 2 else 1
         lanes = group * width
+        tile_rows = min(TILE, row_out)
         for first_band in range(0, bands_out, group):
             for member in range(group):
                 band = first_band + member
@@ -69,9 +70,9 @@
                         parts[side, piece, pl.ds(0, depth), pl.ds(member * width, width)] = value
 
             def tile(index, carry, target=target, first_band=first_band, depth=depth,
-                     row_out=row_out, group=group, lanes=lanes,
+                     row_out=row_out, group=group, lanes=lanes, tile_rows=tile_rows,
                      pick_low=pick_low, pick_high=pick_high, delay=delay):
-                rows = pl.ds(pl.multiple_of(index * TILE, TILE), TILE)
+                rows = pl.ds(pl.multiple_of(index * tile_rows, tile_rows), tile_rows)
                 low_sel = pick_low[rows, :]
                 high_sel = pick_high[rows, :]
                 lower = None
@@ -89,20 +90,20 @@
                 merged = lower + upper
                 if target is out_ref:
                     pack[...] = merged
-                    even = pack[pl.ds(0, TILE // 2, stride=2), :]
-                    odd = pack[pl.ds(1, TILE // 2, stride=2), :]
+                    even = pack[pl.ds(0, tile_rows // 2, stride=2), :]
+                    odd = pack[pl.ds(1, tile_rows // 2, stride=2), :]
                     lane = lax.broadcasted_iota(jnp.int32, even.shape, 1)
-                    start = pl.multiple_of(index * (TILE // 2), TILE // 2)
-                    target[pl.ds(start, TILE // 2), :] = jnp.where(
+                    start = pl.multiple_of(index * (tile_rows // 2), tile_rows // 2)
+                    target[pl.ds(start, tile_rows // 2), :] = jnp.where(
                         lane < SUB_HALO, pltpu.roll(even, SUB_HALO, 1), odd
                     )
                     return carry
                 for member in range(group):
-                    start = pl.multiple_of((first_band + member) * row_out + index * TILE, TILE)
-                    target[pl.ds(start, TILE), :] = merged[:, member * width : (member + 1) * width]
+                    start = pl.multiple_of((first_band + member) * row_out + index * tile_rows, tile_rows)
+                    target[pl.ds(start, tile_rows), :] = merged[:, member * width : (member + 1) * width]
                 return carry
 
-            lax.fori_loop(0, row_out // TILE, tile, 0)
+            lax.fori_loop(0, row_out // tile_rows, tile, 0)
         source = target
 
 
@@ -126,7 +127,7 @@
             pltpu.VMEM((buf_rows, width), jnp.float32),
             pltpu.VMEM((buf_rows, width), jnp.float32),
             pltpu.VMEM((2, PIECES, depth_most, 2 * width), jnp.bfloat16),
-            pltpu.VMEM((TILE, width), jnp.float32),
+            pltpu.VMEM((min(TILE, plan[-1][1]), width), jnp.float32),
         ],
         compiler_params=pltpu.CompilerParams(vmem_limit_bytes=60 * 1024 * 1024),
     )(state, *tables)
@@ -170,7 +171,7 @@
                 target[row] = merged
             return carry
 
-        lax.fori_loop(0, row_out, body, 0, unroll=min(row_out, 8))
+        lax.fori_loop(0, row_out, body, 0, unroll=min(row_out, 16))
         source = target
     for dest in range(out_ref.shape[0]):
         start = base + sub * dest

time: 136 us -> 131 us (0.963)
  Pallas kernels: 52.3 us -> 47.5 us
    pallas_call x1, Pallas kernels: 31.9 us -> 29.2 us  [run_matmul_levels(): pl.pallas_call(functools.partial(matmul_kernel, plan), out_shape=jax.Shap...]
    pallas_call x1, Pallas kernels: 14.1 us -> 12 us  [run_local(): pl.pallas_call(functools.partial(local_kernel, plan, sub, base), out_shap...]
where the time goes in v11:
time: 131 us; the launch traced here: 130 us
  Pallas kernels  47.5 us (36%)
  waiting for transfers between devices  25.7 us (20%)
  local copies, waits for them, and re-layouts  21.5 us (16%)
  starting transfers between devices  18.4 us (14%)
  other arithmetic  13.9 us (11%)
  matrix products  2.13 us (2%)
    pallas_call x1, Pallas kernels, run_matmul_levels(): pl.pallas_call(functools.partial(matmul_kernel, plan), out_shape=jax.Shap...  29.2 us
    all_to_all x1, waiting for transfers between devices, on_device(): lax.all_to_all(pieces, 'chan', split_axis=0, concat_axis=0, tiled=True)  14 us
    pallas_call x1, Pallas kernels, run_local(): pl.pallas_call(functools.partial(local_kernel, plan, sub, base), out_shap...  12 us
    all_to_all x1, waiting for transfers between devices, on_device(): lax.all_to_all(outgoing, ('chan', 'tm'), split_axis=0, concat_axis=0, til...  11.1 us
    all_to_all x1, starting transfers between devices, on_device(): lax.all_to_all(pieces, 'chan', split_axis=0, concat_axis=0, tiled=True)  7.79 us
    another operation x7, local copies, waits for them, and re-layouts, run_matmul_levels(): tables.append(shifts[level, :row_out, None])  7.09 us
    convert_element_type x3, other arithmetic, run_matmul_levels(): (first_rows[level, :row_out, None] == columns).astype(jnp.bfloat16)  6.63 us
    pallas_call x1, Pallas kernels, spectra(): pl.pallas_call(harmonic_kernel, out_shape=jax.ShapeDtypeStruct((count, fu...  6.29 us
  transfers between devices with their start and end apart: 3, of which 3 were waited for; matrix products, arithmetic and copies ran while one was open for 15% of the time, Pallas kernels for 0%

profile of v11, /device:TPU:1, one launch (start us, length us, event | category | flops | bytes accessed | tf_op | source)
XLA Modules:
  0.0 129.9 jit_solution(12969194767095742997)
XLA Ops:
  0.6 1.2 copy.10
  1.9 4.5 %collective-permute-start = (bf16[256,256]{0,1:T(8,128)(2,1)S(1)}, bf16[256,256]{0,1:T(8,128)(2,1)S(1)}, u32[]{:S(2)}, u32[]{:S(2)}) collective-permute-start(bf16[256,256]{0,1:T(8,128)(2,1)S(1)} %slice.80), channel_id=1, source_target_pairs={{0,1},{1,2},{2,3},{3,4},{4,5},{5,6},{6,7},{8,9},{9,10},{10,11},{11... | collective-permute-start | bytes 393224 | tf_op jit(solution)/shard_map/ppermute | solution.py:274
  6.4 1.3 %pad_add_fusion.table_ref = s32[3,8,256]{2,1,0:T(8,128)} fusion(s32[1,12,2048]{2,1,0:T(8,128)} %bitcast.63, s32[1,12,2048]{2,1,0:T(8,128)} %bitcast.64, s32[1,12,2048]{2,1,0:T(8,128)} %bitcast.62), kind=kLoop, calls=%fused_computation.68 | loop fusion | flops 12288 | bytes 319488 | tf_op jit(solution)/shard_map/stack | solution.py:286
  7.8 0.6 collective-permute-done
  8.4 1.3 %copy.12 = f32[256,10,128]{2,0,1:T(8,128)} copy(bf16[256,10,128]{0,2,1:T(8,128)(2,1)S(1)} %bitcast.60) | data formatting | bytes 1966080 | tf_op jit(solution)/shard_map/broadcast_in_dim | solution.py:285
  9.7 12.0 %shard_map.68 = f32[16,256,128]{2,1,0:T(8,128)} custom-call(s32[3,8,256]{2,1,0:T(8,128)} %pad_add_fusion.table_ref, f32[1,10,256,128]{3,2,1,0:T(8,128)} %bitcast.58), custom_call_target="tpu_custom_call" | custom-call | tf_op jit(solution)/shard_map/pallas_call | solution.py:195
  21.7 0.7 slice.62
  22.4 0.8 slice.65
  23.2 0.7 slice.63
  23.9 0.8 slice.66
  24.7 0.7 slice_bitcast_fusion.3
  25.4 0.8 slice_bitcast_fusion.2
  26.1 0.9 fusion.48
  27.1 1.0 slice_bitcast_fusion
  28.1 7.8 %all-to-all-start = ((f32[16,256,128]{2,1,0:T(8,128)}), f32[16,256,128]{2,1,0:T(8,128)S(1)}, u32[]{:S(2)}, u32[]{:S(2)}) async-start(f32[16,256,128]{2,1,0:T(8,128)} %shard_map.68), calls=%async_computation | async-start | bytes 4194304 | tf_op jit(solution)/shard_map/all_to_all | solution.py:296
  35.8 0.9 copy.13.refs_2_
  36.7 1.0 copy.14.refs_5_
  37.7 1.4 %copy.15.refs_8_ = s32[2048,1]{1,0:T(8,128)} copy(s32[2048,1]{0,1:T(1,128)S(1)} %get-tuple-element.17) | data formatting | bytes 16384 | tf_op jit(solution)/shard_map/broadcast_in_dim;squeeze | solution.py:117
  39.1 1.4 %copy.16.refs_11_ = s32[2048,1]{1,0:T(8,128)} copy(s32[2048,1]{0,1:T(1,128)S(1)} %get-tuple-element.16) | data formatting | bytes 16384 | tf_op jit(solution)/shard_map/broadcast_in_dim;squeeze | solution.py:117
  40.5 1.7 %fusion.4 = (bf16[1024,512]{1,0:T(8,128)(2,1)}, bf16[1024,512]{1,0:T(8,128)(2,1)}) fusion(s32[1024]{0:T(1024)S(1)} %bitcast.69, s32[1024]{0:T(1024)S(1)} %bitcast.70), kind=kLoop, calls=%fused_computation.10 | loop fusion | flops 2097152 | bytes 2105344 | tf_op jit(solution)/shard_map/convert_element_type | solution.py:115
  42.2 1.0 fusion.15
  43.2 2.4 %fusion.1.refs_7_ = bf16[2048,1024]{1,0:T(8,128)(2,1)} fusion(s32[2048]{0:T(1024)S(1)} %bitcast.66), kind=kLoop, calls=%fused_computation.5 | loop fusion | flops 4194304 | bytes 4202496 | tf_op jit(solution)/shard_map/convert_element_type | solution.py:116
  45.5 2.3 %fusion.3.refs_10_ = bf16[2048,1024]{1,0:T(8,128)(2,1)} fusion(s32[2048]{0:T(1024)S(1)} %bitcast.65), kind=kLoop, calls=%fused_computation.7 | loop fusion | flops 4194304 | bytes 4202496 | tf_op jit(solution)/shard_map/convert_element_type | solution.py:116
  47.9 4.0 %fusion = (bf16[2048,1024]{1,0:T(8,128)(2,1)}, bf16[2048,1024]{1,0:T(8,128)(2,1)}) fusion(s32[2048]{0:T(1024)S(1)} %bitcast.68, s32[2048]{0:T(1024)S(1)} %bitcast.67), kind=kLoop, calls=%fused_computation.4 | loop fusion | flops 8388608 | bytes 8404992 | tf_op jit(solution)/shard_map/convert_element_type | solution.py:115
  51.8 14.0 %all-to-all-done = f32[16,256,128]{2,1,0:T(8,128)S(1)} async-done(((f32[16,256,128]{2,1,0:T(8,128)}), f32[16,256,128]{2,1,0:T(8,128)S(1)}, u32[]{:S(2)}, u32[]{:S(2)}) %all-to-all-start) | async-done | bytes 2097184 | tf_op jit(solution)/shard_map/all_to_all | solution.py:296
  65.9 0.0 copy-start.1
  65.9 1.3 %copy-done.1 = f32[16,256,128]{2,1,0:T(8,128)} copy-done((f32[16,256,128]{2,1,0:T(8,128)}, f32[16,256,128]{2,1,0:T(8,128)S(1)}, u32[]{:S(2)}) %copy-start.1) | copy-done | bytes 2097176
  67.2 29.2 %shard_map.69 = f32[1024,128]{1,0:T(8,128)} custom-call(f32[4096,128]{1,0:T(8,128)} %bitcast.57, bf16[512,256]{1,0:T(8,128)(2,1)} %get-tuple-element.28.refs_0_, bf16[512,256]{1,0:T(8,128)(2,1)} %get-tuple-element.29.refs_1_, s32[512,1]{1,0:T(8,128)} %copy.13.refs_2_, bf16[1024,512]{1,0:T(8,128)(2,1)} %get-tuple-element.26.refs_3_, ...), custom_call_target="tpu_custom_call" | custom-call | tf_op jit(solution)/shard_map/pallas_call | solution.py:121
  96.4 6.1 %all-to-all-start.1 = ((f32[128,8,128]{2,1,0:T(8,128)}), f32[128,8,128]{2,1,0:T(8,128)S(1)}, u32[]{:S(2)}, u32[]{:S(2)}) async-start(f32[128,8,128]{2,1,0:T(8,128)} %bitcast.61), calls=%async_computation.1 | async-start | bytes 1048576 | tf_op jit(solution)/shard_map/all_to_all | solution.py:314
  102.5 0.0 copy-done.2
  102.5 0.1 subtract_bitcast_fusion.1
  102.6 2.0 %copy.19.offset_ref = s32[8,512,1]{2,1,0:T(8,128)} copy(s32[8,512,1]{1,0,2:T(8,128)S(1)} %subtract_bitcast_fusion.1) | data formatting | bytes 32768 | tf_op jit(solution)/shard_map/broadcast_in_dim | solution.py:255
  104.6 0.1 fusion.43
  104.7 0.1 fusion.41
  104.9 0.3 fusion.33
  105.2 11.1 %all-to-all-done.1 = f32[128,8,128]{2,1,0:T(8,128)S(1)} async-done(((f32[128,8,128]{2,1,0:T(8,128)}), f32[128,8,128]{2,1,0:T(8,128)S(1)}, u32[]{:S(2)}, u32[]{:S(2)}) %all-to-all-start.1) | async-done | bytes 524320 | tf_op jit(solution)/shard_map/all_to_all | solution.py:314
  116.2 0.6 reshape.77
  116.9 0.6 copy.23
  117.5 0.2 reshape_reshape.3
  117.7 1.1 convolution_bitcast_fusion
  118.8 0.2 add_bitcast_fusion
  118.9 1.0 fusion.6
  120.0 0.3 fusion.13
  120.3 1.9 %copy.18 = f32[16,64,64]{0,2,1:T(8,128)S(1)} copy(f32[16,64,64]{1,2,0:T(8,128)S(1)} %fusion.13) | data formatting | bytes 524288 | tf_op jit(solution)/shard_map/transpose | solution.py:251
  122.2 0.0 copy-start
  122.2 1.4 %copy.20 = f32[16,4096]{1,0:T(8,128)} copy(f32[16,4096]{0,1:T(8,128)S(1)} %bitcast.55) | data formatting | bytes 524288
  123.6 0.0 copy-done
  123.6 6.3 %shard_map.70 = f32[16,512]{1,0:T(8,128)} custom-call(f32[4096,16]{1,0:T(8,128)} %bitcast.56, s32[8,512,1]{2,1,0:T(8,128)} %copy.19.offset_ref), custom_call_target="tpu_custom_call" | custom-call | tf_op jit(solution)/shard_map/pallas_call | solution.py:257
  (4 shorter events, 0.1 us)
Async XLA Ops:
  1.9 6.4 %collective-permute-start = (bf16[256,256]{0,1:T(8,128)(2,1)S(1)}, bf16[256,256]{0,1:T(8,128)(2,1)S(1)}, u32[]{:S(2)}, u32[]{:S(2)}) collective-permute-start(bf16[256,256]{0,1:T(8,128)(2,1)S(1)} %slice.80), channel_id=1, source_target_pairs={{0,1},{1,2},{2,3},{3,4},{4,5},{5,6},{6,7},{8,9},{9,10},{10,11},{11... | collective-permute-start | bytes 393224 | tf_op jit(solution)/shard_map/ppermute | solution.py:274
  28.1 37.8 %all-to-all-start = ((f32[16,256,128]{2,1,0:T(8,128)}), f32[16,256,128]{2,1,0:T(8,128)S(1)}, u32[]{:S(2)}, u32[]{:S(2)}) async-start(f32[16,256,128]{2,1,0:T(8,128)} %shard_map.68), calls=%async_computation | async-start | bytes 4194304 | tf_op jit(solution)/shard_map/all_to_all | solution.py:296
  65.9 1.3 %copy-start.1 = (f32[16,256,128]{2,1,0:T(8,128)}, f32[16,256,128]{2,1,0:T(8,128)S(1)}, u32[]{:S(2)}) copy-start(f32[16,256,128]{2,1,0:T(8,128)S(1)} %all-to-all-done) | copy-start | bytes 6291460
  67.2 35.3 %copy-start.2 = (s32[8,512]{1,0:T(8,128)S(1)}, s32[8,512]{1,0:T(8,128)}, u32[]{:S(2)}) copy-start(s32[8,512]{1,0:T(8,128)} %param.9) | copy-start | bytes 49156
  96.4 19.8 %all-to-all-start.1 = ((f32[128,8,128]{2,1,0:T(8,128)}), f32[128,8,128]{2,1,0:T(8,128)S(1)}, u32[]{:S(2)}, u32[]{:S(2)}) async-start(f32[128,8,128]{2,1,0:T(8,128)} %bitcast.61), calls=%async_computation.1 | async-start | bytes 1048576 | tf_op jit(solution)/shard_map/all_to_all | solution.py:314
  122.2 1.4 %copy-start = (f32[16,64,64]{0,2,1:T(8,128)}, f32[16,64,64]{0,2,1:T(8,128)S(1)}, u32[]{:S(2)}) copy-start(f32[16,64,64]{0,2,1:T(8,128)S(1)} %copy.18) | copy-start | bytes 786436

commit v12 on v11

--- a/solution.py
+++ b/solution.py
@@ -289,9 +289,8 @@
         sub,
         RAW_HALO - SUB_HALO,
     )
-    pieces, first_rows, second_rows, shifts = lax.optimization_barrier(
-        (pieces, first_rows, second_rows, shifts)
-    )
+    cross_tables = jnp.stack([first_rows, second_rows, shifts])[:, local_levels:]
+    pieces, cross_tables = lax.optimization_barrier((pieces, cross_tables))
     window = sub + SUB_HALO
     layers = lax.all_to_all(pieces, "chan", split_axis=0, concat_axis=0, tiled=True)
     cross_plan = []
@@ -302,10 +301,10 @@
         cross_plan.append((rows_in, min(2 ** (level + 1), NDM), bands, min(rows_in, NDM // 2)))
     plane = run_matmul_levels(
         layers.reshape(chan_count * channels, window),
-        first_rows,
-        second_rows,
-        shifts,
-        list(range(local_levels, levels)),
+        cross_tables[0],
+        cross_tables[1],
+        cross_tables[2],
+        list(range(levels - local_levels)),
         cross_plan,
     )
     groups = chan_count * tm_count

time: 131 us -> 125 us (0.954)
  local copies, waits for them, and re-layouts: 21.5 us -> 15.3 us
    convert_element_type x2 -> x0, other arithmetic: 4.72 us -> none  [run_matmul_levels(): (second_rows[level, :row_out, None] == columns).astype(jnp.bfloat16)]
    convert_element_type x3 -> x4, other arithmetic: 6.63 us -> 10.6 us  [run_matmul_levels(): (first_rows[level, :row_out, None] == columns).astype(jnp.bfloat16)]
    slice x3 -> x2, local copies, waits for them, and re-layouts: 2.41 us -> 0.01 us  [run_matmul_levels(): first_rows[level, :row_out, None] == columns]
    another operation x7, local copies, waits for them, and re-layouts: 7.09 us -> 4.7 us  [run_matmul_levels(): tables.append(shifts[level, :row_out, None])]
    slice x2, local copies, waits for them, and re-layouts: 1.48 us -> 0.01 us  [run_matmul_levels(): second_rows[level, :row_out, None] == columns]
    slice x0 -> x1, other arithmetic: none -> 1.34 us  [on_device(): jnp.stack([first_rows, second_rows, shifts])[:, :local_levels, :channels]]
  transfers between devices with their start and end apart: 3 -> 3, of which waited for: 3 -> 2; matrix products, arithmetic and copies ran while one was open for 15% -> 16% of each run, Pallas kernels for 0% -> 0%
where the time goes in v12:
time: 125 us; the launch traced here: 124 us
  Pallas kernels  47.5 us (38%)
  waiting for transfers between devices  25.3 us (20%)
  starting transfers between devices  19.1 us (15%)
  local copies, waits for them, and re-layouts  15.3 us (12%)
  other arithmetic  14.1 us (11%)
  matrix products  2.13 us (2%)
    pallas_call x1, Pallas kernels, run_matmul_levels(): pl.pallas_call(functools.partial(matmul_kernel, plan), out_shape=jax.Shap...  29.2 us
    all_to_all x1, waiting for transfers between devices, on_device(): lax.all_to_all(pieces, 'chan', split_axis=0, concat_axis=0, tiled=True)  14.2 us
    pallas_call x1, Pallas kernels, run_local(): pl.pallas_call(functools.partial(local_kernel, plan, sub, base), out_shap...  12 us
    all_to_all x1, waiting for transfers between devices, on_device(): lax.all_to_all(outgoing, ('chan', 'tm'), split_axis=0, concat_axis=0, til...  11.1 us
    convert_element_type x4, other arithmetic, run_matmul_levels(): (first_rows[level, :row_out, None] == columns).astype(jnp.bfloat16)  10.6 us
    all_to_all x1, starting transfers between devices, on_device(): lax.all_to_all(pieces, 'chan', split_axis=0, concat_axis=0, tiled=True)  7.79 us
    all_to_all x1, starting transfers between devices, on_device(): lax.all_to_all(outgoing, ('chan', 'tm'), split_axis=0, concat_axis=0, til...  6.85 us
    pallas_call x1, Pallas kernels, spectra(): pl.pallas_call(harmonic_kernel, out_shape=jax.ShapeDtypeStruct((count, fu...  6.29 us
  transfers between devices with their start and end apart: 3, of which 2 were waited for; matrix products, arithmetic and copies ran while one was open for 16% of the time, Pallas kernels for 0%

profile of v12, /device:TPU:1, one launch (start us, length us, event | category | flops | bytes accessed | tf_op | source)
XLA Modules:
  0.0 124.3 jit_solution(7926346822797933556)
XLA Ops:
  0.6 1.2 %copy.10 = bf16[256,1024]{0,1:T(8,128)(2,1)S(1)} copy(bf16[256,1024]{1,0:T(8,128)(2,1)} %param.5) | data formatting | bytes 1048576 | tf_op args[0]
  1.9 4.5 %collective-permute-start = (bf16[256,256]{0,1:T(8,128)(2,1)S(1)}, bf16[256,256]{0,1:T(8,128)(2,1)S(1)}, u32[]{:S(2)}, u32[]{:S(2)}) collective-permute-start(bf16[256,256]{0,1:T(8,128)(2,1)S(1)} %slice.108), channel_id=1, source_target_pairs={{0,1},{1,2},{2,3},{3,4},{4,5},{5,6},{6,7},{8,9},{9,10},{10,11},{11... | collective-permute-start | bytes 393224 | tf_op jit(solution)/shard_map/ppermute | solution.py:274
  6.4 0.9 pad_add_fusion
  7.4 1.3 %pad_add_fusion.2.table_ref = s32[3,8,256]{2,1,0:T(8,128)} fusion(s32[1,12,2048]{2,1,0:T(8,128)} %bitcast.69, s32[1,12,2048]{2,1,0:T(8,128)} %bitcast.71, s32[1,12,2048]{2,1,0:T(8,128)} %bitcast.73), kind=kLoop, calls=%fused_computation.73 | loop fusion | flops 12288 | bytes 319488 | tf_op jit(solution)/shard_map/slice | solution.py:286
  8.7 0.0 collective-permute-done
  8.7 1.3 %copy.12 = f32[256,10,128]{2,0,1:T(8,128)} copy(bf16[256,10,128]{0,2,1:T(8,128)(2,1)S(1)} %bitcast.66) | data formatting | bytes 1966080 | tf_op jit(solution)/shard_map/broadcast_in_dim | solution.py:285
  10.1 12.0 %shard_map.68 = f32[16,256,128]{2,1,0:T(8,128)} custom-call(s32[3,8,256]{2,1,0:T(8,128)} %pad_add_fusion.2.table_ref, f32[1,10,256,128]{3,2,1,0:T(8,128)} %bitcast.64), custom_call_target="tpu_custom_call" | custom-call | tf_op jit(solution)/shard_map/pallas_call | solution.py:195
  22.2 7.8 %all-to-all-start = ((f32[16,256,128]{2,1,0:T(8,128)}), f32[16,256,128]{2,1,0:T(8,128)S(1)}, u32[]{:S(2)}, u32[]{:S(2)}) async-start(f32[16,256,128]{2,1,0:T(8,128)} %shard_map.68), calls=%async_computation | async-start | bytes 4194304 | tf_op jit(solution)/shard_map/all_to_all | solution.py:295
  30.0 0.9 copy.13.refs_2_
  30.9 1.0 copy.14.refs_5_
  31.9 1.4 %copy.15.refs_8_ = s32[2048,1]{1,0:T(8,128)} copy(s32[2048,1]{0,1:T(1,128)S(1)} %get-tuple-element.15) | data formatting | bytes 16384 | tf_op jit(solution)/shard_map/broadcast_in_dim;squeeze | solution.py:117
  33.3 1.4 %copy.16.refs_11_ = s32[2048,1]{1,0:T(8,128)} copy(s32[2048,1]{0,1:T(1,128)S(1)} %get-tuple-element.12) | data formatting | bytes 16384 | tf_op jit(solution)/shard_map/broadcast_in_dim;squeeze | solution.py:117
  34.7 1.0 fusion.15
  35.6 1.7 %fusion.4 = (bf16[1024,512]{1,0:T(8,128)(2,1)}, bf16[1024,512]{1,0:T(8,128)(2,1)}) fusion(s32[1024]{0:T(1024)S(1)} %bitcast.78, s32[1024]{0:T(1024)S(1)} %bitcast.79), kind=kLoop, calls=%fused_computation.10 | loop fusion | flops 2097152 | bytes 2105344 | tf_op jit(solution)/shard_map/convert_element_type | solution.py:115
  37.3 4.0 %fusion = (bf16[2048,1024]{1,0:T(8,128)(2,1)}, bf16[2048,1024]{1,0:T(8,128)(2,1)}) fusion(s32[2048]{0:T(1024)S(1)} %bitcast.77, s32[2048]{0:T(1024)S(1)} %bitcast.76), kind=kLoop, calls=%fused_computation.4 | loop fusion | flops 8388608 | bytes 8404992 | tf_op jit(solution)/shard_map/convert_element_type | solution.py:115
  41.3 4.0 %fusion.2 = (bf16[2048,1024]{1,0:T(8,128)(2,1)}, bf16[2048,1024]{1,0:T(8,128)(2,1)}) fusion(s32[2048]{0:T(1024)S(1)} %bitcast.75, s32[2048]{0:T(1024)S(1)} %bitcast.74), kind=kLoop, calls=%fused_computation.6 | loop fusion | flops 8388608 | bytes 8404992 | tf_op jit(solution)/shard_map/convert_element_type | solution.py:115
  45.3 14.2 %all-to-all-done = f32[16,256,128]{2,1,0:T(8,128)S(1)} async-done(((f32[16,256,128]{2,1,0:T(8,128)}), f32[16,256,128]{2,1,0:T(8,128)S(1)}, u32[]{:S(2)}, u32[]{:S(2)}) %all-to-all-start) | async-done | bytes 2097184 | tf_op jit(solution)/shard_map/all_to_all | solution.py:295
  59.5 0.0 copy-start.1
  59.5 1.3 %copy-done.1 = f32[16,256,128]{2,1,0:T(8,128)} copy-done((f32[16,256,128]{2,1,0:T(8,128)}, f32[16,256,128]{2,1,0:T(8,128)S(1)}, u32[]{:S(2)}) %copy-start.1) | copy-done | bytes 2097176
  60.8 0.0 copy-start.2
  60.8 29.2 %shard_map.69 = f32[1024,128]{1,0:T(8,128)} custom-call(f32[4096,128]{1,0:T(8,128)} %bitcast.63, bf16[512,256]{1,0:T(8,128)(2,1)} %get-tuple-element.27.refs_0_, bf16[512,256]{1,0:T(8,128)(2,1)} %get-tuple-element.28.refs_1_, s32[512,1]{1,0:T(8,128)} %copy.13.refs_2_, bf16[1024,512]{1,0:T(8,128)(2,1)} %get-tuple-element.25.refs_3_, ...), custom_call_target="tpu_custom_call" | custom-call | tf_op jit(solution)/shard_map/pallas_call | solution.py:121
  90.1 6.8 %all-to-all-start.1 = ((f32[128,8,128]{2,1,0:T(8,128)}), f32[128,8,128]{2,1,0:T(8,128)S(1)}, u32[]{:S(2)}, u32[]{:S(2)}) async-start(f32[128,8,128]{2,1,0:T(8,128)} %bitcast.67), calls=%async_computation.1 | async-start | bytes 1048576 | tf_op jit(solution)/shard_map/all_to_all | solution.py:313
  96.9 0.0 copy-done.2
  96.9 0.1 subtract_bitcast_fusion.1
  97.0 2.0 %copy.19.offset_ref = s32[8,512,1]{2,1,0:T(8,128)} copy(s32[8,512,1]{1,0,2:T(8,128)S(1)} %subtract_bitcast_fusion.1) | data formatting | bytes 32768 | tf_op jit(solution)/shard_map/broadcast_in_dim | solution.py:255
  99.0 0.1 fusion.43
  99.1 0.1 fusion.41
  99.3 0.3 fusion.33
  99.6 11.1 %all-to-all-done.1 = f32[128,8,128]{2,1,0:T(8,128)S(1)} async-done(((f32[128,8,128]{2,1,0:T(8,128)}), f32[128,8,128]{2,1,0:T(8,128)S(1)}, u32[]{:S(2)}, u32[]{:S(2)}) %all-to-all-start.1) | async-done | bytes 524320 | tf_op jit(solution)/shard_map/all_to_all | solution.py:313
  110.6 0.6 reshape.89
  111.2 0.6 copy.23
  111.9 0.2 reshape_reshape.3
  112.1 1.1 convolution_bitcast_fusion
  113.2 0.2 add_bitcast_fusion
  113.3 1.0 fusion.6
  114.4 0.3 fusion.13
  114.7 1.9 %copy.18 = f32[16,64,64]{0,2,1:T(8,128)S(1)} copy(f32[16,64,64]{1,2,0:T(8,128)S(1)} %fusion.13) | data formatting | bytes 524288 | tf_op jit(solution)/shard_map/transpose | solution.py:251
  116.6 0.0 copy-start
  116.7 1.4 %copy.20 = f32[16,4096]{1,0:T(8,128)} copy(f32[16,4096]{0,1:T(8,128)S(1)} %bitcast.61) | data formatting | bytes 524288
  118.0 0.0 copy-done
  118.0 6.3 %shard_map.70 = f32[16,512]{1,0:T(8,128)} custom-call(f32[4096,16]{1,0:T(8,128)} %bitcast.62, s32[8,512,1]{2,1,0:T(8,128)} %copy.19.offset_ref), custom_call_target="tpu_custom_call" | custom-call | tf_op jit(solution)/shard_map/pallas_call | solution.py:257
  (11 shorter events, 0.1 us)
Async XLA Ops:
  1.9 6.8 %collective-permute-start = (bf16[256,256]{0,1:T(8,128)(2,1)S(1)}, bf16[256,256]{0,1:T(8,128)(2,1)S(1)}, u32[]{:S(2)}, u32[]{:S(2)}) collective-permute-start(bf16[256,256]{0,1:T(8,128)(2,1)S(1)} %slice.108), channel_id=1, source_target_pairs={{0,1},{1,2},{2,3},{3,4},{4,5},{5,6},{6,7},{8,9},{9,10},{10,11},{11... | collective-permute-start | bytes 393224 | tf_op jit(solution)/shard_map/ppermute | solution.py:274
  22.2 37.3 %all-to-all-start = ((f32[16,256,128]{2,1,0:T(8,128)}), f32[16,256,128]{2,1,0:T(8,128)S(1)}, u32[]{:S(2)}, u32[]{:S(2)}) async-start(f32[16,256,128]{2,1,0:T(8,128)} %shard_map.68), calls=%async_computation | async-start | bytes 4194304 | tf_op jit(solution)/shard_map/all_to_all | solution.py:295
  59.5 1.3 %copy-start.1 = (f32[16,256,128]{2,1,0:T(8,128)}, f32[16,256,128]{2,1,0:T(8,128)S(1)}, u32[]{:S(2)}) copy-start(f32[16,256,128]{2,1,0:T(8,128)S(1)} %all-to-all-done) | copy-start | bytes 6291460
  60.8 36.1 %copy-start.2 = (s32[8,512]{1,0:T(8,128)S(1)}, s32[8,512]{1,0:T(8,128)}, u32[]{:S(2)}) copy-start(s32[8,512]{1,0:T(8,128)} %param.9) | copy-start | bytes 49156
  90.1 20.6 %all-to-all-start.1 = ((f32[128,8,128]{2,1,0:T(8,128)}), f32[128,8,128]{2,1,0:T(8,128)S(1)}, u32[]{:S(2)}, u32[]{:S(2)}) async-start(f32[128,8,128]{2,1,0:T(8,128)} %bitcast.67), calls=%async_computation.1 | async-start | bytes 1048576 | tf_op jit(solution)/shard_map/all_to_all | solution.py:313
  116.6 1.4 %copy-start = (f32[16,64,64]{0,2,1:T(8,128)}, f32[16,64,64]{0,2,1:T(8,128)S(1)}, u32[]{:S(2)}) copy-start(f32[16,64,64]{0,2,1:T(8,128)S(1)} %copy.18) | copy-start | bytes 786436

commit v13 on v12

--- a/solution.py
+++ b/solution.py
@@ -133,8 +133,9 @@
     )(state, *tables)
 
 
-def harmonic_kernel(power_ref, offset_ref, out_ref):
+def harmonic_kernel(spectrum_ref, offset_ref, out_ref, power_ref):
     fundamentals = out_ref.shape[1]
+    power_ref[...] = jnp.transpose(spectrum_ref[...])
     total = None
     for order in range(HARM):
         stride = order + 1
@@ -259,7 +260,8 @@
         out_shape=jax.ShapeDtypeStruct((count, fundamentals), jnp.float32),
         in_specs=[vmem, vmem],
         out_specs=vmem,
-    )(jnp.transpose(spectrum_power), offsets)
+        scratch_shapes=[pltpu.VMEM((total // 2, count), jnp.float32)],
+    )(spectrum_power, offsets)
     return spectrum_power, harmonic
 
 

time: 125 us -> 123 us (0.984)
  local copies, waits for them, and re-layouts: 15.3 us -> 13.1 us
    transpose x1, local copies, waits for them, and re-layouts: 1.89 us -> 0.2 us  [spectra(): jnp.transpose(spectrum_power, (0, 2, 1)).reshape(count, total // 2)]
    unnamed x8 -> x5, local copies, waits for them, and re-layouts: 3.99 us -> 2.57 us
where the time goes in v13:
time: 123 us; the launch traced here: 122 us
  Pallas kernels  47.8 us (39%)
  waiting for transfers between devices  25.3 us (21%)
  starting transfers between devices  19.1 us (16%)
  other arithmetic  14.1 us (11%)
  local copies, waits for them, and re-layouts  13.1 us (11%)
  matrix products  2.13 us (2%)
    pallas_call x1, Pallas kernels, run_matmul_levels(): pl.pallas_call(functools.partial(matmul_kernel, plan), out_shape=jax.Shap...  29.2 us
    all_to_all x1, waiting for transfers between devices, on_device(): lax.all_to_all(pieces, 'chan', split_axis=0, concat_axis=0, tiled=True)  14.2 us
    pallas_call x1, Pallas kernels, run_local(): pl.pallas_call(functools.partial(local_kernel, plan, sub, base), out_shap...  12 us
    all_to_all x1, waiting for transfers between devices, on_device(): lax.all_to_all(outgoing, ('chan', 'tm'), split_axis=0, concat_axis=0, til...  11.1 us
    convert_element_type x4, other arithmetic, run_matmul_levels(): (first_rows[level, :row_out, None] == columns).astype(jnp.bfloat16)  10.6 us
    all_to_all x1, starting transfers between devices, on_device(): lax.all_to_all(pieces, 'chan', split_axis=0, concat_axis=0, tiled=True)  7.79 us
    all_to_all x1, starting transfers between devices, on_device(): lax.all_to_all(outgoing, ('chan', 'tm'), split_axis=0, concat_axis=0, til...  6.84 us
    pallas_call x1, Pallas kernels, spectra(): pl.pallas_call(harmonic_kernel, out_shape=jax.ShapeDtypeStruct((count, fu...  6.55 us
  transfers between devices with their start and end apart: 3, of which 2 were waited for; matrix products, arithmetic and copies ran while one was open for 16% of the time, Pallas kernels for 0%

profile of v13, /device:TPU:1, one launch (start us, length us, event | category | flops | bytes accessed | tf_op | source)
XLA Modules:
  0.0 122.4 jit_solution(8462359391716510114)
XLA Ops:
  0.6 1.2 %copy.9 = bf16[256,1024]{0,1:T(8,128)(2,1)S(1)} copy(bf16[256,1024]{1,0:T(8,128)(2,1)} %param.5) | data formatting | bytes 1048576 | tf_op args[0]
  1.9 4.5 %collective-permute-start = (bf16[256,256]{0,1:T(8,128)(2,1)S(1)}, bf16[256,256]{0,1:T(8,128)(2,1)S(1)}, u32[]{:S(2)}, u32[]{:S(2)}) collective-permute-start(bf16[256,256]{0,1:T(8,128)(2,1)S(1)} %slice.108), channel_id=1, source_target_pairs={{0,1},{1,2},{2,3},{3,4},{4,5},{5,6},{6,7},{8,9},{9,10},{10,11},{11... | collective-permute-start | bytes 393224 | tf_op jit(solution)/shard_map/ppermute | solution.py:276
  6.4 0.9 pad_add_fusion
  7.4 1.3 %pad_add_fusion.2.table_ref = s32[3,8,256]{2,1,0:T(8,128)} fusion(s32[1,12,2048]{2,1,0:T(8,128)} %bitcast.64, s32[1,12,2048]{2,1,0:T(8,128)} %bitcast.66, s32[1,12,2048]{2,1,0:T(8,128)} %bitcast.68), kind=kLoop, calls=%fused_computation.73 | loop fusion | flops 12288 | bytes 319488 | tf_op jit(solution)/shard_map/slice | solution.py:288
  8.7 0.0 collective-permute-done
  8.7 1.3 %copy.11 = f32[256,10,128]{2,0,1:T(8,128)} copy(bf16[256,10,128]{0,2,1:T(8,128)(2,1)S(1)} %bitcast.61) | data formatting | bytes 1966080 | tf_op jit(solution)/shard_map/broadcast_in_dim | solution.py:287
  10.1 12.0 %shard_map.68 = f32[16,256,128]{2,1,0:T(8,128)} custom-call(s32[3,8,256]{2,1,0:T(8,128)} %pad_add_fusion.2.table_ref, f32[1,10,256,128]{3,2,1,0:T(8,128)} %bitcast.59), custom_call_target="tpu_custom_call" | custom-call | tf_op jit(solution)/shard_map/pallas_call | solution.py:196
  22.2 7.8 %all-to-all-start = ((f32[16,256,128]{2,1,0:T(8,128)}), f32[16,256,128]{2,1,0:T(8,128)S(1)}, u32[]{:S(2)}, u32[]{:S(2)}) async-start(f32[16,256,128]{2,1,0:T(8,128)} %shard_map.68), calls=%async_computation | async-start | bytes 4194304 | tf_op jit(solution)/shard_map/all_to_all | solution.py:297
  30.0 0.9 copy.12.refs_2_
  30.9 1.0 copy.13.refs_5_
  31.9 1.4 %copy.14.refs_8_ = s32[2048,1]{1,0:T(8,128)} copy(s32[2048,1]{0,1:T(1,128)S(1)} %get-tuple-element.11) | data formatting | bytes 16384 | tf_op jit(solution)/shard_map/broadcast_in_dim;squeeze | solution.py:117
  33.3 1.4 %copy.15.refs_11_ = s32[2048,1]{1,0:T(8,128)} copy(s32[2048,1]{0,1:T(1,128)S(1)} %get-tuple-element.8) | data formatting | bytes 16384 | tf_op jit(solution)/shard_map/broadcast_in_dim;squeeze | solution.py:117
  34.6 1.0 fusion.15
  35.6 1.7 %fusion.4 = (bf16[1024,512]{1,0:T(8,128)(2,1)}, bf16[1024,512]{1,0:T(8,128)(2,1)}) fusion(s32[1024]{0:T(1024)S(1)} %bitcast.73, s32[1024]{0:T(1024)S(1)} %bitcast.74), kind=kLoop, calls=%fused_computation.10 | loop fusion | flops 2097152 | bytes 2105344 | tf_op jit(solution)/shard_map/convert_element_type | solution.py:115
  37.3 4.0 %fusion = (bf16[2048,1024]{1,0:T(8,128)(2,1)}, bf16[2048,1024]{1,0:T(8,128)(2,1)}) fusion(s32[2048]{0:T(1024)S(1)} %bitcast.72, s32[2048]{0:T(1024)S(1)} %bitcast.71), kind=kLoop, calls=%fused_computation.4 | loop fusion | flops 8388608 | bytes 8404992 | tf_op jit(solution)/shard_map/convert_element_type | solution.py:115
  41.3 4.0 %fusion.2 = (bf16[2048,1024]{1,0:T(8,128)(2,1)}, bf16[2048,1024]{1,0:T(8,128)(2,1)}) fusion(s32[2048]{0:T(1024)S(1)} %bitcast.70, s32[2048]{0:T(1024)S(1)} %bitcast.69), kind=kLoop, calls=%fused_computation.6 | loop fusion | flops 8388608 | bytes 8404992 | tf_op jit(solution)/shard_map/convert_element_type | solution.py:115
  45.2 14.2 %all-to-all-done = f32[16,256,128]{2,1,0:T(8,128)S(1)} async-done(((f32[16,256,128]{2,1,0:T(8,128)}), f32[16,256,128]{2,1,0:T(8,128)S(1)}, u32[]{:S(2)}, u32[]{:S(2)}) %all-to-all-start) | async-done | bytes 2097184 | tf_op jit(solution)/shard_map/all_to_all | solution.py:297
  59.5 0.0 copy-start
  59.5 1.3 %copy-done = f32[16,256,128]{2,1,0:T(8,128)} copy-done((f32[16,256,128]{2,1,0:T(8,128)}, f32[16,256,128]{2,1,0:T(8,128)S(1)}, u32[]{:S(2)}) %copy-start) | copy-done | bytes 2097176
  60.8 0.0 copy-start.1
  60.8 29.2 %shard_map.69 = f32[1024,128]{1,0:T(8,128)} custom-call(f32[4096,128]{1,0:T(8,128)} %bitcast.58, bf16[512,256]{1,0:T(8,128)(2,1)} %get-tuple-element.23.refs_0_, bf16[512,256]{1,0:T(8,128)(2,1)} %get-tuple-element.24.refs_1_, s32[512,1]{1,0:T(8,128)} %copy.12.refs_2_, bf16[1024,512]{1,0:T(8,128)(2,1)} %get-tuple-element.21.refs_3_, ...), custom_call_target="tpu_custom_call" | custom-call | tf_op jit(solution)/shard_map/pallas_call | solution.py:121
  90.0 6.8 %all-to-all-start.1 = ((f32[128,8,128]{2,1,0:T(8,128)}), f32[128,8,128]{2,1,0:T(8,128)S(1)}, u32[]{:S(2)}, u32[]{:S(2)}) async-start(f32[128,8,128]{2,1,0:T(8,128)} %bitcast.62), calls=%async_computation.1 | async-start | bytes 1048576 | tf_op jit(solution)/shard_map/all_to_all | solution.py:315
  96.9 0.0 copy-done.1
  96.9 0.1 subtract_bitcast_fusion.1
  97.0 2.0 %copy.18.offset_ref = s32[8,512,1]{2,1,0:T(8,128)} copy(s32[8,512,1]{1,0,2:T(8,128)S(1)} %subtract_bitcast_fusion.1) | data formatting | bytes 32768 | tf_op jit(solution)/shard_map/broadcast_in_dim | solution.py:256
  98.9 0.1 fusion.43
  99.1 0.1 fusion.41
  99.2 0.3 fusion.33
  99.5 11.1 %all-to-all-done.1 = f32[128,8,128]{2,1,0:T(8,128)S(1)} async-done(((f32[128,8,128]{2,1,0:T(8,128)}), f32[128,8,128]{2,1,0:T(8,128)S(1)}, u32[]{:S(2)}, u32[]{:S(2)}) %all-to-all-start.1) | async-done | bytes 524320 | tf_op jit(solution)/shard_map/all_to_all | solution.py:315
  110.6 0.6 reshape.89
  111.2 0.6 copy.21
  111.8 0.2 reshape_reshape.3
  112.0 1.1 convolution_bitcast_fusion
  113.1 0.2 add_bitcast_fusion
  113.3 1.0 fusion.6
  114.4 0.3 fusion.13
  114.7 0.2 copy.17
  114.9 0.9 reshape.90.spectrum_ref
  115.8 6.6 %shard_map.70 = f32[16,512]{1,0:T(8,128)} custom-call(f32[16,4096]{1,0:T(8,128)} %reshape.90.spectrum_ref, s32[8,512,1]{2,1,0:T(8,128)} %copy.18.offset_ref), custom_call_target="tpu_custom_call" | custom-call | tf_op jit(solution)/shard_map/pallas_call | solution.py:258
  (11 shorter events, 0.1 us)
Async XLA Ops:
  1.9 6.8 %collective-permute-start = (bf16[256,256]{0,1:T(8,128)(2,1)S(1)}, bf16[256,256]{0,1:T(8,128)(2,1)S(1)}, u32[]{:S(2)}, u32[]{:S(2)}) collective-permute-start(bf16[256,256]{0,1:T(8,128)(2,1)S(1)} %slice.108), channel_id=1, source_target_pairs={{0,1},{1,2},{2,3},{3,4},{4,5},{5,6},{6,7},{8,9},{9,10},{10,11},{11... | collective-permute-start | bytes 393224 | tf_op jit(solution)/shard_map/ppermute | solution.py:276
  22.2 37.3 %all-to-all-start = ((f32[16,256,128]{2,1,0:T(8,128)}), f32[16,256,128]{2,1,0:T(8,128)S(1)}, u32[]{:S(2)}, u32[]{:S(2)}) async-start(f32[16,256,128]{2,1,0:T(8,128)} %shard_map.68), calls=%async_computation | async-start | bytes 4194304 | tf_op jit(solution)/shard_map/all_to_all | solution.py:297
  59.5 1.3 %copy-start = (f32[16,256,128]{2,1,0:T(8,128)}, f32[16,256,128]{2,1,0:T(8,128)S(1)}, u32[]{:S(2)}) copy-start(f32[16,256,128]{2,1,0:T(8,128)S(1)} %all-to-all-done) | copy-start | bytes 6291460
  60.8 36.1 %copy-start.1 = (s32[8,512]{1,0:T(8,128)S(1)}, s32[8,512]{1,0:T(8,128)}, u32[]{:S(2)}) copy-start(s32[8,512]{1,0:T(8,128)} %param.9) | copy-start | bytes 49156
  90.0 20.6 %all-to-all-start.1 = ((f32[128,8,128]{2,1,0:T(8,128)}), f32[128,8,128]{2,1,0:T(8,128)S(1)}, u32[]{:S(2)}, u32[]{:S(2)}) async-start(f32[128,8,128]{2,1,0:T(8,128)} %bitcast.62), calls=%async_computation.1 | async-start | bytes 1048576 | tf_op jit(solution)/shard_map/all_to_all | solution.py:315

commit v14 on v13

--- a/solution.py
+++ b/solution.py
@@ -139,11 +139,12 @@
     total = None
     for order in range(HARM):
         stride = order + 1
-        offset = offset_ref[order]
-        for phase in range(stride):
+        offset = jnp.broadcast_to(offset_ref[order], (fundamentals, power_ref.shape[1]))
+        term = power_ref[pl.ds(0, fundamentals, stride=stride), :]
+        for phase in range(1, stride):
             picked = power_ref[pl.ds(phase, fundamentals, stride=stride), :]
-            term = jnp.where(offset == phase, picked, 0.0)
-            total = term if total is None else total + term
+            term = jnp.where(offset == phase, picked, term)
+        total = term if total is None else total + term
     out_ref[...] = jnp.transpose(total * (1.0 / HARM))
 
 

time: 123 us -> 120 us (0.976)
  Pallas kernels: 47.8 us -> 45.3 us
    pallas_call x1, Pallas kernels: 6.55 us -> 4.11 us  [spectra(): pl.pallas_call(harmonic_kernel, out_shape=jax.ShapeDtypeStruct((count, fu...]
  transfers between devices with their start and end apart: 3 -> 3, of which waited for: 2 -> 2; matrix products, arithmetic and copies ran while one was open for 16% -> 17% of each run, Pallas kernels for 0% -> 0%
where the time goes in v14:
time: 120 us
  Pallas kernels  45.3 us (38%)
  waiting for transfers between devices  25.3 us (21%)
  starting transfers between devices  19.1 us (16%)
  other arithmetic  14.1 us (12%)
  local copies, waits for them, and re-layouts  13.1 us (11%)
  matrix products  2.14 us (2%)
    pallas_call x1, Pallas kernels, run_matmul_levels(): pl.pallas_call(functools.partial(matmul_kernel, plan), out_shape=jax.Shap...  29.2 us
    all_to_all x1, waiting for transfers between devices, on_device(): lax.all_to_all(pieces, 'chan', split_axis=0, concat_axis=0, tiled=True)  14.2 us
    pallas_call x1, Pallas kernels, run_local(): pl.pallas_call(functools.partial(local_kernel, plan, sub, base), out_shap...  12 us
    all_to_all x1, waiting for transfers between devices, on_device(): lax.all_to_all(outgoing, ('chan', 'tm'), split_axis=0, concat_axis=0, til...  11.1 us
    convert_element_type x4, other arithmetic, run_matmul_levels(): (first_rows[level, :row_out, None] == columns).astype(jnp.bfloat16)  10.6 us
    all_to_all x1, starting transfers between devices, on_device(): lax.all_to_all(pieces, 'chan', split_axis=0, concat_axis=0, tiled=True)  7.79 us
    all_to_all x1, starting transfers between devices, on_device(): lax.all_to_all(outgoing, ('chan', 'tm'), split_axis=0, concat_axis=0, til...  6.84 us
    another operation x7, local copies, waits for them, and re-layouts, run_matmul_levels(): tables.append(shifts[level, :row_out, None])  4.7 us
  transfers between devices with their start and end apart: 3, of which 2 were waited for; matrix products, arithmetic and copies ran while one was open for 17% of the time, Pallas kernels for 0%

profile of v14, /device:TPU:1, one launch (start us, length us, event | category | flops | bytes accessed | tf_op | source)
XLA Modules:
  0.0 119.9 jit_solution(136689067642810211)
XLA Ops:
  0.6 1.2 %copy.9 = bf16[256,1024]{0,1:T(8,128)(2,1)S(1)} copy(bf16[256,1024]{1,0:T(8,128)(2,1)} %param.5) | data formatting | bytes 1048576 | tf_op args[0]
  1.9 4.5 %collective-permute-start = (bf16[256,256]{0,1:T(8,128)(2,1)S(1)}, bf16[256,256]{0,1:T(8,128)(2,1)S(1)}, u32[]{:S(2)}, u32[]{:S(2)}) collective-permute-start(bf16[256,256]{0,1:T(8,128)(2,1)S(1)} %slice.108), channel_id=1, source_target_pairs={{0,1},{1,2},{2,3},{3,4},{4,5},{5,6},{6,7},{8,9},{9,10},{10,11},{11... | collective-permute-start | bytes 393224 | tf_op jit(solution)/shard_map/ppermute | solution.py:277
  6.4 0.9 pad_add_fusion
  7.4 1.3 %pad_add_fusion.2.table_ref = s32[3,8,256]{2,1,0:T(8,128)} fusion(s32[1,12,2048]{2,1,0:T(8,128)} %bitcast.64, s32[1,12,2048]{2,1,0:T(8,128)} %bitcast.66, s32[1,12,2048]{2,1,0:T(8,128)} %bitcast.68), kind=kLoop, calls=%fused_computation.73 | loop fusion | flops 12288 | bytes 319488 | tf_op jit(solution)/shard_map/slice | solution.py:289
  8.7 0.0 collective-permute-done
  8.7 1.3 %copy.11 = f32[256,10,128]{2,0,1:T(8,128)} copy(bf16[256,10,128]{0,2,1:T(8,128)(2,1)S(1)} %bitcast.61) | data formatting | bytes 1966080 | tf_op jit(solution)/shard_map/broadcast_in_dim | solution.py:288
  10.1 12.0 %shard_map.68 = f32[16,256,128]{2,1,0:T(8,128)} custom-call(s32[3,8,256]{2,1,0:T(8,128)} %pad_add_fusion.2.table_ref, f32[1,10,256,128]{3,2,1,0:T(8,128)} %bitcast.59), custom_call_target="tpu_custom_call" | custom-call | tf_op jit(solution)/shard_map/pallas_call | solution.py:197
  22.2 7.8 %all-to-all-start = ((f32[16,256,128]{2,1,0:T(8,128)}), f32[16,256,128]{2,1,0:T(8,128)S(1)}, u32[]{:S(2)}, u32[]{:S(2)}) async-start(f32[16,256,128]{2,1,0:T(8,128)} %shard_map.68), calls=%async_computation | async-start | bytes 4194304 | tf_op jit(solution)/shard_map/all_to_all | solution.py:298
  30.0 0.9 copy.12.refs_2_
  30.9 1.0 copy.13.refs_5_
  31.9 1.4 %copy.14.refs_8_ = s32[2048,1]{1,0:T(8,128)} copy(s32[2048,1]{0,1:T(1,128)S(1)} %get-tuple-element.11) | data formatting | bytes 16384 | tf_op jit(solution)/shard_map/broadcast_in_dim;squeeze | solution.py:117
  33.2 1.4 %copy.15.refs_11_ = s32[2048,1]{1,0:T(8,128)} copy(s32[2048,1]{0,1:T(1,128)S(1)} %get-tuple-element.8) | data formatting | bytes 16384 | tf_op jit(solution)/shard_map/broadcast_in_dim;squeeze | solution.py:117
  34.6 1.0 fusion.15
  35.6 1.7 %fusion.4 = (bf16[1024,512]{1,0:T(8,128)(2,1)}, bf16[1024,512]{1,0:T(8,128)(2,1)}) fusion(s32[1024]{0:T(1024)S(1)} %bitcast.73, s32[1024]{0:T(1024)S(1)} %bitcast.74), kind=kLoop, calls=%fused_computation.10 | loop fusion | flops 2097152 | bytes 2105344 | tf_op jit(solution)/shard_map/convert_element_type | solution.py:115
  37.3 4.0 %fusion = (bf16[2048,1024]{1,0:T(8,128)(2,1)}, bf16[2048,1024]{1,0:T(8,128)(2,1)}) fusion(s32[2048]{0:T(1024)S(1)} %bitcast.72, s32[2048]{0:T(1024)S(1)} %bitcast.71), kind=kLoop, calls=%fused_computation.4 | loop fusion | flops 8388608 | bytes 8404992 | tf_op jit(solution)/shard_map/convert_element_type | solution.py:115
  41.3 4.0 %fusion.2 = (bf16[2048,1024]{1,0:T(8,128)(2,1)}, bf16[2048,1024]{1,0:T(8,128)(2,1)}) fusion(s32[2048]{0:T(1024)S(1)} %bitcast.70, s32[2048]{0:T(1024)S(1)} %bitcast.69), kind=kLoop, calls=%fused_computation.6 | loop fusion | flops 8388608 | bytes 8404992 | tf_op jit(solution)/shard_map/convert_element_type | solution.py:115
  45.2 14.2 %all-to-all-done = f32[16,256,128]{2,1,0:T(8,128)S(1)} async-done(((f32[16,256,128]{2,1,0:T(8,128)}), f32[16,256,128]{2,1,0:T(8,128)S(1)}, u32[]{:S(2)}, u32[]{:S(2)}) %all-to-all-start) | async-done | bytes 2097184 | tf_op jit(solution)/shard_map/all_to_all | solution.py:298
  59.5 0.0 copy-start
  59.5 1.3 %copy-done = f32[16,256,128]{2,1,0:T(8,128)} copy-done((f32[16,256,128]{2,1,0:T(8,128)}, f32[16,256,128]{2,1,0:T(8,128)S(1)}, u32[]{:S(2)}) %copy-start) | copy-done | bytes 2097176
  60.8 0.0 copy-start.1
  60.8 29.2 %shard_map.69 = f32[1024,128]{1,0:T(8,128)} custom-call(f32[4096,128]{1,0:T(8,128)} %bitcast.58, bf16[512,256]{1,0:T(8,128)(2,1)} %get-tuple-element.23.refs_0_, bf16[512,256]{1,0:T(8,128)(2,1)} %get-tuple-element.24.refs_1_, s32[512,1]{1,0:T(8,128)} %copy.12.refs_2_, bf16[1024,512]{1,0:T(8,128)(2,1)} %get-tuple-element.21.refs_3_, ...), custom_call_target="tpu_custom_call" | custom-call | tf_op jit(solution)/shard_map/pallas_call | solution.py:121
  90.0 6.8 %all-to-all-start.1 = ((f32[128,8,128]{2,1,0:T(8,128)}), f32[128,8,128]{2,1,0:T(8,128)S(1)}, u32[]{:S(2)}, u32[]{:S(2)}) async-start(f32[128,8,128]{2,1,0:T(8,128)} %bitcast.62), calls=%async_computation.1 | async-start | bytes 1048576 | tf_op jit(solution)/shard_map/all_to_all | solution.py:316
  96.9 0.0 copy-done.1
  96.9 0.1 subtract_bitcast_fusion.1
  97.0 2.0 %copy.18.offset_ref = s32[8,512,1]{2,1,0:T(8,128)} copy(s32[8,512,1]{1,0,2:T(8,128)S(1)} %subtract_bitcast_fusion.1) | data formatting | bytes 32768 | tf_op jit(solution)/shard_map/broadcast_in_dim | solution.py:257
  98.9 0.1 fusion.43
  99.1 0.1 fusion.41
  99.2 0.3 fusion.33
  99.5 11.1 %all-to-all-done.1 = f32[128,8,128]{2,1,0:T(8,128)S(1)} async-done(((f32[128,8,128]{2,1,0:T(8,128)}), f32[128,8,128]{2,1,0:T(8,128)S(1)}, u32[]{:S(2)}, u32[]{:S(2)}) %all-to-all-start.1) | async-done | bytes 524320 | tf_op jit(solution)/shard_map/all_to_all | solution.py:316
  110.6 0.6 reshape.89
  111.2 0.6 copy.21
  111.8 0.2 reshape_reshape.3
  112.0 1.1 convolution_bitcast_fusion
  113.1 0.2 add_bitcast_fusion
  113.3 1.0 fusion.6
  114.4 0.3 fusion.13
  114.7 0.2 copy.17
  114.9 0.9 reshape.90.spectrum_ref
  115.8 4.1 %shard_map.70 = f32[16,512]{1,0:T(8,128)} custom-call(f32[16,4096]{1,0:T(8,128)} %reshape.90.spectrum_ref, s32[8,512,1]{2,1,0:T(8,128)} %copy.18.offset_ref), custom_call_target="tpu_custom_call" | custom-call | tf_op jit(solution)/shard_map/pallas_call | solution.py:259
  (11 shorter events, 0.1 us)
Async XLA Ops:
  1.9 6.8 %collective-permute-start = (bf16[256,256]{0,1:T(8,128)(2,1)S(1)}, bf16[256,256]{0,1:T(8,128)(2,1)S(1)}, u32[]{:S(2)}, u32[]{:S(2)}) collective-permute-start(bf16[256,256]{0,1:T(8,128)(2,1)S(1)} %slice.108), channel_id=1, source_target_pairs={{0,1},{1,2},{2,3},{3,4},{4,5},{5,6},{6,7},{8,9},{9,10},{10,11},{11... | collective-permute-start | bytes 393224 | tf_op jit(solution)/shard_map/ppermute | solution.py:277
  22.2 37.3 %all-to-all-start = ((f32[16,256,128]{2,1,0:T(8,128)}), f32[16,256,128]{2,1,0:T(8,128)S(1)}, u32[]{:S(2)}, u32[]{:S(2)}) async-start(f32[16,256,128]{2,1,0:T(8,128)} %shard_map.68), calls=%async_computation | async-start | bytes 4194304 | tf_op jit(solution)/shard_map/all_to_all | solution.py:298
  59.5 1.3 %copy-start = (f32[16,256,128]{2,1,0:T(8,128)}, f32[16,256,128]{2,1,0:T(8,128)S(1)}, u32[]{:S(2)}) copy-start(f32[16,256,128]{2,1,0:T(8,128)S(1)} %all-to-all-done) | copy-start | bytes 6291460
  60.8 36.1 %copy-start.1 = (s32[8,512]{1,0:T(8,128)S(1)}, s32[8,512]{1,0:T(8,128)}, u32[]{:S(2)}) copy-start(s32[8,512]{1,0:T(8,128)} %param.9) | copy-start | bytes 49156
  90.0 20.6 %all-to-all-start.1 = ((f32[128,8,128]{2,1,0:T(8,128)}), f32[128,8,128]{2,1,0:T(8,128)S(1)}, u32[]{:S(2)}, u32[]{:S(2)}) async-start(f32[128,8,128]{2,1,0:T(8,128)} %bitcast.62), calls=%async_computation.1 | async-start | bytes 1048576 | tf_op jit(solution)/shard_map/all_to_all | solution.py:316

commit v15 on v14

--- a/solution.py
+++ b/solution.py
@@ -173,7 +173,7 @@
                 target[row] = merged
             return carry
 
-        lax.fori_loop(0, row_out, body, 0, unroll=min(row_out, 16))
+        lax.fori_loop(0, row_out, body, 0, unroll=min(row_out, 32 if bands_out <= 2 else 16))
         source = target
     for dest in range(out_ref.shape[0]):
         start = base + sub * dest

time: 120 us -> 120 us (level)
  no operation moved by 1% of the time
where the time goes in v15:
time: 120 us; the launch traced here: 119 us
  Pallas kernels  44.5 us (37%)
  waiting for transfers between devices  25.3 us (21%)
  starting transfers between devices  19.1 us (16%)
  other arithmetic  14.1 us (12%)
  local copies, waits for them, and re-layouts  13.1 us (11%)
  matrix products  2.13 us (2%)
    pallas_call x1, Pallas kernels, run_matmul_levels(): pl.pallas_call(functools.partial(matmul_kernel, plan), out_shape=jax.Shap...  29.2 us
    all_to_all x1, waiting for transfers between devices, on_device(): lax.all_to_all(pieces, 'chan', split_axis=0, concat_axis=0, tiled=True)  14.2 us
    pallas_call x1, Pallas kernels, run_local(): pl.pallas_call(functools.partial(local_kernel, plan, sub, base), out_shap...  11.2 us
    all_to_all x1, waiting for transfers between devices, on_device(): lax.all_to_all(outgoing, ('chan', 'tm'), split_axis=0, concat_axis=0, til...  11.1 us
    convert_element_type x4, other arithmetic, run_matmul_levels(): (first_rows[level, :row_out, None] == columns).astype(jnp.bfloat16)  10.6 us
    all_to_all x1, starting transfers between devices, on_device(): lax.all_to_all(pieces, 'chan', split_axis=0, concat_axis=0, tiled=True)  7.79 us
    all_to_all x1, starting transfers between devices, on_device(): lax.all_to_all(outgoing, ('chan', 'tm'), split_axis=0, concat_axis=0, til...  6.84 us
    another operation x7, local copies, waits for them, and re-layouts, run_matmul_levels(): tables.append(shifts[level, :row_out, None])  4.7 us
  transfers between devices with their start and end apart: 3, of which 2 were waited for; matrix products, arithmetic and copies ran while one was open for 17% of the time, Pallas kernels for 0%

profile of v15, /device:TPU:1, one launch (start us, length us, event | category | flops | bytes accessed | tf_op | source)
XLA Modules:
  0.0 119.1 jit_solution(1074477438338535661)
XLA Ops:
  0.6 1.2 %copy.9 = bf16[256,1024]{0,1:T(8,128)(2,1)S(1)} copy(bf16[256,1024]{1,0:T(8,128)(2,1)} %param.5) | data formatting | bytes 1048576 | tf_op args[0]
  1.9 4.5 %collective-permute-start = (bf16[256,256]{0,1:T(8,128)(2,1)S(1)}, bf16[256,256]{0,1:T(8,128)(2,1)S(1)}, u32[]{:S(2)}, u32[]{:S(2)}) collective-permute-start(bf16[256,256]{0,1:T(8,128)(2,1)S(1)} %slice.108), channel_id=1, source_target_pairs={{0,1},{1,2},{2,3},{3,4},{4,5},{5,6},{6,7},{8,9},{9,10},{10,11},{11... | collective-permute-start | bytes 393224 | tf_op jit(solution)/shard_map/ppermute | solution.py:277
  6.4 0.9 pad_add_fusion
  7.4 1.3 %pad_add_fusion.2.table_ref = s32[3,8,256]{2,1,0:T(8,128)} fusion(s32[1,12,2048]{2,1,0:T(8,128)} %bitcast.64, s32[1,12,2048]{2,1,0:T(8,128)} %bitcast.66, s32[1,12,2048]{2,1,0:T(8,128)} %bitcast.68), kind=kLoop, calls=%fused_computation.73 | loop fusion | flops 12288 | bytes 319488 | tf_op jit(solution)/shard_map/slice | solution.py:289
  8.7 0.0 collective-permute-done
  8.7 1.3 %copy.11 = f32[256,10,128]{2,0,1:T(8,128)} copy(bf16[256,10,128]{0,2,1:T(8,128)(2,1)S(1)} %bitcast.61) | data formatting | bytes 1966080 | tf_op jit(solution)/shard_map/broadcast_in_dim | solution.py:288
  10.1 11.2 %shard_map.68 = f32[16,256,128]{2,1,0:T(8,128)} custom-call(s32[3,8,256]{2,1,0:T(8,128)} %pad_add_fusion.2.table_ref, f32[1,10,256,128]{3,2,1,0:T(8,128)} %bitcast.59), custom_call_target="tpu_custom_call" | custom-call | tf_op jit(solution)/shard_map/pallas_call | solution.py:197
  21.3 7.8 %all-to-all-start = ((f32[16,256,128]{2,1,0:T(8,128)}), f32[16,256,128]{2,1,0:T(8,128)S(1)}, u32[]{:S(2)}, u32[]{:S(2)}) async-start(f32[16,256,128]{2,1,0:T(8,128)} %shard_map.68), calls=%async_computation | async-start | bytes 4194304 | tf_op jit(solution)/shard_map/all_to_all | solution.py:298
  29.2 0.9 copy.12.refs_2_
  30.0 1.0 copy.13.refs_5_
  31.1 1.4 %copy.14.refs_8_ = s32[2048,1]{1,0:T(8,128)} copy(s32[2048,1]{0,1:T(1,128)S(1)} %get-tuple-element.11) | data formatting | bytes 16384 | tf_op jit(solution)/shard_map/broadcast_in_dim;squeeze | solution.py:117
  32.4 1.4 %copy.15.refs_11_ = s32[2048,1]{1,0:T(8,128)} copy(s32[2048,1]{0,1:T(1,128)S(1)} %get-tuple-element.8) | data formatting | bytes 16384 | tf_op jit(solution)/shard_map/broadcast_in_dim;squeeze | solution.py:117
  33.8 1.0 fusion.15
  34.8 1.7 %fusion.4 = (bf16[1024,512]{1,0:T(8,128)(2,1)}, bf16[1024,512]{1,0:T(8,128)(2,1)}) fusion(s32[1024]{0:T(1024)S(1)} %bitcast.73, s32[1024]{0:T(1024)S(1)} %bitcast.74), kind=kLoop, calls=%fused_computation.10 | loop fusion | flops 2097152 | bytes 2105344 | tf_op jit(solution)/shard_map/convert_element_type | solution.py:115
  36.5 4.0 %fusion = (bf16[2048,1024]{1,0:T(8,128)(2,1)}, bf16[2048,1024]{1,0:T(8,128)(2,1)}) fusion(s32[2048]{0:T(1024)S(1)} %bitcast.72, s32[2048]{0:T(1024)S(1)} %bitcast.71), kind=kLoop, calls=%fused_computation.4 | loop fusion | flops 8388608 | bytes 8404992 | tf_op jit(solution)/shard_map/convert_element_type | solution.py:115
  40.4 4.0 %fusion.2 = (bf16[2048,1024]{1,0:T(8,128)(2,1)}, bf16[2048,1024]{1,0:T(8,128)(2,1)}) fusion(s32[2048]{0:T(1024)S(1)} %bitcast.70, s32[2048]{0:T(1024)S(1)} %bitcast.69), kind=kLoop, calls=%fused_computation.6 | loop fusion | flops 8388608 | bytes 8404992 | tf_op jit(solution)/shard_map/convert_element_type | solution.py:115
  44.4 14.2 %all-to-all-done = f32[16,256,128]{2,1,0:T(8,128)S(1)} async-done(((f32[16,256,128]{2,1,0:T(8,128)}), f32[16,256,128]{2,1,0:T(8,128)S(1)}, u32[]{:S(2)}, u32[]{:S(2)}) %all-to-all-start) | async-done | bytes 2097184 | tf_op jit(solution)/shard_map/all_to_all | solution.py:298
  58.6 0.0 copy-start
  58.6 1.3 %copy-done = f32[16,256,128]{2,1,0:T(8,128)} copy-done((f32[16,256,128]{2,1,0:T(8,128)}, f32[16,256,128]{2,1,0:T(8,128)S(1)}, u32[]{:S(2)}) %copy-start) | copy-done | bytes 2097176
  60.0 0.0 copy-start.1
  60.0 29.2 %shard_map.69 = f32[1024,128]{1,0:T(8,128)} custom-call(f32[4096,128]{1,0:T(8,128)} %bitcast.58, bf16[512,256]{1,0:T(8,128)(2,1)} %get-tuple-element.23.refs_0_, bf16[512,256]{1,0:T(8,128)(2,1)} %get-tuple-element.24.refs_1_, s32[512,1]{1,0:T(8,128)} %copy.12.refs_2_, bf16[1024,512]{1,0:T(8,128)(2,1)} %get-tuple-element.21.refs_3_, ...), custom_call_target="tpu_custom_call" | custom-call | tf_op jit(solution)/shard_map/pallas_call | solution.py:121
  89.2 6.8 %all-to-all-start.1 = ((f32[128,8,128]{2,1,0:T(8,128)}), f32[128,8,128]{2,1,0:T(8,128)S(1)}, u32[]{:S(2)}, u32[]{:S(2)}) async-start(f32[128,8,128]{2,1,0:T(8,128)} %bitcast.62), calls=%async_computation.1 | async-start | bytes 1048576 | tf_op jit(solution)/shard_map/all_to_all | solution.py:316
  96.1 0.0 copy-done.1
  96.1 0.1 subtract_bitcast_fusion.1
  96.1 2.0 %copy.18.offset_ref = s32[8,512,1]{2,1,0:T(8,128)} copy(s32[8,512,1]{1,0,2:T(8,128)S(1)} %subtract_bitcast_fusion.1) | data formatting | bytes 32768 | tf_op jit(solution)/shard_map/broadcast_in_dim | solution.py:257
  98.1 0.1 fusion.43
  98.3 0.1 fusion.41
  98.4 0.3 fusion.33
  98.7 11.1 %all-to-all-done.1 = f32[128,8,128]{2,1,0:T(8,128)S(1)} async-done(((f32[128,8,128]{2,1,0:T(8,128)}), f32[128,8,128]{2,1,0:T(8,128)S(1)}, u32[]{:S(2)}, u32[]{:S(2)}) %all-to-all-start.1) | async-done | bytes 524320 | tf_op jit(solution)/shard_map/all_to_all | solution.py:316
  109.8 0.6 reshape.89
  110.4 0.6 copy.21
  111.0 0.2 reshape_reshape.3
  111.2 1.1 convolution_bitcast_fusion
  112.3 0.2 add_bitcast_fusion
  112.5 1.0 fusion.6
  113.5 0.3 fusion.13
  113.9 0.2 copy.17
  114.1 0.9 reshape.90.spectrum_ref
  115.0 4.1 %shard_map.70 = f32[16,512]{1,0:T(8,128)} custom-call(f32[16,4096]{1,0:T(8,128)} %reshape.90.spectrum_ref, s32[8,512,1]{2,1,0:T(8,128)} %copy.18.offset_ref), custom_call_target="tpu_custom_call" | custom-call | tf_op jit(solution)/shard_map/pallas_call | solution.py:259
  (11 shorter events, 0.1 us)
Async XLA Ops:
  1.9 6.8 %collective-permute-start = (bf16[256,256]{0,1:T(8,128)(2,1)S(1)}, bf16[256,256]{0,1:T(8,128)(2,1)S(1)}, u32[]{:S(2)}, u32[]{:S(2)}) collective-permute-start(bf16[256,256]{0,1:T(8,128)(2,1)S(1)} %slice.108), channel_id=1, source_target_pairs={{0,1},{1,2},{2,3},{3,4},{4,5},{5,6},{6,7},{8,9},{9,10},{10,11},{11... | collective-permute-start | bytes 393224 | tf_op jit(solution)/shard_map/ppermute | solution.py:277
  21.3 37.3 %all-to-all-start = ((f32[16,256,128]{2,1,0:T(8,128)}), f32[16,256,128]{2,1,0:T(8,128)S(1)}, u32[]{:S(2)}, u32[]{:S(2)}) async-start(f32[16,256,128]{2,1,0:T(8,128)} %shard_map.68), calls=%async_computation | async-start | bytes 4194304 | tf_op jit(solution)/shard_map/all_to_all | solution.py:298
  58.6 1.3 %copy-start = (f32[16,256,128]{2,1,0:T(8,128)}, f32[16,256,128]{2,1,0:T(8,128)S(1)}, u32[]{:S(2)}) copy-start(f32[16,256,128]{2,1,0:T(8,128)S(1)} %all-to-all-done) | copy-start | bytes 6291460
  60.0 36.1 %copy-start.1 = (s32[8,512]{1,0:T(8,128)S(1)}, s32[8,512]{1,0:T(8,128)}, u32[]{:S(2)}) copy-start(s32[8,512]{1,0:T(8,128)} %param.9) | copy-start | bytes 49156
  89.2 20.6 %all-to-all-start.1 = ((f32[128,8,128]{2,1,0:T(8,128)}), f32[128,8,128]{2,1,0:T(8,128)S(1)}, u32[]{:S(2)}, u32[]{:S(2)}) async-start(f32[128,8,128]{2,1,0:T(8,128)} %bitcast.62), calls=%async_computation.1 | async-start | bytes 1048576 | tf_op jit(solution)/shard_map/all_to_all | solution.py:316

commit v16 on v15

--- a/solution.py
+++ b/solution.py
@@ -15,7 +15,7 @@
 HARM = 8
 RAW_HALO = 256
 SUB_HALO = 64
-TILE = 1024
+TILE = 2048
 LANES = 128
 PIECES = 2
 

time: 120 us -> 120 us (level)
  no operation moved by 1% of the time
where the time goes in v16:
time: 120 us
  Pallas kernels  44.9 us (37%)
  waiting for transfers between devices  25.3 us (21%)
  starting transfers between devices  19.1 us (16%)
  other arithmetic  14.1 us (12%)
  local copies, waits for them, and re-layouts  13.1 us (11%)
  matrix products  2.13 us (2%)
    pallas_call x1, Pallas kernels, run_matmul_levels(): pl.pallas_call(functools.partial(matmul_kernel, plan), out_shape=jax.Shap...  29.6 us
    all_to_all x1, waiting for transfers between devices, on_device(): lax.all_to_all(pieces, 'chan', split_axis=0, concat_axis=0, tiled=True)  14.2 us
    pallas_call x1, Pallas kernels, run_local(): pl.pallas_call(functools.partial(local_kernel, plan, sub, base), out_shap...  11.2 us
    all_to_all x1, waiting for transfers between devices, on_device(): lax.all_to_all(outgoing, ('chan', 'tm'), split_axis=0, concat_axis=0, til...  11.1 us
    convert_element_type x4, other arithmetic, run_matmul_levels(): (first_rows[level, :row_out, None] == columns).astype(jnp.bfloat16)  10.6 us
    all_to_all x1, starting transfers between devices, on_device(): lax.all_to_all(pieces, 'chan', split_axis=0, concat_axis=0, tiled=True)  7.78 us
    all_to_all x1, starting transfers between devices, on_device(): lax.all_to_all(outgoing, ('chan', 'tm'), split_axis=0, concat_axis=0, til...  6.85 us
    another operation x7, local copies, waits for them, and re-layouts, run_matmul_levels(): tables.append(shifts[level, :row_out, None])  4.7 us
  transfers between devices with their start and end apart: 3, of which 2 were waited for; matrix products, arithmetic and copies ran while one was open for 17% of the time, Pallas kernels for 0%

profile of v16, /device:TPU:1, one launch (start us, length us, event | category | flops | bytes accessed | tf_op | source)
XLA Modules:
  0.0 119.5 jit_solution(8925288997075788477)
XLA Ops:
  0.6 1.2 %copy.9 = bf16[256,1024]{0,1:T(8,128)(2,1)S(1)} copy(bf16[256,1024]{1,0:T(8,128)(2,1)} %param.5) | data formatting | bytes 1048576 | tf_op args[0]
  1.9 4.5 %collective-permute-start = (bf16[256,256]{0,1:T(8,128)(2,1)S(1)}, bf16[256,256]{0,1:T(8,128)(2,1)S(1)}, u32[]{:S(2)}, u32[]{:S(2)}) collective-permute-start(bf16[256,256]{0,1:T(8,128)(2,1)S(1)} %slice.108), channel_id=1, source_target_pairs={{0,1},{1,2},{2,3},{3,4},{4,5},{5,6},{6,7},{8,9},{9,10},{10,11},{11... | collective-permute-start | bytes 393224 | tf_op jit(solution)/shard_map/ppermute | solution.py:277
  6.4 0.9 pad_add_fusion
  7.4 1.3 %pad_add_fusion.2.table_ref = s32[3,8,256]{2,1,0:T(8,128)} fusion(s32[1,12,2048]{2,1,0:T(8,128)} %bitcast.64, s32[1,12,2048]{2,1,0:T(8,128)} %bitcast.66, s32[1,12,2048]{2,1,0:T(8,128)} %bitcast.68), kind=kLoop, calls=%fused_computation.73 | loop fusion | flops 12288 | bytes 319488 | tf_op jit(solution)/shard_map/slice | solution.py:289
  8.7 0.0 collective-permute-done
  8.7 1.3 %copy.11 = f32[256,10,128]{2,0,1:T(8,128)} copy(bf16[256,10,128]{0,2,1:T(8,128)(2,1)S(1)} %bitcast.61) | data formatting | bytes 1966080 | tf_op jit(solution)/shard_map/broadcast_in_dim | solution.py:288
  10.1 11.2 %shard_map.68 = f32[16,256,128]{2,1,0:T(8,128)} custom-call(s32[3,8,256]{2,1,0:T(8,128)} %pad_add_fusion.2.table_ref, f32[1,10,256,128]{3,2,1,0:T(8,128)} %bitcast.59), custom_call_target="tpu_custom_call" | custom-call | tf_op jit(solution)/shard_map/pallas_call | solution.py:197
  21.4 7.8 %all-to-all-start = ((f32[16,256,128]{2,1,0:T(8,128)}), f32[16,256,128]{2,1,0:T(8,128)S(1)}, u32[]{:S(2)}, u32[]{:S(2)}) async-start(f32[16,256,128]{2,1,0:T(8,128)} %shard_map.68), calls=%async_computation | async-start | bytes 4194304 | tf_op jit(solution)/shard_map/all_to_all | solution.py:298
  29.2 0.9 copy.12.refs_2_
  30.0 1.0 copy.13.refs_5_
  31.1 1.4 %copy.14.refs_8_ = s32[2048,1]{1,0:T(8,128)} copy(s32[2048,1]{0,1:T(1,128)S(1)} %get-tuple-element.11) | data formatting | bytes 16384 | tf_op jit(solution)/shard_map/broadcast_in_dim;squeeze | solution.py:117
  32.4 1.4 %copy.15.refs_11_ = s32[2048,1]{1,0:T(8,128)} copy(s32[2048,1]{0,1:T(1,128)S(1)} %get-tuple-element.8) | data formatting | bytes 16384 | tf_op jit(solution)/shard_map/broadcast_in_dim;squeeze | solution.py:117
  33.8 1.0 fusion.15
  34.8 1.7 %fusion.4 = (bf16[1024,512]{1,0:T(8,128)(2,1)}, bf16[1024,512]{1,0:T(8,128)(2,1)}) fusion(s32[1024]{0:T(1024)S(1)} %bitcast.73, s32[1024]{0:T(1024)S(1)} %bitcast.74), kind=kLoop, calls=%fused_computation.10 | loop fusion | flops 2097152 | bytes 2105344 | tf_op jit(solution)/shard_map/convert_element_type | solution.py:115
  36.5 4.0 %fusion = (bf16[2048,1024]{1,0:T(8,128)(2,1)}, bf16[2048,1024]{1,0:T(8,128)(2,1)}) fusion(s32[2048]{0:T(1024)S(1)} %bitcast.72, s32[2048]{0:T(1024)S(1)} %bitcast.71), kind=kLoop, calls=%fused_computation.4 | loop fusion | flops 8388608 | bytes 8404992 | tf_op jit(solution)/shard_map/convert_element_type | solution.py:115
  40.4 4.0 %fusion.2 = (bf16[2048,1024]{1,0:T(8,128)(2,1)}, bf16[2048,1024]{1,0:T(8,128)(2,1)}) fusion(s32[2048]{0:T(1024)S(1)} %bitcast.70, s32[2048]{0:T(1024)S(1)} %bitcast.69), kind=kLoop, calls=%fused_computation.6 | loop fusion | flops 8388608 | bytes 8404992 | tf_op jit(solution)/shard_map/convert_element_type | solution.py:115
  44.4 14.2 %all-to-all-done = f32[16,256,128]{2,1,0:T(8,128)S(1)} async-done(((f32[16,256,128]{2,1,0:T(8,128)}), f32[16,256,128]{2,1,0:T(8,128)S(1)}, u32[]{:S(2)}, u32[]{:S(2)}) %all-to-all-start) | async-done | bytes 2097184 | tf_op jit(solution)/shard_map/all_to_all | solution.py:298
  58.6 0.0 copy-start
  58.7 1.3 %copy-done = f32[16,256,128]{2,1,0:T(8,128)} copy-done((f32[16,256,128]{2,1,0:T(8,128)}, f32[16,256,128]{2,1,0:T(8,128)S(1)}, u32[]{:S(2)}) %copy-start) | copy-done | bytes 2097176
  60.0 0.0 copy-start.1
  60.0 29.6 %shard_map.69 = f32[1024,128]{1,0:T(8,128)} custom-call(f32[4096,128]{1,0:T(8,128)} %bitcast.58, bf16[512,256]{1,0:T(8,128)(2,1)} %get-tuple-element.23.refs_0_, bf16[512,256]{1,0:T(8,128)(2,1)} %get-tuple-element.24.refs_1_, s32[512,1]{1,0:T(8,128)} %copy.12.refs_2_, bf16[1024,512]{1,0:T(8,128)(2,1)} %get-tuple-element.21.refs_3_, ...), custom_call_target="tpu_custom_call" | custom-call | tf_op jit(solution)/shard_map/pallas_call | solution.py:121
  89.6 6.8 %all-to-all-start.1 = ((f32[128,8,128]{2,1,0:T(8,128)}), f32[128,8,128]{2,1,0:T(8,128)S(1)}, u32[]{:S(2)}, u32[]{:S(2)}) async-start(f32[128,8,128]{2,1,0:T(8,128)} %bitcast.62), calls=%async_computation.1 | async-start | bytes 1048576 | tf_op jit(solution)/shard_map/all_to_all | solution.py:316
  96.5 0.0 copy-done.1
  96.5 0.1 subtract_bitcast_fusion.1
  96.6 2.0 %copy.18.offset_ref = s32[8,512,1]{2,1,0:T(8,128)} copy(s32[8,512,1]{1,0,2:T(8,128)S(1)} %subtract_bitcast_fusion.1) | data formatting | bytes 32768 | tf_op jit(solution)/shard_map/broadcast_in_dim | solution.py:257
  98.5 0.1 fusion.43
  98.7 0.1 fusion.41
  98.8 0.3 fusion.33
  99.1 11.1 %all-to-all-done.1 = f32[128,8,128]{2,1,0:T(8,128)S(1)} async-done(((f32[128,8,128]{2,1,0:T(8,128)}), f32[128,8,128]{2,1,0:T(8,128)S(1)}, u32[]{:S(2)}, u32[]{:S(2)}) %all-to-all-start.1) | async-done | bytes 524320 | tf_op jit(solution)/shard_map/all_to_all | solution.py:316
  110.2 0.6 reshape.89
  110.8 0.6 copy.21
  111.4 0.2 reshape_reshape.3
  111.6 1.1 convolution_bitcast_fusion
  112.7 0.2 add_bitcast_fusion
  112.9 1.0 fusion.6
  114.0 0.3 fusion.13
  114.3 0.2 copy.17
  114.5 0.9 reshape.90.spectrum_ref
  115.4 4.1 %shard_map.70 = f32[16,512]{1,0:T(8,128)} custom-call(f32[16,4096]{1,0:T(8,128)} %reshape.90.spectrum_ref, s32[8,512,1]{2,1,0:T(8,128)} %copy.18.offset_ref), custom_call_target="tpu_custom_call" | custom-call | tf_op jit(solution)/shard_map/pallas_call | solution.py:259
  (11 shorter events, 0.1 us)
Async XLA Ops:
  1.9 6.8 %collective-permute-start = (bf16[256,256]{0,1:T(8,128)(2,1)S(1)}, bf16[256,256]{0,1:T(8,128)(2,1)S(1)}, u32[]{:S(2)}, u32[]{:S(2)}) collective-permute-start(bf16[256,256]{0,1:T(8,128)(2,1)S(1)} %slice.108), channel_id=1, source_target_pairs={{0,1},{1,2},{2,3},{3,4},{4,5},{5,6},{6,7},{8,9},{9,10},{10,11},{11... | collective-permute-start | bytes 393224 | tf_op jit(solution)/shard_map/ppermute | solution.py:277
  21.4 37.3 %all-to-all-start = ((f32[16,256,128]{2,1,0:T(8,128)}), f32[16,256,128]{2,1,0:T(8,128)S(1)}, u32[]{:S(2)}, u32[]{:S(2)}) async-start(f32[16,256,128]{2,1,0:T(8,128)} %shard_map.68), calls=%async_computation | async-start | bytes 4194304 | tf_op jit(solution)/shard_map/all_to_all | solution.py:298
  58.6 1.3 %copy-start = (f32[16,256,128]{2,1,0:T(8,128)}, f32[16,256,128]{2,1,0:T(8,128)S(1)}, u32[]{:S(2)}) copy-start(f32[16,256,128]{2,1,0:T(8,128)S(1)} %all-to-all-done) | copy-start | bytes 6291460
  60.0 36.5 %copy-start.1 = (s32[8,512]{1,0:T(8,128)S(1)}, s32[8,512]{1,0:T(8,128)}, u32[]{:S(2)}) copy-start(s32[8,512]{1,0:T(8,128)} %param.9) | copy-start | bytes 49156
  89.6 20.6 %all-to-all-start.1 = ((f32[128,8,128]{2,1,0:T(8,128)}), f32[128,8,128]{2,1,0:T(8,128)S(1)}, u32[]{:S(2)}, u32[]{:S(2)}) async-start(f32[128,8,128]{2,1,0:T(8,128)} %bitcast.62), calls=%async_computation.1 | async-start | bytes 1048576 | tf_op jit(solution)/shard_map/all_to_all | solution.py:316

commit v17 on v15

--- a/solution.py
+++ b/solution.py
@@ -157,8 +157,9 @@
 
 def local_kernel(plan, sub, base, table_ref, x_ref, out_ref, *bufs):
     count = len(plan)
-    final = bufs[-1]
-    source = x_ref
+    final = bufs[-2]
+    source = bufs[-1]
+    source[...] = x_ref[...].astype(jnp.float32)
     for step, (row_in, row_out, bands_out) in enumerate(plan):
         target = final if step == count - 1 else bufs[step]
 
@@ -194,6 +195,7 @@
     vmem = pl.BlockSpec(memory_space=pltpu.VMEM)
     scratch = [pltpu.VMEM((p[1], slabs, p[2], LANES), jnp.float32) for p in plan[:-1]]
     scratch.append(pltpu.VMEM((slabs, rows_last, LANES), jnp.float32))
+    scratch.append(pltpu.VMEM(state.shape, jnp.float32))
     return pl.pallas_call(
         functools.partial(local_kernel, plan, sub, base),
         out_shape=jax.ShapeDtypeStruct((parts, rows_last, sub + SUB_HALO), jnp.float32),
@@ -285,7 +287,7 @@
     ]
     sub = samples // chan_count
     pieces = run_local(
-        widened.astype(jnp.float32).reshape(channels, -1, LANES).transpose(1, 0, 2)[None],
+        widened.reshape(channels, -1, LANES).transpose(1, 0, 2)[None],
         jnp.stack([first_rows, second_rows, shifts])[:, :local_levels, :channels],
         local_plan,
         chan_count,

time: 120 us -> 119 us (level)
    broadcast_in_dim x1 -> x0, local copies, waits for them, and re-layouts: 1.31 us -> none  [on_device(): widened.astype(jnp.float32).reshape(channels, -1, LANES).transpose(1, 0, 2)]
where the time goes in v17:
time: 119 us
  Pallas kernels  44.4 us (37%)
  waiting for transfers between devices  25.3 us (21%)
  starting transfers between devices  19.1 us (16%)
  other arithmetic  14.1 us (12%)
  local copies, waits for them, and re-layouts  12.9 us (11%)
  matrix products  2.14 us (2%)
    pallas_call x1, Pallas kernels, run_matmul_levels(): pl.pallas_call(functools.partial(matmul_kernel, plan), out_shape=jax.Shap...  29.2 us
    all_to_all x1, waiting for transfers between devices, on_device(): lax.all_to_all(pieces, 'chan', split_axis=0, concat_axis=0, tiled=True)  14.2 us
    all_to_all x1, waiting for transfers between devices, on_device(): lax.all_to_all(outgoing, ('chan', 'tm'), split_axis=0, concat_axis=0, til...  11.1 us
    pallas_call x1, Pallas kernels, run_local(): pl.pallas_call(functools.partial(local_kernel, plan, sub, base), out_shap...  11 us
    convert_element_type x4, other arithmetic, run_matmul_levels(): (first_rows[level, :row_out, None] == columns).astype(jnp.bfloat16)  10.6 us
    all_to_all x1, starting transfers between devices, on_device(): lax.all_to_all(pieces, 'chan', split_axis=0, concat_axis=0, tiled=True)  7.79 us
    all_to_all x1, starting transfers between devices, on_device(): lax.all_to_all(outgoing, ('chan', 'tm'), split_axis=0, concat_axis=0, til...  6.84 us
    another operation x7, local copies, waits for them, and re-layouts, run_matmul_levels(): tables.append(shifts[level, :row_out, None])  4.7 us
  transfers between devices with their start and end apart: 3, of which 2 were waited for; matrix products, arithmetic and copies ran while one was open for 17% of the time, Pallas kernels for 0%

profile of v17, /device:TPU:1, one launch (start us, length us, event | category | flops | bytes accessed | tf_op | source)
XLA Modules:
  0.0 118.7 jit_solution(5658168478445498100)
XLA Ops:
  0.6 1.2 %copy.9 = bf16[256,1024]{0,1:T(8,128)(2,1)S(1)} copy(bf16[256,1024]{1,0:T(8,128)(2,1)} %param.5) | data formatting | bytes 1048576 | tf_op args[0]
  1.9 4.5 %collective-permute-start = (bf16[256,256]{0,1:T(8,128)(2,1)S(1)}, bf16[256,256]{0,1:T(8,128)(2,1)S(1)}, u32[]{:S(2)}, u32[]{:S(2)}) collective-permute-start(bf16[256,256]{0,1:T(8,128)(2,1)S(1)} %slice.108), channel_id=1, source_target_pairs={{0,1},{1,2},{2,3},{3,4},{4,5},{5,6},{6,7},{8,9},{9,10},{10,11},{11... | collective-permute-start | bytes 393224 | tf_op jit(solution)/shard_map/ppermute | solution.py:279
  6.4 0.9 pad_add_fusion
  7.4 1.3 %pad_add_fusion.2.table_ref = s32[3,8,256]{2,1,0:T(8,128)} fusion(s32[1,12,2048]{2,1,0:T(8,128)} %bitcast.63, s32[1,12,2048]{2,1,0:T(8,128)} %bitcast.65, s32[1,12,2048]{2,1,0:T(8,128)} %bitcast.67), kind=kLoop, calls=%fused_computation.73 | loop fusion | flops 12288 | bytes 319488 | tf_op jit(solution)/shard_map/slice | solution.py:291
  8.7 0.0 collective-permute-done
  8.7 1.1 copy.11
  9.8 11.0 %shard_map.68 = f32[16,256,128]{2,1,0:T(8,128)} custom-call(s32[3,8,256]{2,1,0:T(8,128)} %pad_add_fusion.2.table_ref, bf16[1,10,256,128]{3,2,1,0:T(8,128)(2,1)} %bitcast.60), custom_call_target="tpu_custom_call" | custom-call | tf_op jit(solution)/shard_map/pallas_call | solution.py:199
  21.0 7.8 %all-to-all-start = ((f32[16,256,128]{2,1,0:T(8,128)}), f32[16,256,128]{2,1,0:T(8,128)S(1)}, u32[]{:S(2)}, u32[]{:S(2)}) async-start(f32[16,256,128]{2,1,0:T(8,128)} %shard_map.68), calls=%async_computation | async-start | bytes 4194304 | tf_op jit(solution)/shard_map/all_to_all | solution.py:300
  28.8 0.9 copy.12.refs_2_
  29.7 1.0 copy.13.refs_5_
  30.7 1.4 %copy.14.refs_8_ = s32[2048,1]{1,0:T(8,128)} copy(s32[2048,1]{0,1:T(1,128)S(1)} %get-tuple-element.11) | data formatting | bytes 16384 | tf_op jit(solution)/shard_map/broadcast_in_dim;squeeze | solution.py:117
  32.1 1.4 %copy.15.refs_11_ = s32[2048,1]{1,0:T(8,128)} copy(s32[2048,1]{0,1:T(1,128)S(1)} %get-tuple-element.8) | data formatting | bytes 16384 | tf_op jit(solution)/shard_map/broadcast_in_dim;squeeze | solution.py:117
  33.4 1.0 fusion.15
  34.4 1.7 %fusion.4 = (bf16[1024,512]{1,0:T(8,128)(2,1)}, bf16[1024,512]{1,0:T(8,128)(2,1)}) fusion(s32[1024]{0:T(1024)S(1)} %bitcast.72, s32[1024]{0:T(1024)S(1)} %bitcast.73), kind=kLoop, calls=%fused_computation.10 | loop fusion | flops 2097152 | bytes 2105344 | tf_op jit(solution)/shard_map/convert_element_type | solution.py:115
  36.1 4.0 %fusion = (bf16[2048,1024]{1,0:T(8,128)(2,1)}, bf16[2048,1024]{1,0:T(8,128)(2,1)}) fusion(s32[2048]{0:T(1024)S(1)} %bitcast.71, s32[2048]{0:T(1024)S(1)} %bitcast.70), kind=kLoop, calls=%fused_computation.4 | loop fusion | flops 8388608 | bytes 8404992 | tf_op jit(solution)/shard_map/convert_element_type | solution.py:115
  40.1 4.0 %fusion.2 = (bf16[2048,1024]{1,0:T(8,128)(2,1)}, bf16[2048,1024]{1,0:T(8,128)(2,1)}) fusion(s32[2048]{0:T(1024)S(1)} %bitcast.69, s32[2048]{0:T(1024)S(1)} %bitcast.68), kind=kLoop, calls=%fused_computation.6 | loop fusion | flops 8388608 | bytes 8404992 | tf_op jit(solution)/shard_map/convert_element_type | solution.py:115
  44.0 14.2 %all-to-all-done = f32[16,256,128]{2,1,0:T(8,128)S(1)} async-done(((f32[16,256,128]{2,1,0:T(8,128)}), f32[16,256,128]{2,1,0:T(8,128)S(1)}, u32[]{:S(2)}, u32[]{:S(2)}) %all-to-all-start) | async-done | bytes 2097184 | tf_op jit(solution)/shard_map/all_to_all | solution.py:300
  58.3 0.0 copy-start
  58.3 1.3 %copy-done = f32[16,256,128]{2,1,0:T(8,128)} copy-done((f32[16,256,128]{2,1,0:T(8,128)}, f32[16,256,128]{2,1,0:T(8,128)S(1)}, u32[]{:S(2)}) %copy-start) | copy-done | bytes 2097176
  59.6 0.0 copy-start.1
  59.6 29.2 %shard_map.69 = f32[1024,128]{1,0:T(8,128)} custom-call(f32[4096,128]{1,0:T(8,128)} %bitcast.57, bf16[512,256]{1,0:T(8,128)(2,1)} %get-tuple-element.23.refs_0_, bf16[512,256]{1,0:T(8,128)(2,1)} %get-tuple-element.24.refs_1_, s32[512,1]{1,0:T(8,128)} %copy.12.refs_2_, bf16[1024,512]{1,0:T(8,128)(2,1)} %get-tuple-element.21.refs_3_, ...), custom_call_target="tpu_custom_call" | custom-call | tf_op jit(solution)/shard_map/pallas_call | solution.py:121
  88.8 6.8 %all-to-all-start.1 = ((f32[128,8,128]{2,1,0:T(8,128)}), f32[128,8,128]{2,1,0:T(8,128)S(1)}, u32[]{:S(2)}, u32[]{:S(2)}) async-start(f32[128,8,128]{2,1,0:T(8,128)} %bitcast.61), calls=%async_computation.1 | async-start | bytes 1048576 | tf_op jit(solution)/shard_map/all_to_all | solution.py:318
  95.7 0.0 copy-done.1
  95.7 0.1 subtract_bitcast_fusion.1
  95.8 2.0 %copy.18.offset_ref = s32[8,512,1]{2,1,0:T(8,128)} copy(s32[8,512,1]{1,0,2:T(8,128)S(1)} %subtract_bitcast_fusion.1) | data formatting | bytes 32768 | tf_op jit(solution)/shard_map/broadcast_in_dim | solution.py:259
  97.8 0.1 fusion.43
  97.9 0.1 fusion.41
  98.1 0.3 fusion.33
  98.3 11.1 %all-to-all-done.1 = f32[128,8,128]{2,1,0:T(8,128)S(1)} async-done(((f32[128,8,128]{2,1,0:T(8,128)}), f32[128,8,128]{2,1,0:T(8,128)S(1)}, u32[]{:S(2)}, u32[]{:S(2)}) %all-to-all-start.1) | async-done | bytes 524320 | tf_op jit(solution)/shard_map/all_to_all | solution.py:318
  109.4 0.6 reshape.89
  110.0 0.6 copy.21
  110.6 0.2 reshape_reshape.3
  110.8 1.1 convolution_bitcast_fusion
  112.0 0.2 add_bitcast_fusion
  112.1 1.0 fusion.6
  113.2 0.3 fusion.13
  113.5 0.2 copy.17
  113.7 0.9 reshape.90.spectrum_ref
  114.6 4.1 %shard_map.70 = f32[16,512]{1,0:T(8,128)} custom-call(f32[16,4096]{1,0:T(8,128)} %reshape.90.spectrum_ref, s32[8,512,1]{2,1,0:T(8,128)} %copy.18.offset_ref), custom_call_target="tpu_custom_call" | custom-call | tf_op jit(solution)/shard_map/pallas_call | solution.py:261
  (11 shorter events, 0.1 us)
Async XLA Ops:
  1.9 6.8 %collective-permute-start = (bf16[256,256]{0,1:T(8,128)(2,1)S(1)}, bf16[256,256]{0,1:T(8,128)(2,1)S(1)}, u32[]{:S(2)}, u32[]{:S(2)}) collective-permute-start(bf16[256,256]{0,1:T(8,128)(2,1)S(1)} %slice.108), channel_id=1, source_target_pairs={{0,1},{1,2},{2,3},{3,4},{4,5},{5,6},{6,7},{8,9},{9,10},{10,11},{11... | collective-permute-start | bytes 393224 | tf_op jit(solution)/shard_map/ppermute | solution.py:279
  21.0 37.3 %all-to-all-start = ((f32[16,256,128]{2,1,0:T(8,128)}), f32[16,256,128]{2,1,0:T(8,128)S(1)}, u32[]{:S(2)}, u32[]{:S(2)}) async-start(f32[16,256,128]{2,1,0:T(8,128)} %shard_map.68), calls=%async_computation | async-start | bytes 4194304 | tf_op jit(solution)/shard_map/all_to_all | solution.py:300
  58.3 1.3 %copy-start = (f32[16,256,128]{2,1,0:T(8,128)}, f32[16,256,128]{2,1,0:T(8,128)S(1)}, u32[]{:S(2)}) copy-start(f32[16,256,128]{2,1,0:T(8,128)S(1)} %all-to-all-done) | copy-start | bytes 6291460
  59.6 36.1 %copy-start.1 = (s32[8,512]{1,0:T(8,128)S(1)}, s32[8,512]{1,0:T(8,128)}, u32[]{:S(2)}) copy-start(s32[8,512]{1,0:T(8,128)} %param.9) | copy-start | bytes 49156
  88.8 20.6 %all-to-all-start.1 = ((f32[128,8,128]{2,1,0:T(8,128)}), f32[128,8,128]{2,1,0:T(8,128)S(1)}, u32[]{:S(2)}, u32[]{:S(2)}) async-start(f32[128,8,128]{2,1,0:T(8,128)} %bitcast.61), calls=%async_computation.1 | async-start | bytes 1048576 | tf_op jit(solution)/shard_map/all_to_all | solution.py:318

commit v18 on v15

--- a/solution.py
+++ b/solution.py
@@ -210,7 +210,7 @@
     outer = DFT_OUTER
     inner = total // outer
     half_inner = inner // 2
-    highest = lax.Precision.HIGHEST
+    highest = lax.Precision.HIGH
     grid = series.reshape(count, outer, inner)
     outer_index = jnp.arange(outer, dtype=jnp.int32)
     inner_index = jnp.arange(inner, dtype=jnp.int32)

time: 120 us -> 119 us (level)
  no operation moved by 1% of the time
where the time goes in v18:
time: 119 us; the launch traced here: 118 us
  Pallas kernels  44.5 us (37%)
  waiting for transfers between devices  25.3 us (21%)
  starting transfers between devices  19.1 us (16%)
  other arithmetic  14.1 us (12%)
  local copies, waits for them, and re-layouts  13.1 us (11%)
  matrix products  1.33 us (1%)
    pallas_call x1, Pallas kernels, run_matmul_levels(): pl.pallas_call(functools.partial(matmul_kernel, plan), out_shape=jax.Shap...  29.2 us
    all_to_all x1, waiting for transfers between devices, on_device(): lax.all_to_all(pieces, 'chan', split_axis=0, concat_axis=0, tiled=True)  14.2 us
    pallas_call x1, Pallas kernels, run_local(): pl.pallas_call(functools.partial(local_kernel, plan, sub, base), out_shap...  11.2 us
    all_to_all x1, waiting for transfers between devices, on_device(): lax.all_to_all(outgoing, ('chan', 'tm'), split_axis=0, concat_axis=0, til...  11.1 us
    convert_element_type x4, other arithmetic, run_matmul_levels(): (first_rows[level, :row_out, None] == columns).astype(jnp.bfloat16)  10.6 us
    all_to_all x1, starting transfers between devices, on_device(): lax.all_to_all(pieces, 'chan', split_axis=0, concat_axis=0, tiled=True)  7.79 us
    all_to_all x1, starting transfers between devices, on_device(): lax.all_to_all(outgoing, ('chan', 'tm'), split_axis=0, concat_axis=0, til...  6.84 us
    another operation x7, local copies, waits for them, and re-layouts, run_matmul_levels(): tables.append(shifts[level, :row_out, None])  4.7 us
  transfers between devices with their start and end apart: 3, of which 2 were waited for; matrix products, arithmetic and copies ran while one was open for 17% of the time, Pallas kernels for 0%

profile of v18, /device:TPU:1, one launch (start us, length us, event | category | flops | bytes accessed | tf_op | source)
XLA Modules:
  0.0 118.3 jit_solution(18290322158647196321)
XLA Ops:
  0.6 1.2 %copy.9 = bf16[256,1024]{0,1:T(8,128)(2,1)S(1)} copy(bf16[256,1024]{1,0:T(8,128)(2,1)} %param.5) | data formatting | bytes 1048576 | tf_op args[0]
  1.9 4.5 %collective-permute-start = (bf16[256,256]{0,1:T(8,128)(2,1)S(1)}, bf16[256,256]{0,1:T(8,128)(2,1)S(1)}, u32[]{:S(2)}, u32[]{:S(2)}) collective-permute-start(bf16[256,256]{0,1:T(8,128)(2,1)S(1)} %slice.108), channel_id=1, source_target_pairs={{0,1},{1,2},{2,3},{3,4},{4,5},{5,6},{6,7},{8,9},{9,10},{10,11},{11... | collective-permute-start | bytes 393224 | tf_op jit(solution)/shard_map/ppermute | solution.py:277
  6.4 0.9 pad_add_fusion
  7.4 1.3 %pad_add_fusion.2.table_ref = s32[3,8,256]{2,1,0:T(8,128)} fusion(s32[1,12,2048]{2,1,0:T(8,128)} %bitcast.64, s32[1,12,2048]{2,1,0:T(8,128)} %bitcast.66, s32[1,12,2048]{2,1,0:T(8,128)} %bitcast.68), kind=kLoop, calls=%fused_computation.73 | loop fusion | flops 12288 | bytes 319488 | tf_op jit(solution)/shard_map/slice | solution.py:289
  8.7 0.0 collective-permute-done
  8.7 1.3 %copy.11 = f32[256,10,128]{2,0,1:T(8,128)} copy(bf16[256,10,128]{0,2,1:T(8,128)(2,1)S(1)} %bitcast.61) | data formatting | bytes 1966080 | tf_op jit(solution)/shard_map/broadcast_in_dim | solution.py:288
  10.1 11.2 %shard_map.68 = f32[16,256,128]{2,1,0:T(8,128)} custom-call(s32[3,8,256]{2,1,0:T(8,128)} %pad_add_fusion.2.table_ref, f32[1,10,256,128]{3,2,1,0:T(8,128)} %bitcast.59), custom_call_target="tpu_custom_call" | custom-call | tf_op jit(solution)/shard_map/pallas_call | solution.py:197
  21.3 7.8 %all-to-all-start = ((f32[16,256,128]{2,1,0:T(8,128)}), f32[16,256,128]{2,1,0:T(8,128)S(1)}, u32[]{:S(2)}, u32[]{:S(2)}) async-start(f32[16,256,128]{2,1,0:T(8,128)} %shard_map.68), calls=%async_computation | async-start | bytes 4194304 | tf_op jit(solution)/shard_map/all_to_all | solution.py:298
  29.2 0.9 copy.12.refs_2_
  30.0 1.0 copy.13.refs_5_
  31.1 1.4 %copy.14.refs_8_ = s32[2048,1]{1,0:T(8,128)} copy(s32[2048,1]{0,1:T(1,128)S(1)} %get-tuple-element.11) | data formatting | bytes 16384 | tf_op jit(solution)/shard_map/broadcast_in_dim;squeeze | solution.py:117
  32.4 1.4 %copy.15.refs_11_ = s32[2048,1]{1,0:T(8,128)} copy(s32[2048,1]{0,1:T(1,128)S(1)} %get-tuple-element.8) | data formatting | bytes 16384 | tf_op jit(solution)/shard_map/broadcast_in_dim;squeeze | solution.py:117
  33.8 1.0 fusion.15
  34.8 1.7 %fusion.4 = (bf16[1024,512]{1,0:T(8,128)(2,1)}, bf16[1024,512]{1,0:T(8,128)(2,1)}) fusion(s32[1024]{0:T(1024)S(1)} %bitcast.73, s32[1024]{0:T(1024)S(1)} %bitcast.74), kind=kLoop, calls=%fused_computation.10 | loop fusion | flops 2097152 | bytes 2105344 | tf_op jit(solution)/shard_map/convert_element_type | solution.py:115
  36.5 4.0 %fusion = (bf16[2048,1024]{1,0:T(8,128)(2,1)}, bf16[2048,1024]{1,0:T(8,128)(2,1)}) fusion(s32[2048]{0:T(1024)S(1)} %bitcast.72, s32[2048]{0:T(1024)S(1)} %bitcast.71), kind=kLoop, calls=%fused_computation.4 | loop fusion | flops 8388608 | bytes 8404992 | tf_op jit(solution)/shard_map/convert_element_type | solution.py:115
  40.4 4.0 %fusion.2 = (bf16[2048,1024]{1,0:T(8,128)(2,1)}, bf16[2048,1024]{1,0:T(8,128)(2,1)}) fusion(s32[2048]{0:T(1024)S(1)} %bitcast.70, s32[2048]{0:T(1024)S(1)} %bitcast.69), kind=kLoop, calls=%fused_computation.6 | loop fusion | flops 8388608 | bytes 8404992 | tf_op jit(solution)/shard_map/convert_element_type | solution.py:115
  44.4 14.2 %all-to-all-done = f32[16,256,128]{2,1,0:T(8,128)S(1)} async-done(((f32[16,256,128]{2,1,0:T(8,128)}), f32[16,256,128]{2,1,0:T(8,128)S(1)}, u32[]{:S(2)}, u32[]{:S(2)}) %all-to-all-start) | async-done | bytes 2097184 | tf_op jit(solution)/shard_map/all_to_all | solution.py:298
  58.6 0.0 copy-start
  58.6 1.3 %copy-done = f32[16,256,128]{2,1,0:T(8,128)} copy-done((f32[16,256,128]{2,1,0:T(8,128)}, f32[16,256,128]{2,1,0:T(8,128)S(1)}, u32[]{:S(2)}) %copy-start) | copy-done | bytes 2097176
  60.0 0.0 copy-start.1
  60.0 29.2 %shard_map.69 = f32[1024,128]{1,0:T(8,128)} custom-call(f32[4096,128]{1,0:T(8,128)} %bitcast.58, bf16[512,256]{1,0:T(8,128)(2,1)} %get-tuple-element.23.refs_0_, bf16[512,256]{1,0:T(8,128)(2,1)} %get-tuple-element.24.refs_1_, s32[512,1]{1,0:T(8,128)} %copy.12.refs_2_, bf16[1024,512]{1,0:T(8,128)(2,1)} %get-tuple-element.21.refs_3_, ...), custom_call_target="tpu_custom_call" | custom-call | tf_op jit(solution)/shard_map/pallas_call | solution.py:121
  89.2 6.8 %all-to-all-start.1 = ((f32[128,8,128]{2,1,0:T(8,128)}), f32[128,8,128]{2,1,0:T(8,128)S(1)}, u32[]{:S(2)}, u32[]{:S(2)}) async-start(f32[128,8,128]{2,1,0:T(8,128)} %bitcast.62), calls=%async_computation.1 | async-start | bytes 1048576 | tf_op jit(solution)/shard_map/all_to_all | solution.py:316
  96.1 0.0 copy-done.1
  96.1 0.1 subtract_bitcast_fusion.1
  96.1 2.0 %copy.18.offset_ref = s32[8,512,1]{2,1,0:T(8,128)} copy(s32[8,512,1]{1,0,2:T(8,128)S(1)} %subtract_bitcast_fusion.1) | data formatting | bytes 32768 | tf_op jit(solution)/shard_map/broadcast_in_dim | solution.py:257
  98.1 0.1 fusion.43
  98.3 0.1 fusion.41
  98.4 0.3 fusion.33
  98.7 11.1 %all-to-all-done.1 = f32[128,8,128]{2,1,0:T(8,128)S(1)} async-done(((f32[128,8,128]{2,1,0:T(8,128)}), f32[128,8,128]{2,1,0:T(8,128)S(1)}, u32[]{:S(2)}, u32[]{:S(2)}) %all-to-all-start.1) | async-done | bytes 524320 | tf_op jit(solution)/shard_map/all_to_all | solution.py:316
  109.8 0.6 reshape.89
  110.4 0.6 copy.21
  111.0 0.2 reshape_reshape.3
  111.2 0.7 convolution_bitcast_fusion
  111.9 0.2 add_bitcast_fusion
  112.1 0.6 fusion.6
  112.7 0.3 fusion.13
  113.1 0.2 copy.17
  113.3 0.9 reshape.90.spectrum_ref
  114.2 4.1 %shard_map.70 = f32[16,512]{1,0:T(8,128)} custom-call(f32[16,4096]{1,0:T(8,128)} %reshape.90.spectrum_ref, s32[8,512,1]{2,1,0:T(8,128)} %copy.18.offset_ref), custom_call_target="tpu_custom_call" | custom-call | tf_op jit(solution)/shard_map/pallas_call | solution.py:259
  (11 shorter events, 0.1 us)
Async XLA Ops:
  1.9 6.8 %collective-permute-start = (bf16[256,256]{0,1:T(8,128)(2,1)S(1)}, bf16[256,256]{0,1:T(8,128)(2,1)S(1)}, u32[]{:S(2)}, u32[]{:S(2)}) collective-permute-start(bf16[256,256]{0,1:T(8,128)(2,1)S(1)} %slice.108), channel_id=1, source_target_pairs={{0,1},{1,2},{2,3},{3,4},{4,5},{5,6},{6,7},{8,9},{9,10},{10,11},{11... | collective-permute-start | bytes 393224 | tf_op jit(solution)/shard_map/ppermute | solution.py:277
  21.3 37.3 %all-to-all-start = ((f32[16,256,128]{2,1,0:T(8,128)}), f32[16,256,128]{2,1,0:T(8,128)S(1)}, u32[]{:S(2)}, u32[]{:S(2)}) async-start(f32[16,256,128]{2,1,0:T(8,128)} %shard_map.68), calls=%async_computation | async-start | bytes 4194304 | tf_op jit(solution)/shard_map/all_to_all | solution.py:298
  58.6 1.3 %copy-start = (f32[16,256,128]{2,1,0:T(8,128)}, f32[16,256,128]{2,1,0:T(8,128)S(1)}, u32[]{:S(2)}) copy-start(f32[16,256,128]{2,1,0:T(8,128)S(1)} %all-to-all-done) | copy-start | bytes 6291460
  60.0 36.1 %copy-start.1 = (s32[8,512]{1,0:T(8,128)S(1)}, s32[8,512]{1,0:T(8,128)}, u32[]{:S(2)}) copy-start(s32[8,512]{1,0:T(8,128)} %param.9) | copy-start | bytes 49156
  89.2 20.6 %all-to-all-start.1 = ((f32[128,8,128]{2,1,0:T(8,128)}), f32[128,8,128]{2,1,0:T(8,128)S(1)}, u32[]{:S(2)}, u32[]{:S(2)}) async-start(f32[128,8,128]{2,1,0:T(8,128)} %bitcast.62), calls=%async_computation.1 | async-start | bytes 1048576 | tf_op jit(solution)/shard_map/all_to_all | solution.py:316

commit v19 on v18

--- a/solution.py
+++ b/solution.py
@@ -173,7 +173,7 @@
                 target[row] = merged
             return carry
 
-        lax.fori_loop(0, row_out, body, 0, unroll=min(row_out, 32 if bands_out <= 2 else 16))
+        lax.fori_loop(0, row_out, body, 0, unroll=min(row_out, 32 if bands_out <= 4 else 16))
         source = target
     for dest in range(out_ref.shape[0]):
         start = base + sub * dest

time: 119 us -> 119 us (level)
  no operation moved by 1% of the time
where the time goes in v19:
time: 119 us; the launch traced here: 118 us
  Pallas kernels  44.4 us (37%)
  waiting for transfers between devices  25.3 us (21%)
  starting transfers between devices  19.1 us (16%)
  other arithmetic  14.1 us (12%)
  local copies, waits for them, and re-layouts  13.1 us (11%)
  matrix products  1.33 us (1%)
    pallas_call x1, Pallas kernels, run_matmul_levels(): pl.pallas_call(functools.partial(matmul_kernel, plan), out_shape=jax.Shap...  29.2 us
    all_to_all x1, waiting for transfers between devices, on_device(): lax.all_to_all(pieces, 'chan', split_axis=0, concat_axis=0, tiled=True)  14.2 us
    all_to_all x1, waiting for transfers between devices, on_device(): lax.all_to_all(outgoing, ('chan', 'tm'), split_axis=0, concat_axis=0, til...  11.1 us
    pallas_call x1, Pallas kernels, run_local(): pl.pallas_call(functools.partial(local_kernel, plan, sub, base), out_shap...  11 us
    convert_element_type x4, other arithmetic, run_matmul_levels(): (first_rows[level, :row_out, None] == columns).astype(jnp.bfloat16)  10.6 us
    all_to_all x1, starting transfers between devices, on_device(): lax.all_to_all(pieces, 'chan', split_axis=0, concat_axis=0, tiled=True)  7.79 us
    all_to_all x1, starting transfers between devices, on_device(): lax.all_to_all(outgoing, ('chan', 'tm'), split_axis=0, concat_axis=0, til...  6.84 us
    another operation x7, local copies, waits for them, and re-layouts, run_matmul_levels(): tables.append(shifts[level, :row_out, None])  4.7 us
  transfers between devices with their start and end apart: 3, of which 2 were waited for; matrix products, arithmetic and copies ran while one was open for 17% of the time, Pallas kernels for 0%

profile of v19, /device:TPU:1, one launch (start us, length us, event | category | flops | bytes accessed | tf_op | source)
XLA Modules:
  0.0 118.1 jit_solution(15942494810662515941)
XLA Ops:
  0.6 1.2 %copy.9 = bf16[256,1024]{0,1:T(8,128)(2,1)S(1)} copy(bf16[256,1024]{1,0:T(8,128)(2,1)} %param.5) | data formatting | bytes 1048576 | tf_op args[0]
  1.9 4.5 %collective-permute-start = (bf16[256,256]{0,1:T(8,128)(2,1)S(1)}, bf16[256,256]{0,1:T(8,128)(2,1)S(1)}, u32[]{:S(2)}, u32[]{:S(2)}) collective-permute-start(bf16[256,256]{0,1:T(8,128)(2,1)S(1)} %slice.108), channel_id=1, source_target_pairs={{0,1},{1,2},{2,3},{3,4},{4,5},{5,6},{6,7},{8,9},{9,10},{10,11},{11... | collective-permute-start | bytes 393224 | tf_op jit(solution)/shard_map/ppermute | solution.py:277
  6.4 0.9 pad_add_fusion
  7.4 1.3 %pad_add_fusion.2.table_ref = s32[3,8,256]{2,1,0:T(8,128)} fusion(s32[1,12,2048]{2,1,0:T(8,128)} %bitcast.64, s32[1,12,2048]{2,1,0:T(8,128)} %bitcast.66, s32[1,12,2048]{2,1,0:T(8,128)} %bitcast.68), kind=kLoop, calls=%fused_computation.73 | loop fusion | flops 12288 | bytes 319488 | tf_op jit(solution)/shard_map/slice | solution.py:289
  8.7 0.0 collective-permute-done
  8.7 1.3 %copy.11 = f32[256,10,128]{2,0,1:T(8,128)} copy(bf16[256,10,128]{0,2,1:T(8,128)(2,1)S(1)} %bitcast.61) | data formatting | bytes 1966080 | tf_op jit(solution)/shard_map/broadcast_in_dim | solution.py:288
  10.1 11.0 %shard_map.68 = f32[16,256,128]{2,1,0:T(8,128)} custom-call(s32[3,8,256]{2,1,0:T(8,128)} %pad_add_fusion.2.table_ref, f32[1,10,256,128]{3,2,1,0:T(8,128)} %bitcast.59), custom_call_target="tpu_custom_call" | custom-call | tf_op jit(solution)/shard_map/pallas_call | solution.py:197
  21.2 7.8 %all-to-all-start = ((f32[16,256,128]{2,1,0:T(8,128)}), f32[16,256,128]{2,1,0:T(8,128)S(1)}, u32[]{:S(2)}, u32[]{:S(2)}) async-start(f32[16,256,128]{2,1,0:T(8,128)} %shard_map.68), calls=%async_computation | async-start | bytes 4194304 | tf_op jit(solution)/shard_map/all_to_all | solution.py:298
  29.0 0.9 copy.12.refs_2_
  29.9 1.0 copy.13.refs_5_
  30.9 1.4 %copy.14.refs_8_ = s32[2048,1]{1,0:T(8,128)} copy(s32[2048,1]{0,1:T(1,128)S(1)} %get-tuple-element.11) | data formatting | bytes 16384 | tf_op jit(solution)/shard_map/broadcast_in_dim;squeeze | solution.py:117
  32.3 1.4 %copy.15.refs_11_ = s32[2048,1]{1,0:T(8,128)} copy(s32[2048,1]{0,1:T(1,128)S(1)} %get-tuple-element.8) | data formatting | bytes 16384 | tf_op jit(solution)/shard_map/broadcast_in_dim;squeeze | solution.py:117
  33.7 1.0 fusion.15
  34.7 1.7 %fusion.4 = (bf16[1024,512]{1,0:T(8,128)(2,1)}, bf16[1024,512]{1,0:T(8,128)(2,1)}) fusion(s32[1024]{0:T(1024)S(1)} %bitcast.73, s32[1024]{0:T(1024)S(1)} %bitcast.74), kind=kLoop, calls=%fused_computation.10 | loop fusion | flops 2097152 | bytes 2105344 | tf_op jit(solution)/shard_map/convert_element_type | solution.py:115
  36.3 4.0 %fusion = (bf16[2048,1024]{1,0:T(8,128)(2,1)}, bf16[2048,1024]{1,0:T(8,128)(2,1)}) fusion(s32[2048]{0:T(1024)S(1)} %bitcast.72, s32[2048]{0:T(1024)S(1)} %bitcast.71), kind=kLoop, calls=%fused_computation.4 | loop fusion | flops 8388608 | bytes 8404992 | tf_op jit(solution)/shard_map/convert_element_type | solution.py:115
  40.3 4.0 %fusion.2 = (bf16[2048,1024]{1,0:T(8,128)(2,1)}, bf16[2048,1024]{1,0:T(8,128)(2,1)}) fusion(s32[2048]{0:T(1024)S(1)} %bitcast.70, s32[2048]{0:T(1024)S(1)} %bitcast.69), kind=kLoop, calls=%fused_computation.6 | loop fusion | flops 8388608 | bytes 8404992 | tf_op jit(solution)/shard_map/convert_element_type | solution.py:115
  44.3 14.2 %all-to-all-done = f32[16,256,128]{2,1,0:T(8,128)S(1)} async-done(((f32[16,256,128]{2,1,0:T(8,128)}), f32[16,256,128]{2,1,0:T(8,128)S(1)}, u32[]{:S(2)}, u32[]{:S(2)}) %all-to-all-start) | async-done | bytes 2097184 | tf_op jit(solution)/shard_map/all_to_all | solution.py:298
  58.5 0.0 copy-start
  58.5 1.3 %copy-done = f32[16,256,128]{2,1,0:T(8,128)} copy-done((f32[16,256,128]{2,1,0:T(8,128)}, f32[16,256,128]{2,1,0:T(8,128)S(1)}, u32[]{:S(2)}) %copy-start) | copy-done | bytes 2097176
  59.8 0.0 copy-start.1
  59.8 29.2 %shard_map.69 = f32[1024,128]{1,0:T(8,128)} custom-call(f32[4096,128]{1,0:T(8,128)} %bitcast.58, bf16[512,256]{1,0:T(8,128)(2,1)} %get-tuple-element.23.refs_0_, bf16[512,256]{1,0:T(8,128)(2,1)} %get-tuple-element.24.refs_1_, s32[512,1]{1,0:T(8,128)} %copy.12.refs_2_, bf16[1024,512]{1,0:T(8,128)(2,1)} %get-tuple-element.21.refs_3_, ...), custom_call_target="tpu_custom_call" | custom-call | tf_op jit(solution)/shard_map/pallas_call | solution.py:121
  89.1 6.8 %all-to-all-start.1 = ((f32[128,8,128]{2,1,0:T(8,128)}), f32[128,8,128]{2,1,0:T(8,128)S(1)}, u32[]{:S(2)}, u32[]{:S(2)}) async-start(f32[128,8,128]{2,1,0:T(8,128)} %bitcast.62), calls=%async_computation.1 | async-start | bytes 1048576 | tf_op jit(solution)/shard_map/all_to_all | solution.py:316
  95.9 0.0 copy-done.1
  95.9 0.1 subtract_bitcast_fusion.1
  96.0 2.0 %copy.18.offset_ref = s32[8,512,1]{2,1,0:T(8,128)} copy(s32[8,512,1]{1,0,2:T(8,128)S(1)} %subtract_bitcast_fusion.1) | data formatting | bytes 32768 | tf_op jit(solution)/shard_map/broadcast_in_dim | solution.py:257
  98.0 0.1 fusion.43
  98.1 0.1 fusion.41
  98.3 0.3 fusion.33
  98.6 11.1 %all-to-all-done.1 = f32[128,8,128]{2,1,0:T(8,128)S(1)} async-done(((f32[128,8,128]{2,1,0:T(8,128)}), f32[128,8,128]{2,1,0:T(8,128)S(1)}, u32[]{:S(2)}, u32[]{:S(2)}) %all-to-all-start.1) | async-done | bytes 524320 | tf_op jit(solution)/shard_map/all_to_all | solution.py:316
  109.6 0.6 reshape.89
  110.2 0.6 copy.21
  110.9 0.2 reshape_reshape.3
  111.1 0.7 convolution_bitcast_fusion
  111.8 0.2 add_bitcast_fusion
  111.9 0.6 fusion.6
  112.6 0.3 fusion.13
  112.9 0.2 copy.17
  113.1 0.9 reshape.90.spectrum_ref
  114.0 4.1 %shard_map.70 = f32[16,512]{1,0:T(8,128)} custom-call(f32[16,4096]{1,0:T(8,128)} %reshape.90.spectrum_ref, s32[8,512,1]{2,1,0:T(8,128)} %copy.18.offset_ref), custom_call_target="tpu_custom_call" | custom-call | tf_op jit(solution)/shard_map/pallas_call | solution.py:259
  (11 shorter events, 0.1 us)
Async XLA Ops:
  1.9 6.8 %collective-permute-start = (bf16[256,256]{0,1:T(8,128)(2,1)S(1)}, bf16[256,256]{0,1:T(8,128)(2,1)S(1)}, u32[]{:S(2)}, u32[]{:S(2)}) collective-permute-start(bf16[256,256]{0,1:T(8,128)(2,1)S(1)} %slice.108), channel_id=1, source_target_pairs={{0,1},{1,2},{2,3},{3,4},{4,5},{5,6},{6,7},{8,9},{9,10},{10,11},{11... | collective-permute-start | bytes 393224 | tf_op jit(solution)/shard_map/ppermute | solution.py:277
  21.2 37.3 %all-to-all-start = ((f32[16,256,128]{2,1,0:T(8,128)}), f32[16,256,128]{2,1,0:T(8,128)S(1)}, u32[]{:S(2)}, u32[]{:S(2)}) async-start(f32[16,256,128]{2,1,0:T(8,128)} %shard_map.68), calls=%async_computation | async-start | bytes 4194304 | tf_op jit(solution)/shard_map/all_to_all | solution.py:298
  58.5 1.3 %copy-start = (f32[16,256,128]{2,1,0:T(8,128)}, f32[16,256,128]{2,1,0:T(8,128)S(1)}, u32[]{:S(2)}) copy-start(f32[16,256,128]{2,1,0:T(8,128)S(1)} %all-to-all-done) | copy-start | bytes 6291460
  59.8 36.1 %copy-start.1 = (s32[8,512]{1,0:T(8,128)S(1)}, s32[8,512]{1,0:T(8,128)}, u32[]{:S(2)}) copy-start(s32[8,512]{1,0:T(8,128)} %param.9) | copy-start | bytes 49156
  89.1 20.6 %all-to-all-start.1 = ((f32[128,8,128]{2,1,0:T(8,128)}), f32[128,8,128]{2,1,0:T(8,128)S(1)}, u32[]{:S(2)}, u32[]{:S(2)}) async-start(f32[128,8,128]{2,1,0:T(8,128)} %bitcast.62), calls=%async_computation.1 | async-start | bytes 1048576 | tf_op jit(solution)/shard_map/all_to_all | solution.py:316
